TPU v7x, 32 devices: a whole 2x2x4 slice. The times are simulated.
32 devices in a mesh: seq: 8 (over y, x, core), blk: 4 (over z).
Axes of the slice: x: 2, y: 2, z: 4, core: 2. Of those that a mesh axis runs over, the one named last changes fastest.
Arguments:
- states: bfloat16 [8, 2560, 768], P('seq', 'blk'), may hold values from -6 to 6
- cotangent: bfloat16 [8, 2560, 768], P('seq', 'blk'), may hold values from -6 to 6
- lengths: int32 [8, 5], P('seq'), may hold values from 64 to 512, as said below
- w_qkv: bfloat16 [768, 2304], P(('seq', 'blk')), may hold values from -0.21875 to 0.21875
- w_out: bfloat16 [768, 768], P(('seq', 'blk')), may hold values from -1.75 to 1.75
- w_up: bfloat16 [768, 3072], P(('seq', 'blk')), may hold values from -0.21875 to 0.21875
- w_down: bfloat16 [3072, 768], P(('seq', 'blk')), may hold values from -0.109375 to 0.109375
- vectors: bfloat16 [13, 768], P(None, ('seq', 'blk'))
- up_bias: bfloat16 [3072], P(('seq', 'blk')), may hold values from -1.796875 to 1.796875
Outputs:
- result: bfloat16 [8, 2560, 768], P('seq', 'blk')
- grad_states: bfloat16 [8, 2560, 768], P('seq', 'blk')
- grad_qkv: float32 [768, 2304], P(('seq', 'blk'))
- grad_out: float32 [768, 768], P(('seq', 'blk'))
- grad_up: float32 [768, 3072], P(('seq', 'blk'))
- grad_down: float32 [3072, 768], P(('seq', 'blk'))
- grad_vectors: float32 [13, 768], P(None, ('seq', 'blk'))
- grad_up_bias: float32 [3072], P(('seq', 'blk'))
Inputs may be any that keep to these rules, and one draw needn't show every extreme that they name: `lengths`: every sequence's first pass has all 512 slots live; a later pass has between 64 and 512 live slots, the live ones first.
All inputs are finite; a program needn't handle non-finite values.
Results may differ from a plain program's by a relative error of at most 0.015.
Values may be sent and summed in bfloat16 or wider, within the bound.
No kernel may reach another device: no remote copies, remote signals or barrier semaphores. Data moves between devices by JAX's collectives and lax.ppermute only.
A program may use at most 192 MiB of HBM per device.

v0:
```python
import functools

import jax
import jax.numpy as jnp
from jax import lax
from jax.experimental import pallas as pl
from jax.experimental.layout import Layout, with_layout_constraint
from jax.experimental.pallas import tpu as pltpu
from jax.sharding import PartitionSpec as P


HEAD = 64
PASSES = 5
PASS_SLOTS = 512


masked_value = -1e30
both = ("seq", "blk")
f32 = jnp.float32
bf16 = jnp.bfloat16


def layer_norm(values, gain, offset):
    centre = values - jnp.mean(values, axis=-1, keepdims=True)
    spread = jnp.mean(centre * centre, axis=-1, keepdims=True)
    return centre * lax.rsqrt(spread + 1e-05) * gain + offset


def gelu_tanh(values):
    return jax.nn.gelu(values, approximate=True)


def contract(left, right, dims):
    return lax.dot_general(left, right, (dims, ((), ())), preferred_element_type=f32)


def tile_visible(length):
    key_place = lax.broadcasted_iota(jnp.int32, (PASS_SLOTS, PASS_SLOTS), 0)
    query_place = lax.broadcasted_iota(jnp.int32, (PASS_SLOTS, PASS_SLOTS), 1)
    return (key_place <= query_place) & (key_place < length)


def place_pieces(here, pieces, shelf, whole):
    span = pieces[0].shape[1]
    for step, piece in enumerate(pieces):
        shelf[here ^ step] = piece[...]
    for at in range(len(pieces)):
        whole[:, at * span : (at + 1) * span] = shelf[at]


def hand_out(here, whole, shelf, pieces):
    span = pieces[0].shape[1]
    for at in range(len(pieces)):
        shelf[at] = whole[:, at * span : (at + 1) * span]
    for step, piece in enumerate(pieces):
        piece[...] = shelf[here ^ step]


def turned(rows):
    return rows.astype(f32).T.astype(bf16)


def forward_kernel(groups, lengths, here, *refs):
    pieces, refs = refs[:groups], refs[groups:]
    packed, mixed, totals = refs[:3]
    outs, refs = refs[3 : 3 + groups], refs[3 + groups :]
    shelf, out_shelf, key_rows = refs
    place_pieces(here[0], pieces, shelf, packed)
    key_rows[...] = turned(packed[HEAD : 2 * HEAD, :])
    for query_index in range(PASSES):
        query_span = slice(query_index * PASS_SLOTS, (query_index + 1) * PASS_SLOTS)
        queries = packed[:HEAD, query_span] * jnp.asarray(0.125, bf16)
        top = jnp.full((1, PASS_SLOTS), masked_value, f32)
        total = jnp.zeros((1, PASS_SLOTS), f32)
        acc = jnp.zeros((HEAD, PASS_SLOTS), f32)
        for key_index in range(query_index + 1):
            key_span = slice(key_index * PASS_SLOTS, (key_index + 1) * PASS_SLOTS)
            scores = contract(key_rows[key_span, :], queries, ((1,), (0,)))
            scores = jnp.where(tile_visible(lengths[0, key_index]), scores, masked_value)
            newest = jnp.maximum(top, jnp.max(scores, axis=0, keepdims=True))
            shares = jnp.exp(scores - newest)
            fade = jnp.exp(top - newest)
            total = total * fade + jnp.sum(shares, axis=0, keepdims=True)
            values = packed[2 * HEAD :, key_span]
            acc = acc * fade + contract(values, shares.astype(bf16), ((1,), (0,)))
            top = newest
        mixed[:, query_span] = (acc / total).astype(bf16)
        totals[query_index : query_index + 1, :] = top + jnp.log(total)
    hand_out(here[0], mixed, out_shelf, outs)


def backward_kernel(groups, lengths, here, packed, mixed, totals, *refs):
    pieces, refs = refs[:groups], refs[groups:]
    outs, refs = refs[:groups], refs[groups:]
    shelf, out_shelf, grad, rows, grad_rows, grad_query, result = refs
    place_pieces(here[0], pieces, shelf, grad)
    rows[...] = turned(packed[...])
    grad_rows[...] = turned(grad[...])
    grad_query[...] = jnp.zeros_like(grad_query)
    eighth = jnp.asarray(0.125, bf16)

    def key_pass(key_index, _):
        key_at = pl.multiple_of(key_index * PASS_SLOTS, PASS_SLOTS)
        key_span = pl.ds(key_at, PASS_SLOTS)
        keys = rows[key_span, HEAD : 2 * HEAD] * eighth
        keys_turned = packed[HEAD : 2 * HEAD, key_span] * eighth
        values = rows[key_span, 2 * HEAD :]
        shown = tile_visible(lengths[0, key_index])

        def query_pass(query_index, carried):
            grad_key, grad_value = carried
            query_at = pl.multiple_of(query_index * PASS_SLOTS, PASS_SLOTS)
            query_span = pl.ds(query_at, PASS_SLOTS)
            grads = grad[:, query_span]
            product = grads.astype(f32) * mixed[:, query_span].astype(f32)
            delta = jnp.sum(product, axis=0, keepdims=True)
            scores = contract(keys, packed[:HEAD, query_span], ((1,), (0,)))
            shares = jnp.exp(scores - totals[pl.ds(query_index, 1), :])
            shares = jnp.where(shown, shares, 0.0)
            grad_shares = contract(values, grads, ((1,), (0,)))
            grad_scores = (shares * (grad_shares - delta)).astype(bf16)
            grad_query[:, query_span] += contract(keys_turned, grad_scores, ((1,), (0,)))
            grad_value += contract(shares.astype(bf16), grad_rows[query_span, :], ((1,), (0,)))
            queries = rows[query_span, :HEAD] * eighth
            grad_key += contract(grad_scores, queries, ((1,), (0,)))
            return grad_key, grad_value

        empty = jnp.zeros((PASS_SLOTS, HEAD), f32)
        grad_key, grad_value = lax.fori_loop(key_index, PASSES, query_pass, (empty, empty))
        result[HEAD : 2 * HEAD, key_span] = grad_key.T.astype(bf16)
        result[2 * HEAD :, key_span] = grad_value.T.astype(bf16)
        return 0

    lax.fori_loop(0, PASSES, key_pass, 0)
    result[:HEAD, :] = grad_query[...].astype(bf16)
    hand_out(here[0], result, out_shelf, outs)


in_vmem = functools.partial(pl.BlockSpec, memory_space=pltpu.VMEM)
in_smem = functools.partial(pl.BlockSpec, memory_space=pltpu.SMEM)


def attend(lengths, here, pieces):
    groups = len(pieces)
    triple, span = pieces[0].shape
    slots = span * groups
    return pl.pallas_call(
        functools.partial(forward_kernel, groups),
        out_shape=[
            jax.ShapeDtypeStruct((triple, slots), bf16),
            jax.ShapeDtypeStruct((HEAD, slots), bf16),
            jax.ShapeDtypeStruct((PASSES, PASS_SLOTS), f32),
        ]
        + [jax.ShapeDtypeStruct((HEAD, span), bf16)] * groups,
        in_specs=[in_smem(), in_smem()] + [in_vmem()] * groups,
        out_specs=[in_vmem()] * (3 + groups),
        scratch_shapes=[
            pltpu.VMEM((groups, triple, span), bf16),
            pltpu.VMEM((groups, HEAD, span), bf16),
            pltpu.VMEM((slots, HEAD), bf16),
        ],
        compiler_params=pltpu.CompilerParams(vmem_limit_bytes=32 << 20),
        cost_estimate=pl.CostEstimate(flops=10**10, transcendentals=0, bytes_accessed=10**6),
        name="attend",
    )(lengths, here, *pieces)


def attend_back(lengths, here, packed, mixed, totals, pieces):
    groups = len(pieces)
    triple, slots = packed.shape
    span = slots // groups
    return pl.pallas_call(
        functools.partial(backward_kernel, groups),
        out_shape=[jax.ShapeDtypeStruct((triple, span), bf16)] * groups,
        in_specs=[in_smem(), in_smem()] + [in_vmem()] * (3 + groups),
        out_specs=[in_vmem()] * groups,
        scratch_shapes=[
            pltpu.VMEM((groups, HEAD, span), bf16),
            pltpu.VMEM((groups, triple, span), bf16),
            pltpu.VMEM((HEAD, slots), bf16),
            pltpu.VMEM((slots, triple), bf16),
            pltpu.VMEM((slots, HEAD), bf16),
            pltpu.VMEM((HEAD, slots), f32),
            pltpu.VMEM((triple, slots), bf16),
        ],
        compiler_params=pltpu.CompilerParams(vmem_limit_bytes=32 << 20),
        cost_estimate=pl.CostEstimate(
            flops=15 * 10**9, transcendentals=0, bytes_accessed=10**6
        ),
        name="attend_back",
    )(lengths, here, packed, mixed, totals, *pieces)


def row_major(values):
    return with_layout_constraint(values, Layout(tuple(range(values.ndim))))


def after(values, *others):
    return lax.optimization_barrier((values, others))[0]


def swap_with(values, axis, step):
    size = lax.axis_size(axis)
    return lax.ppermute(values, axis, [(i, i ^ step) for i in range(size)])


def axis_bits(axis):
    size = lax.axis_size(axis)
    assert size & (size - 1) == 0
    return [(axis, 1 << n) for n in reversed(range(size.bit_length() - 1))]


def bit_order(flip):
    places = axis_bits("seq") + axis_bits("blk")
    near = axis_bits("seq")
    far = near[:-1][::-1] if flip else near[:-1]
    return places, axis_bits("blk") + far + near[-1:]


def own_bit(bit):
    return (lax.axis_index(bit[0]) & bit[1]) != 0


class Gather:
    def __init__(self, piece, flip):
        self.places, self.order = bit_order(flip)
        self.shape = piece.shape
        self.piece = piece
        self.done = []

    def grow(self, count=None):
        count = len(self.order) if count is None else count
        for bit in self.order[:count]:
            other = swap_with(self.piece, *bit)
            self.done = sorted(self.done + [bit], key=self.places.index)
            mine = own_bit(bit)
            low = jnp.where(mine, other, self.piece)
            high = jnp.where(mine, self.piece, other)
            self.piece = jnp.stack([low, high], axis=self.done.index(bit))
        self.order = self.order[count:]
        return self.piece

    def whole(self):
        return self.grow().reshape((-1,) + self.shape[1:])


class Scatter:
    def __init__(self, whole, flip):
        self.left, order = bit_order(flip)
        self.order = order[::-1]
        self.sent = None
        rows = whole.shape[0] >> len(order)
        self.piece = whole.reshape((2,) * len(order) + (rows,) + whole.shape[1:])

    def send(self):
        bit, self.order = self.order[0], self.order[1:]
        at = self.left.index(bit)
        self.left = [place for place in self.left if place != bit]
        low = lax.index_in_dim(self.piece, 0, at, keepdims=False)
        high = lax.index_in_dim(self.piece, 1, at, keepdims=False)
        mine = own_bit(bit)
        self.bit = bit
        self.sent = jnp.where(mine, low, high)
        self.kept = jnp.where(mine, high, low)
        return (self.sent, self.kept)

    def receive(self, *others):
        if self.sent is None:
            return
        other = after(swap_with(self.sent, *self.bit), others)
        self.sent = None
        self.piece = (self.kept.astype(f32) + other.astype(f32)).astype(bf16)

    def finish(self):
        self.receive()
        while self.order:
            self.send()
            self.receive()
        return self.piece


def swap_pieces(pieces):
    return [swap_with(piece, "blk", step) if step else piece for step, piece in enumerate(pieces)]


def in_order(pieces):
    here = lax.axis_index("blk")
    result = jnp.zeros((len(pieces),) + pieces[0].shape, pieces[0].dtype)
    for step, piece in enumerate(pieces):
        result = lax.dynamic_update_index_in_dim(result, piece, here ^ step, 0)
    return result


def at_group(values, group):
    return lax.dynamic_index_in_dim(values, group, 0, keepdims=False)


def by_head(rows, groups):
    count = rows.shape[0]
    return rows.reshape(count, 3, groups, -1, HEAD).transpose(0, 3, 2, 1, 4).reshape(count, -1)


def by_kind(rows, groups):
    count = rows.shape[0]
    return rows.reshape(count, -1, groups, 3, HEAD).transpose(0, 3, 2, 1, 4).reshape(count, -1)


def norm_parts(values):
    centre = values - jnp.mean(values, axis=-1, keepdims=True)
    spread = jnp.mean(centre * centre, axis=-1, keepdims=True)
    scale = lax.rsqrt(spread + 1e-05)
    return centre * scale, scale


def norm_back(values, gain, grad):
    hat, scale = norm_parts(values)
    edge = grad * gain
    part = scale * (
        edge
        - jnp.mean(edge, axis=-1, keepdims=True)
        - hat * jnp.mean(edge * hat, axis=-1, keepdims=True)
    )
    return part, jnp.sum(grad * hat, axis=0), jnp.sum(grad, axis=0)


def on_device(states, cotangent, lengths, w_qkv, w_out, w_up, w_down, vectors, up_bias):
    _, row_count, width = states.shape
    groups = lax.axis_size("blk")
    own = w_qkv.shape[0]
    wide = w_up.shape[1]
    ratio = wide // width
    vector_count = vectors.shape[0]
    heads = width // HEAD // groups
    span = 3 * HEAD
    small = vector_count + ratio

    here = lax.axis_index("blk").astype(jnp.int32)
    parts = by_head(w_qkv, groups)
    middle_column = parts.shape[1] // 2
    extra = [vectors.T, up_bias.reshape(own, ratio), jnp.zeros((own, -small % 128), bf16)]
    streams = [
        Gather(jnp.concatenate([parts[:, :middle_column]] + extra, axis=1), False),
        Gather(parts[:, middle_column:], True),
    ]
    blk_steps = len(axis_bits("blk"))
    begun = [stream.grow(blk_steps) for stream in streams]
    w_out, w_up, w_down = after((w_out, w_up, w_down), begun)
    later = [Gather(w_up, False), Gather(w_down, True), Gather(w_out, False)]
    for one in later:
        one.grow(blk_steps)
    first = [stream.whole() for stream in streams]
    for one in later:
        one.piece = after(one.piece, first)
        one.grow(1)
    full_qkv = jnp.concatenate([first[0][:, :middle_column], first[1]], axis=1)
    head_qkv = [full_qkv[:, h * groups * span : (h + 1) * groups * span] for h in range(heads)]
    corner = first[0][:, middle_column : middle_column + small]
    table = corner[:, :vector_count].astype(f32).T
    bias_up = corner[:, vector_count:].astype(f32).reshape(wide)

    slots = lax.axis_index("blk") * row_count + jnp.arange(row_count, dtype=jnp.int32)
    pass_of = (slots // PASS_SLOTS)[:, None] == jnp.arange(PASSES, dtype=jnp.int32)[None, :]
    bounds = jnp.sum(jnp.where(pass_of, lengths[0][None, :], 0), axis=1)
    live = (slots % PASS_SLOTS < bounds).astype(f32)[:, None]

    added = jnp.zeros((row_count, width), f32)
    for index in range(PASSES):
        added = jnp.where(pass_of[:, index : index + 1], table[index], added)
    start = states[0].astype(f32) + added
    normed_a = layer_norm(start, table[5], table[6]).astype(bf16)
    column = jnp.arange(3 * width, dtype=jnp.int32)
    kind = column // HEAD % 3
    source = (column // span % groups) * heads + column // (span * groups)
    source = source * HEAD + column % HEAD
    match = source[:, None] == jnp.arange(width, dtype=jnp.int32)[None, :]
    choice = jnp.where((kind == 0)[:, None], table[7], jnp.where((kind == 2)[:, None], table[8], 0.0))
    bias_three = jnp.sum(jnp.where(match, choice, 0.0), axis=1, keepdims=True)
    bias_three = bias_three.reshape(heads, -1, 1)
    sending = []
    for h in range(heads):
        rows = contract(head_qkv[h], normed_a, ((0,), (1,))) + bias_three[h]
        rows = rows.astype(bf16).reshape(groups, span, row_count)
        sending.append([row_major(at_group(rows, here ^ step)) for step in range(groups)])
    for one in later:
        one.piece = after(one.piece, sending[0])
    kept = []
    arrived = []
    returned = []
    for h in range(heads):
        pieces = swap_pieces(after(sending[h], arrived))
        arrived = pieces
        if h == 1:
            pieces = after(pieces, [one.piece for one in later])
        packed, mixed, totals, *pieces = attend(lengths, here[None], pieces)
        kept.append((packed, mixed, totals))
        returned.append(swap_pieces(pieces))
    full_up, full_down, full_out = [one.whole() for one in later]
    returned[:-1] = after(returned[:-1], pieces)
    returned = [in_order(pieces) for pieces in returned]
    heads_out = jnp.stack(returned, axis=1).reshape(width, row_count)
    middle = start + live * (contract(heads_out, full_out, ((0,), (0,))) + table[9])
    normed_b = layer_norm(middle, table[10], table[11]).astype(bf16)
    up_sum = contract(normed_b, full_up, ((1,), (0,))) + bias_up
    activated, gelu_pull = jax.vjp(gelu_tanh, up_sum)
    hidden = activated.astype(bf16)
    outcome = middle + live * (contract(hidden, full_down, ((1,), (0,))) + table[12])
    incoming = cotangent[0].astype(f32)
    grad_branch = (live * incoming).astype(bf16)
    grad_hidden = contract(grad_branch, full_down, ((1,), (1,)))
    grad_upsum = gelu_pull(grad_hidden)[0].astype(bf16)
    grad_normb = contract(grad_upsum, full_up, ((1,), (1,)))
    middle_part, gain_grad_b, shift_grad_b = norm_back(middle, table[10], grad_normb)
    grad_middle = incoming + middle_part
    grad_attn = (live * grad_middle).astype(bf16)
    grad_heads = contract(full_out, grad_attn, ((1,), (1,))).astype(bf16)
    grad_heads = grad_heads.reshape(groups, heads, HEAD, row_count)
    sending = [
        [row_major(at_group(grad_heads[:, h], here ^ step)) for step in range(groups)]
        for h in range(heads)
    ]
    arrived = []
    late = []
    parts = []
    for h in range(heads):
        pieces = swap_pieces(after(sending[h], arrived))
        arrived = pieces
        if h == 0:
            pieces = after(pieces, outcome)
        if late:
            if h > 1:
                for one in late:
                    one.receive(parts[-1])
            pieces = after(pieces, [one.send() for one in late])
        back = attend_back(lengths, here[None], *kept[h], pieces)
        if not late:
            hidden_late, grad_branch_late, grad_upsum_late, grad_attn_late = after(
                (hidden, grad_branch, grad_upsum, grad_attn), back
            )
            grad_down = contract(hidden_late, grad_branch_late, ((0,), (0,))).astype(bf16)
            grad_up = contract(normed_b, grad_upsum_late, ((0,), (0,))).astype(bf16)
            grad_out = contract(heads_out, grad_attn_late, ((1,), (0,))).astype(bf16)
            grad_up = jnp.concatenate([grad_up, grad_out], axis=1)
            late = [Scatter(grad_down, True), Scatter(grad_up, False)]
        parts.append(back)
    grad_projected = []
    for back in parts:
        grad_projected.append(swap_pieces(back))
    grad_projected[:-1] = after(grad_projected[:-1], parts[-1])
    for one in late:
        one.receive(parts[-1])
    sent = [one.send() for one in late]

    whole = [in_order(pieces).reshape(groups * span, row_count) for pieces in grad_projected[:-1]]
    early = [row_major(contract(normed_a, part, ((0,), (1,))).astype(bf16)) for part in whole]
    early = Scatter(after(jnp.concatenate(early, axis=1), sent), True)
    pieces = after(grad_projected[-1], early.send())
    whole.append(in_order(pieces).reshape(groups * span, row_count))
    final = row_major(contract(normed_a, whole[-1], ((0,), (1,))).astype(bf16))
    grad_norma = sum(contract(part, weights, ((0,), (1,))) for part, weights in zip(whole, head_qkv))
    started = early.sent
    early.receive(whole[-1])
    sent = [early.send()]
    for one in late:
        one.receive(started)
        sent.append(one.send())
    grad_norma = after(grad_norma, sent)
    sums = [jnp.sum(part.astype(f32), axis=1) for part in whole]
    column_sums = by_kind(jnp.concatenate(sums)[None], groups)[0]
    start_part, gain_grad_a, shift_grad_a = norm_back(start, table[5], grad_norma)
    grad_start = grad_middle + start_part
    grad_embed = [
        jnp.sum(jnp.where(pass_of[:, index : index + 1], grad_start, 0.0), axis=0)
        for index in range(PASSES)
    ]
    vector_grads = jnp.stack(
        grad_embed
        + [
            gain_grad_a,
            shift_grad_a,
            column_sums[:width],
            column_sums[2 * width :],
            jnp.sum(grad_attn.astype(f32), axis=0),
            gain_grad_b,
            shift_grad_b,
            jnp.sum(grad_branch.astype(f32), axis=0),
        ]
    )
    bias_grads = jnp.sum(grad_upsum.astype(f32), axis=0)
    extra = [vector_grads.T.astype(bf16), bias_grads.reshape(width, ratio).astype(bf16)]
    last = Scatter(jnp.concatenate([final] + extra + [jnp.zeros((width, -small % 128), bf16)], axis=1), False)
    wave = 0
    tied = last.send()
    early.receive(tied)
    while last.order:
        sent = [early.send()] if early.order else []
        if wave % 2 == 0 and late[0].order:
            for one in late:
                one.receive(tied)
                sent.append(one.send())
        elif not late[0].order:
            for one in late:
                one.receive(tied)
                sent.append(one.piece)
        last.receive(sent)
        tied = last.send()
        early.receive(tied)
        wave += 1
    last.receive()
    for one in late:
        one.receive(tied)
        one.finish()
    grad_down = late[0].piece
    grad_up = late[1].piece[:, :wide]
    grad_out = late[1].piece[:, wide:]
    grad_qkv = [early.finish(), last.piece[:, : groups * span]]
    extra = last.piece[:, groups * span :].astype(f32)
    return (
        outcome.astype(bf16)[None],
        grad_start.astype(bf16)[None],
        by_kind(jnp.concatenate(grad_qkv, axis=1).astype(f32), groups),
        grad_out.astype(f32),
        grad_up.astype(f32),
        grad_down.astype(f32),
        extra[:, :vector_count].T,
        extra[:, vector_count:small].reshape(own * ratio),
    )


def solution(mesh):
    split = P(both, None)
    return jax.shard_map(
        on_device,
        mesh=mesh,
        in_specs=(
            P("seq", "blk", None),
            P("seq", "blk", None),
            P("seq", None),
            split,
            split,
            split,
            split,
            P(None, both),
            P(both),
        ),
        out_specs=(
            P("seq", "blk", None),
            P("seq", "blk", None),
            split,
            split,
            split,
            split,
            P(None, both),
            P(both),
        ),
        check_vma=False,
    )
```

profile of v0, /device:TPU:0, one launch (start us, length us, event | category | flops | bytes accessed | tf_op | source)
XLA Modules:
  0.0 476.2 jit_solution(11915102437641689824)
XLA Ops:
  2.1 4.1 collective-permute-start.11
  9.1 2.4 collective-permute-start
  19.4 3.0 collective-permute-start.25
  29.6 6.2 %collective-permute-start.22 = (bf16[96,768]{1,0:T(8,128)(2,1)S(1)}, bf16[96,768]{1,0:T(8,128)(2,1)S(1)}, u32[]{:S(2)}, u32[]{:S(2)}) collective-permute-start(bf16[96,768]{1,0:T(8,128)(2,1)S(1)} %copy-done.38), channel_id=1, source_target_pairs={{0,2},{1,3},{2,0},{3,1},{4,6},{5,7},{6,4},{7,5},{8,10},{9,11},{10,... | collective-permute-start | bytes 442376 | tf_op jit(solution)/shard_map/ppermute | solution.py:204
  35.9 4.6 collective-permute-done.22
  40.8 2.6 collective-permute-done.19
  44.0 7.6 %collective-permute-done.20 = bf16[2,24,3072]{2,1,0:T(8,128)(2,1)S(1)} collective-permute-done((bf16[2,24,3072]{2,1,0:T(8,128)(2,1)S(1)}, bf16[2,24,3072]{2,1,0:T(8,128)(2,1)S(1)}, u32[]{:S(2)}, u32[]{:S(2)}) %collective-permute-start.20) | collective-permute-done | bytes 294944 | tf_op jit(solution)/shard_map/ppermute | solution.py:204
  57.3 2.6 slice_reduce_fusion
  59.9 2.7 select_reduce_fusion
  66.7 2.7 add_convert_fusion.9
  72.5 3.1 collective-permute-start.6
  75.6 2.1 add_convert_fusion.6
  85.3 6.6 %collective-permute-done.6.refs_2_ = bf16[192,640]{1,0:T(8,128)(2,1)S(1)} collective-permute-done((bf16[192,640]{1,0:T(8,128)(2,1)}, bf16[192,640]{1,0:T(8,128)(2,1)S(1)}, u32[]{:S(2)}, u32[]{:S(2)}) %collective-permute-start.6) | collective-permute-done | bytes 245792 | tf_op jit(solution)/shard_map/ppermute | solution.py:204
  91.9 5.6 %collective-permute-start.16 = (bf16[192,640]{1,0:T(8,128)(2,1)S(1)}, bf16[192,640]{1,0:T(8,128)(2,1)S(1)}, u32[]{:S(2)}, u32[]{:S(2)}) collective-permute-start(bf16[192,640]{1,0:T(8,128)(2,1)S(1)} %copy-done.37), channel_id=1, source_target_pairs={{0,1},{1,0},{2,3},{3,2},{4,5},{5,4},{6,7},{7,6},{8,9},{9,8},{10,11... | collective-permute-start | bytes 737288 | tf_op jit(solution)/shard_map/ppermute | solution.py:204
  98.5 7.3 %attend.3 = (bf16[192,2560]{1,0:T(8,128)(2,1)S(1)}, bf16[64,2560]{1,0:T(8,128)(2,1)S(1)}, f32[5,512]{1,0:T(8,128)S(1)}, bf16[64,640]{1,0:T(8,128)(2,1)S(1)}, bf1...) custom-call(s32[1,5]{1,0:T(1,128)S(1)} %copy-done, s32[1]{0:T(128)} %bitcast.16.here, ...), custom_call_target="tpu_custom_call" | custom-call | flops 10000000000 | bytes 1000000 | tf_op jit(solution)/shard_map/attend/pallas_call | solution.py:147
  107.4 2.4 collective-permute-start.10
  109.9 9.7 %collective-permute-done.17.refs_2_ = bf16[192,640]{1,0:T(8,128)(2,1)S(1)} collective-permute-done((bf16[192,640]{1,0:T(8,128)(2,1)S(1)}, bf16[192,640]{1,0:T(8,128)(2,1)S(1)}, u32[]{:S(2)}, u32[]{:S(2)}) %collective-permute-start.17) | collective-permute-done | bytes 245792 | tf_op jit(solution)/shard_map/ppermute | solution.py:204
  119.5 5.4 %collective-permute-start.31 = (bf16[192,640]{1,0:T(8,128)(2,1)S(1)}, bf16[192,640]{1,0:T(8,128)(2,1)S(1)}, u32[]{:S(2)}, u32[]{:S(2)}) collective-permute-start(bf16[192,640]{1,0:T(8,128)(2,1)S(1)} %get-tuple-element.165), channel_id=1, source_target_pairs={{0,1},{1,0},{2,3},{3,2},{4,5},{5,4},{6,7},{7,6},{8,9},{9,8},{10,11... | collective-permute-start | bytes 737288 | tf_op jit(solution)/shard_map/ppermute | solution.py:204
  125.1 2.4 collective-permute-start.33
  128.9 7.5 %attend.4 = (bf16[192,2560]{1,0:T(8,128)(2,1)S(1)}, bf16[64,2560]{1,0:T(8,128)(2,1)S(1)}, f32[5,512]{1,0:T(8,128)S(1)}, bf16[64,640]{1,0:T(8,128)(2,1)S(1)}, bf1...) custom-call(s32[1,5]{1,0:T(1,128)S(1)} %copy-done, s32[1]{0:T(128)} %bitcast.16.here, ...), custom_call_target="tpu_custom_call" | custom-call | flops 10000000000 | bytes 1000000 | tf_op jit(solution)/shard_map/attend/pallas_call | solution.py:147
  138.5 10.2 %collective-permute-done.32.refs_2_ = bf16[192,640]{1,0:T(8,128)(2,1)S(1)} collective-permute-done((bf16[192,640]{1,0:T(8,128)(2,1)S(1)}, bf16[192,640]{1,0:T(8,128)(2,1)S(1)}, u32[]{:S(2)}, u32[]{:S(2)}) %collective-permute-start.32) | collective-permute-done | bytes 245792 | tf_op jit(solution)/shard_map/ppermute | solution.py:204
  149.1 7.3 %attend.5 = (bf16[192,2560]{1,0:T(8,128)(2,1)S(1)}, bf16[64,2560]{1,0:T(8,128)(2,1)S(1)}, f32[5,512]{1,0:T(8,128)S(1)}, bf16[64,640]{1,0:T(8,128)(2,1)S(1)}, bf1...) custom-call(s32[1,5]{1,0:T(1,128)S(1)} %copy-done, s32[1]{0:T(128)} %bitcast.16.here, ...), custom_call_target="tpu_custom_call" | custom-call | flops 10000000000 | bytes 1000000 | tf_op jit(solution)/shard_map/attend/pallas_call | solution.py:147
  157.5 2.2 collective-permute-start.39
  159.6 6.7 %collective-permute-start.34 = (bf16[64,640]{1,0:T(8,128)(2,1)S(1)}, bf16[64,640]{1,0:T(8,128)(2,1)S(1)}, u32[]{:S(2)}, u32[]{:S(2)}) collective-permute-start(bf16[64,640]{1,0:T(8,128)(2,1)S(1)} %get-tuple-element.169), channel_id=1, source_target_pairs={{0,1},{1,0},{2,3},{3,2},{4,5},{5,4},{6,7},{7,6},{8,9},{9,8},{10,11... | collective-permute-start | bytes 245768 | tf_op jit(solution)/shard_map/ppermute | solution.py:204
  168.8 3.1 collective-permute-start.36
  171.9 3.3 collective-permute-done.35
  175.2 9.7 %collective-permute-done.41 = bf16[2,2,2,96,768]{4,3,2,1,0:T(8,128)(2,1)S(1)} collective-permute-done((bf16[2,2,2,96,768]{4,3,2,1,0:T(8,128)(2,1)S(1)}, bf16[2,2,2,96,768]{4,3,2,1,0:T(8,128)(2,1)S(1)}, u32[]{:S(2)}, u32[]{:S(2)}) %collective-permute-start.41) | collective-permute-done | bytes 1179680 | tf_op jit(solution)/shard_map/ppermute | solution.py:204
  190.6 2.6 collective-permute-done.40
  194.0 8.1 %multiply_convert_fusion = (bf16[640,3072]{1,0:T(8,128)(2,1)}, f32[640,3072]{1,0:T(8,128)}) fusion(f32[3072]{0:T(1024)S(1)} %reshape.913, bf16[768,3072]{1,0:T(8,128)(2,1)S(1)} %bitcast.431, f32[640,768]{1,0:T(8,128)S(1)} %get-tuple-element.450, f32[768]{0:T(1024)S(1)} %get-tuple-element.292, f32[768]{0:T(1024)S(1)} %get-tuple-element.293, ...), kind=kOutput, calls=%fused_computation.9 | convolution fusion | flops 3042017280 | bytes 18504704 | tf_op jit(solution)/shard_map/dot_general | solution.py:34
  202.1 11.4 %fusion.75 = (bf16[3072]{0:T(1024)(128)(2,1)S(1)}, bf16[640,3072]{1,0:T(8,128)(2,1)}) fusion(f32[640,3072]{1,0:T(8,128)} %get-tuple-element.452, f32[3072]{0:T(1024)S(1)} %reshape.913, bf16[3072,768]{1,0:T(8,128)(2,1)S(1)} %bitcast.429, bf16[1,640,768]{2,1,0:T(8,128)(2,1)S(1)} %copy-done.27, f32[640]{0:T(1024)S(1)} %fusion.59), kind=kOutput, calls=%fused_computation.362 | convolution fusion | flops 3064624128 | bytes 17519104 | tf_op jit(solution)/shard_map/dot_general | solution.py:34
  213.5 5.9 %multiply_reduce_fusion = (bf16[768]{0:T(1024)(128)(2,1)S(1)}, f32[640]{0:T(1024)S(1)}, f32[640]{0:T(1024)S(1)}, bf16[768]{0:T(1024)(128)(2,1)S(1)}, f32[640,768]{1,0:T(8,128)S(1)}) fusion(f32[640,768]{1,0:T(8,128)S(1)} %get-tuple-element.450, f32[640]{0:T(1024)S(1)} %add_rsqrt_fusion, f32[640]{0:T(1024)S(1)} %broadcast_multiply_fusion.4, ...), kind=kOutput, calls=%fused_computation.48 | convolution fusion | flops 3024319744 | bytes 12599296 | tf_op jit(solution)/shard_map/dot_general | solution.py:34
  219.4 2.3 fusion.64
  223.7 6.7 %collective-permute-start.43 = (bf16[64,640]{1,0:T(8,128)(2,1)S(1)}, bf16[64,640]{1,0:T(8,128)(2,1)S(1)}, u32[]{:S(2)}, u32[]{:S(2)}) collective-permute-start(bf16[64,640]{1,0:T(8,128)(2,1)S(1)} %get-tuple-element.184), channel_id=1, source_target_pairs={{0,1},{1,0},{2,3},{3,2},{4,5},{5,4},{6,7},{7,6},{8,9},{9,8},{10,11... | collective-permute-start | bytes 245768 | tf_op jit(solution)/shard_map/ppermute | solution.py:204
  233.2 4.2 multiply_add_fusion.1
  237.4 2.5 collective-permute-done.44.refs_2_
  239.9 17.7 %attend_back.3 = (bf16[192,640]{1,0:T(8,128)(2,1)S(1)}, bf16[192,640]{1,0:T(8,128)(2,1)S(1)}, bf16[192,640]{1,0:T(8,128)(2,1)S(1)}, bf16[192,640]{1,0:T(8,128)(2,1)S(1)}) custom-call(s32[1,5]{1,0:T(1,128)S(1)} %copy-done, s32[1]{0:T(128)} %bitcast.16.here, bf16[192,2560]{1,0:T(8,128)(2,1)S(1)} %get-tuple-element.180.packed, ...), custom_call_target="tpu_custom_call" | custom-call | flops 15000000512 | bytes 1000000 | tf_op jit(solution)/shard_map/attend_back/pallas_call | solution.py:172
  257.6 6.5 %convolution_convert_fusion = bf16[768,3072]{1,0:T(8,128)(2,1)} fusion(bf16[640,3072]{1,0:T(8,128)(2,1)S(1)} %copy-done.66, f32[640,768]{1,0:T(8,128)S(1)} %get-tuple-element.450, f32[768]{0:T(1024)S(1)} %get-tuple-element.292, f32[768]{0:T(1024)S(1)} %get-tuple-element.293, f32[640]{0:T(1024)S(1)} %add_rsqrt_fusion, f32[640]{0:T(1024)S(1)} %broadcast_multiply_fusion.4), kind=kOutput, calls=%fused_computation.14 | convolution fusion | flops 3024715776 | bytes 10628096 | tf_op jit(solution)/shard_map/dot_general | solution.py:34
  264.1 2.1 convolution_convert_fusion.5
  266.2 3.1 pad_maximum_fusion
  271.7 4.2 convolution_convert_fusion.1
  276.2 2.6 select_bitcast_fusion.2
  278.8 2.9 select_bitcast_fusion
  282.9 2.3 fusion.28
  293.2 2.4 collective-permute-start.46
  295.6 4.2 collective-permute-done.50.refs_2_
  299.8 2.6 collective-permute-start.55
  303.7 17.7 %attend_back.4 = (bf16[192,640]{1,0:T(8,128)(2,1)S(1)}, bf16[192,640]{1,0:T(8,128)(2,1)S(1)}, bf16[192,640]{1,0:T(8,128)(2,1)S(1)}, bf16[192,640]{1,0:T(8,128)(2,1)S(1)}) custom-call(s32[1,5]{1,0:T(1,128)S(1)} %copy-done, s32[1]{0:T(128)} %bitcast.16.here, bf16[192,2560]{1,0:T(8,128)(2,1)S(1)} %copy-done.2, bf16[64,2560]{1,0:T(8,128)(2,1)S(1)} %get-tuple-element.196.mixed, ...), custom_call_target="tpu_custom_call" | custom-call | flops 15000000512 | bytes 1000000 | tf_op jit(solution)/shard_map/attend_back/pallas_call | solution.py:172
  321.8 2.4 add_convert_fusion.1
  327.8 2.6 add_convert_fusion
  334.5 2.2 collective-permute-start.53
  338.4 18.1 %attend_back.5 = (bf16[192,640]{1,0:T(8,128)(2,1)S(1)}, bf16[192,640]{1,0:T(8,128)(2,1)S(1)}, bf16[192,640]{1,0:T(8,128)(2,1)S(1)}, bf16[192,640]{1,0:T(8,128)(2,1)S(1)}) custom-call(s32[1,5]{1,0:T(1,128)S(1)} %copy-done, s32[1]{0:T(128)} %bitcast.16.here, bf16[192,2560]{1,0:T(8,128)(2,1)S(1)} %get-tuple-element.214.packed, ...), custom_call_target="tpu_custom_call" | custom-call | flops 15000000512 | bytes 1000000 | tf_op jit(solution)/shard_map/attend_back/pallas_call | solution.py:172
  370.3 2.8 convolution_convert_fusion.4
  375.1 2.2 fusion.60
  378.9 3.6 fusion.20
  386.4 6.5 %collective-permute-done.64 = bf16[2,2,2,24,3840]{4,3,1,2,0:T(8,128)(2,1)} collective-permute-done((bf16[2,2,2,24,3840]{4,3,1,2,0:T(8,128)(2,1)}, bf16[2,2,2,24,3840]{4,3,1,2,0:T(8,128)(2,1)}, u32[]{:S(2)}, u32[]{:S(2)}) %collective-permute-start.64) | collective-permute-done | bytes 1474592 | tf_op jit(solution)/shard_map/ppermute | solution.py:204
  404.7 10.6 %collective-permute-start.71 = (bf16[2,96,768]{2,1,0:T(8,128)(2,1)}, bf16[2,96,768]{2,1,0:T(8,128)(2,1)}, u32[]{:S(2)}, u32[]{:S(2)}) collective-permute-start(bf16[2,96,768]{2,1,0:T(8,128)(2,1)} %get-tuple-element.392), channel_id=1, source_target_pairs={{0,1},{1,0},{2,3},{3,2},{4,5},{5,4},{6,7},{7,6},{8,9},{9,8},{10,11... | collective-permute-start | bytes 884744 | tf_op jit(solution)/shard_map/ppermute | solution.py:204
  415.3 3.5 convolution_convert_fusion.2
  427.4 2.8 select_reduce_fusion.1
  431.4 2.7 collective-permute-start.76
  441.4 5.6 %collective-permute-done.76 = bf16[24,3840]{1,0:T(8,128)(2,1)S(1)} collective-permute-done((bf16[24,3840]{1,0:T(8,128)(2,1)S(1)}, bf16[24,3840]{1,0:T(8,128)(2,1)S(1)}, u32[]{:S(2)}, u32[]{:S(2)}) %collective-permute-start.76) | collective-permute-done | bytes 184352 | tf_op jit(solution)/shard_map/ppermute | solution.py:204
  450.9 2.3 collective-permute-done.74
  456.1 2.6 collective-permute-done.78
  463.4 4.5 collective-permute-done.77
  468.3 4.7 collective-permute-done.80
  (471 shorter events, 148.7 us)
Async XLA Ops:
  24.4 11.4 %collective-permute-start.26 = (bf16[2,24,768]{2,1,0:T(8,128)(2,1)S(1)}, bf16[2,24,768]{2,1,0:T(8,128)(2,1)S(1)}, u32[]{:S(2)}, u32[]{:S(2)}) collective-permute-start(bf16[2,24,768]{2,1,0:T(8,128)(2,1)S(1)} %pad_maximum_fusion.28), channel_id=1, source_target_pairs={{0,1},{1,0},{2,3},{3,2},{4,5},{5,4},{6,7},{7,6},{8,9},{9,8},{10,11... | collective-permute-start | bytes 221192 | tf_op jit(solution)/shard_map/ppermute | solution.py:204
  26.5 14.1 %collective-permute-start.13 = (bf16[2,2,24,1152]{3,2,0,1:T(8,128)(2,1)S(1)}, bf16[2,2,24,1152]{3,2,0,1:T(8,128)(2,1)S(1)}, u32[]{:S(2)}, u32[]{:S(2)}) collective-permute-start(bf16[2,2,24,1152]{3,2,0,1:T(8,128)(2,1)S(1)} %pad_maximum_fusion.24), channel_id=1, source_target_pairs={{0,8},{4,12},{8,0},{12,4},{16,24},{20,28},{24,16},{28,20},{1,9},{5... | collective-permute-start | bytes 663560 | tf_op jit(solution)/shard_map/ppermute | solution.py:204
  28.1 15.7 %collective-permute-start.2 = (bf16[2,2,24,1280]{3,2,0,1:T(8,128)(2,1)S(1)}, bf16[2,2,24,1280]{3,2,0,1:T(8,128)(2,1)S(1)}, u32[]{:S(2)}, u32[]{:S(2)}) collective-permute-start(bf16[2,2,24,1280]{3,2,0,1:T(8,128)(2,1)S(1)} %pad_maximum_fusion.23), channel_id=1, source_target_pairs={{0,16},{4,20},{8,24},{12,28},{16,0},{20,4},{24,8},{28,12},{1,17},{... | collective-permute-start | bytes 737288 | tf_op jit(solution)/shard_map/ppermute | solution.py:204
  29.6 10.9 %collective-permute-start.22 = (bf16[96,768]{1,0:T(8,128)(2,1)S(1)}, bf16[96,768]{1,0:T(8,128)(2,1)S(1)}, u32[]{:S(2)}, u32[]{:S(2)}) collective-permute-start(bf16[96,768]{1,0:T(8,128)(2,1)S(1)} %copy-done.38), channel_id=1, source_target_pairs={{0,2},{1,3},{2,0},{3,1},{4,6},{5,7},{6,4},{7,5},{8,10},{9,11},{10,... | collective-permute-start | bytes 442376 | tf_op jit(solution)/shard_map/ppermute | solution.py:204
  40.5 11.1 %collective-permute-start.23 = (bf16[2,96,768]{2,1,0:T(8,128)(2,1)S(1)}, bf16[2,96,768]{2,1,0:T(8,128)(2,1)S(1)}, u32[]{:S(2)}, u32[]{:S(2)}) collective-permute-start(bf16[2,96,768]{2,1,0:T(8,128)(2,1)S(1)} %pad_maximum_fusion.21), channel_id=1, source_target_pairs={{0,1},{1,0},{2,3},{3,2},{4,5},{5,4},{6,7},{7,6},{8,9},{9,8},{10,11... | collective-permute-start | bytes 884744 | tf_op jit(solution)/shard_map/ppermute | solution.py:204
  40.8 11.0 %collective-permute-start.14 = (bf16[2,2,2,24,1152]{4,3,1,2,0:T(8,128)(2,1)S(1)}, bf16[2,2,2,24,1152]{4,3,1,2,0:T(8,128)(2,1)S(1)}, u32[]{:S(2)}, u32[]{:S(2)}) collective-permute-start(bf16[2,2,2,24,1152]{4,3,1,2,0:T(8,128)(2,1)S(1)} %pad_maximum_fusion.19), channel_id=1, source_target_pairs={{0,16},{4,20},{8,24},{12,28},{16,0},{20,4},{24,8},{28,12},{1,17},{... | collective-permute-start | bytes 1327112 | tf_op jit(solution)/shard_map/ppermute | solution.py:204
  43.9 8.9 %collective-permute-start.3 = (bf16[2,2,2,24,1280]{4,3,1,2,0:T(8,128)(2,1)S(1)}, bf16[2,2,2,24,1280]{4,3,1,2,0:T(8,128)(2,1)S(1)}, u32[]{:S(2)}, u32[]{:S(2)}) collective-permute-start(bf16[2,2,2,24,1280]{4,3,1,2,0:T(8,128)(2,1)S(1)} %pad_maximum_fusion.18), channel_id=1, source_target_pairs={{0,8},{4,12},{8,0},{12,4},{16,24},{20,28},{24,16},{28,20},{1,9},{5... | collective-permute-start | bytes 1474568 | tf_op jit(solution)/shard_map/ppermute | solution.py:204
  56.7 68.2 %collective-permute-start.24 = (bf16[2,2,96,768]{3,2,1,0:T(8,128)(2,1)S(1)}, bf16[2,2,96,768]{3,2,1,0:T(8,128)(2,1)S(1)}, u32[]{:S(2)}, u32[]{:S(2)}) collective-permute-start(bf16[2,2,96,768]{3,2,1,0:T(8,128)(2,1)S(1)} %pad_maximum_fusion.16), channel_id=1, source_target_pairs={{0,8},{4,12},{8,0},{12,4},{16,24},{20,28},{24,16},{28,20},{1,9},{5... | collective-permute-start | bytes 1769480 | tf_op jit(solution)/shard_map/ppermute | solution.py:204
  64.6 16.9 %collective-permute-start.27 = (bf16[2,2,24,768]{3,2,1,0:T(8,128)(2,1)S(1)}, bf16[2,2,24,768]{3,2,1,0:T(8,128)(2,1)S(1)}, u32[]{:S(2)}, u32[]{:S(2)}) collective-permute-start(bf16[2,2,24,768]{3,2,1,0:T(8,128)(2,1)S(1)} %pad_maximum_fusion.25), channel_id=1, source_target_pairs={{0,16},{4,20},{8,24},{12,28},{16,0},{20,4},{24,8},{28,12},{1,17},{... | collective-permute-start | bytes 442376 | tf_op jit(solution)/shard_map/ppermute | solution.py:204
  65.1 60.0 %collective-permute-start.21 = (bf16[2,2,24,3072]{3,2,1,0:T(8,128)(2,1)S(1)}, bf16[2,2,24,3072]{3,2,1,0:T(8,128)(2,1)}, u32[]{:S(2)}, u32[]{:S(2)}) collective-permute-start(bf16[2,2,24,3072]{3,2,1,0:T(8,128)(2,1)S(1)} %pad_maximum_fusion.15), channel_id=1, source_target_pairs={{0,16},{4,20},{8,24},{12,28},{16,0},{20,4},{24,8},{28,12},{1,17},{... | collective-permute-start | bytes 1769480 | tf_op jit(solution)/shard_map/ppermute | solution.py:204
  71.4 12.4 %collective-permute-start.5 = (bf16[192,640]{1,0:T(8,128)(2,1)}, bf16[192,640]{1,0:T(8,128)(2,1)S(1)}, u32[]{:S(2)}, u32[]{:S(2)}) collective-permute-start(bf16[192,640]{1,0:T(8,128)(2,1)} %get-tuple-element.136), channel_id=1, source_target_pairs={{0,1},{1,0},{2,3},{3,2},{4,5},{5,4},{6,7},{7,6},{8,9},{9,8},{10,11... | collective-permute-start | bytes 737288 | tf_op jit(solution)/shard_map/ppermute | solution.py:204
  72.5 19.4 %collective-permute-start.6 = (bf16[192,640]{1,0:T(8,128)(2,1)}, bf16[192,640]{1,0:T(8,128)(2,1)S(1)}, u32[]{:S(2)}, u32[]{:S(2)}) collective-permute-start(bf16[192,640]{1,0:T(8,128)(2,1)} %get-tuple-element.137), channel_id=1, source_target_pairs={{0,2},{1,3},{2,0},{3,1},{4,6},{5,7},{6,4},{7,5},{8,10},{9,11},{10,... | collective-permute-start | bytes 737288 | tf_op jit(solution)/shard_map/ppermute | solution.py:204
  82.2 9.7 %collective-permute-start.7 = (bf16[192,640]{1,0:T(8,128)(2,1)}, bf16[192,640]{1,0:T(8,128)(2,1)S(1)}, u32[]{:S(2)}, u32[]{:S(2)}) collective-permute-start(bf16[192,640]{1,0:T(8,128)(2,1)} %get-tuple-element.138), channel_id=1, source_target_pairs={{0,3},{1,2},{2,1},{3,0},{4,7},{5,6},{6,5},{7,4},{8,11},{9,10},{10,... | collective-permute-start | bytes 737288 | tf_op jit(solution)/shard_map/ppermute | solution.py:204
  83.9 21.9 %collective-permute-start.37 = (bf16[2,2,2,24,768]{4,3,2,1,0:T(8,128)(2,1)S(1)}, bf16[2,2,2,24,768]{4,3,2,1,0:T(8,128)(2,1)S(1)}, u32[]{:S(2)}, u32[]{:S(2)}) collective-permute-start(bf16[2,2,2,24,768]{4,3,2,1,0:T(8,128)(2,1)S(1)} %pad_maximum_fusion.22), channel_id=1, source_target_pairs={{0,8},{4,12},{8,0},{12,4},{16,24},{20,28},{24,16},{28,20},{1,9},{5... | collective-permute-start | bytes 884744 | tf_op jit(solution)/shard_map/ppermute | solution.py:204
  91.9 15.5 %collective-permute-start.16 = (bf16[192,640]{1,0:T(8,128)(2,1)S(1)}, bf16[192,640]{1,0:T(8,128)(2,1)S(1)}, u32[]{:S(2)}, u32[]{:S(2)}) collective-permute-start(bf16[192,640]{1,0:T(8,128)(2,1)S(1)} %copy-done.37), channel_id=1, source_target_pairs={{0,1},{1,0},{2,3},{3,2},{4,5},{5,4},{6,7},{7,6},{8,9},{9,8},{10,11... | collective-permute-start | bytes 737288 | tf_op jit(solution)/shard_map/ppermute | solution.py:204
  97.5 22.0 %collective-permute-start.17 = (bf16[192,640]{1,0:T(8,128)(2,1)S(1)}, bf16[192,640]{1,0:T(8,128)(2,1)S(1)}, u32[]{:S(2)}, u32[]{:S(2)}) collective-permute-start(bf16[192,640]{1,0:T(8,128)(2,1)S(1)} %copy-done.36), channel_id=1, source_target_pairs={{0,2},{1,3},{2,0},{3,1},{4,6},{5,7},{6,4},{7,5},{8,10},{9,11},{10,... | collective-permute-start | bytes 737288 | tf_op jit(solution)/shard_map/ppermute | solution.py:204
  105.8 13.8 %collective-permute-start.18 = (bf16[192,640]{1,0:T(8,128)(2,1)S(1)}, bf16[192,640]{1,0:T(8,128)(2,1)S(1)}, u32[]{:S(2)}, u32[]{:S(2)}) collective-permute-start(bf16[192,640]{1,0:T(8,128)(2,1)S(1)} %copy-done.35), channel_id=1, source_target_pairs={{0,3},{1,2},{2,1},{3,0},{4,7},{5,6},{6,5},{7,4},{8,11},{9,10},{10,... | collective-permute-start | bytes 737288 | tf_op jit(solution)/shard_map/ppermute | solution.py:204
  107.4 28.9 %collective-permute-start.10 = (bf16[64,640]{1,0:T(8,128)(2,1)S(1)}, bf16[64,640]{1,0:T(8,128)(2,1)S(1)}, u32[]{:S(2)}, u32[]{:S(2)}) collective-permute-start(bf16[64,640]{1,0:T(8,128)(2,1)S(1)} %get-tuple-element.142), channel_id=1, source_target_pairs={{0,3},{1,2},{2,1},{3,0},{4,7},{5,6},{6,5},{7,4},{8,11},{9,10},{10,... | collective-permute-start | bytes 245768 | tf_op jit(solution)/shard_map/ppermute | solution.py:204
  119.5 36.9 %collective-permute-start.8 = (bf16[64,640]{1,0:T(8,128)(2,1)S(1)}, bf16[64,640]{1,0:T(8,128)(2,1)S(1)}, u32[]{:S(2)}, u32[]{:S(2)}) collective-permute-start(bf16[64,640]{1,0:T(8,128)(2,1)S(1)} %get-tuple-element.140), channel_id=1, source_target_pairs={{0,1},{1,0},{2,3},{3,2},{4,5},{5,4},{6,7},{7,6},{8,9},{9,8},{10,11... | collective-permute-start | bytes 245768 | tf_op jit(solution)/shard_map/ppermute | solution.py:204
  119.5 17.5 %collective-permute-start.31 = (bf16[192,640]{1,0:T(8,128)(2,1)S(1)}, bf16[192,640]{1,0:T(8,128)(2,1)S(1)}, u32[]{:S(2)}, u32[]{:S(2)}) collective-permute-start(bf16[192,640]{1,0:T(8,128)(2,1)S(1)} %get-tuple-element.165), channel_id=1, source_target_pairs={{0,1},{1,0},{2,3},{3,2},{4,5},{5,4},{6,7},{7,6},{8,9},{9,8},{10,11... | collective-permute-start | bytes 737288 | tf_op jit(solution)/shard_map/ppermute | solution.py:204
  124.9 23.8 %collective-permute-start.32 = (bf16[192,640]{1,0:T(8,128)(2,1)S(1)}, bf16[192,640]{1,0:T(8,128)(2,1)S(1)}, u32[]{:S(2)}, u32[]{:S(2)}) collective-permute-start(bf16[192,640]{1,0:T(8,128)(2,1)S(1)} %get-tuple-element.166), channel_id=1, source_target_pairs={{0,2},{1,3},{2,0},{3,1},{4,6},{5,7},{6,4},{7,5},{8,10},{9,11},{10,... | collective-permute-start | bytes 737288 | tf_op jit(solution)/shard_map/ppermute | solution.py:204
  125.1 23.6 %collective-permute-start.33 = (bf16[192,640]{1,0:T(8,128)(2,1)S(1)}, bf16[192,640]{1,0:T(8,128)(2,1)S(1)}, u32[]{:S(2)}, u32[]{:S(2)}) collective-permute-start(bf16[192,640]{1,0:T(8,128)(2,1)S(1)} %get-tuple-element.167), channel_id=1, source_target_pairs={{0,3},{1,2},{2,1},{3,0},{4,7},{5,6},{6,5},{7,4},{8,11},{9,10},{10,... | collective-permute-start | bytes 737288 | tf_op jit(solution)/shard_map/ppermute | solution.py:204
  136.4 20.1 %collective-permute-start.9 = (bf16[64,640]{1,0:T(8,128)(2,1)S(1)}, bf16[64,640]{1,0:T(8,128)(2,1)S(1)}, u32[]{:S(2)}, u32[]{:S(2)}) collective-permute-start(bf16[64,640]{1,0:T(8,128)(2,1)S(1)} %get-tuple-element.141), channel_id=1, source_target_pairs={{0,2},{1,3},{2,0},{3,1},{4,6},{5,7},{6,4},{7,5},{8,10},{9,11},{10,... | collective-permute-start | bytes 245768 | tf_op jit(solution)/shard_map/ppermute | solution.py:204
  137.0 20.4 %collective-permute-start.28 = (bf16[64,640]{1,0:T(8,128)(2,1)S(1)}, bf16[64,640]{1,0:T(8,128)(2,1)S(1)}, u32[]{:S(2)}, u32[]{:S(2)}) collective-permute-start(bf16[64,640]{1,0:T(8,128)(2,1)S(1)} %get-tuple-element.161), channel_id=1, source_target_pairs={{0,1},{1,0},{2,3},{3,2},{4,5},{5,4},{6,7},{7,6},{8,9},{9,8},{10,11... | collective-permute-start | bytes 245768 | tf_op jit(solution)/shard_map/ppermute | solution.py:204
  148.7 10.9 %collective-permute-start.29 = (bf16[64,640]{1,0:T(8,128)(2,1)S(1)}, bf16[64,640]{1,0:T(8,128)(2,1)S(1)}, u32[]{:S(2)}, u32[]{:S(2)}) collective-permute-start(bf16[64,640]{1,0:T(8,128)(2,1)S(1)} %get-tuple-element.162), channel_id=1, source_target_pairs={{0,2},{1,3},{2,0},{3,1},{4,6},{5,7},{6,4},{7,5},{8,10},{9,11},{10,... | collective-permute-start | bytes 245768 | tf_op jit(solution)/shard_map/ppermute | solution.py:204
  148.7 17.6 %collective-permute-start.30 = (bf16[64,640]{1,0:T(8,128)(2,1)S(1)}, bf16[64,640]{1,0:T(8,128)(2,1)S(1)}, u32[]{:S(2)}, u32[]{:S(2)}) collective-permute-start(bf16[64,640]{1,0:T(8,128)(2,1)S(1)} %get-tuple-element.163), channel_id=1, source_target_pairs={{0,3},{1,2},{2,1},{3,0},{4,7},{5,6},{6,5},{7,4},{8,11},{9,10},{10,... | collective-permute-start | bytes 245768 | tf_op jit(solution)/shard_map/ppermute | solution.py:204
  156.4 30.1 %collective-permute-start.38 = (bf16[2,2,2,2,24,768]{5,4,3,2,1,0:T(8,128)(2,1)S(1)}, bf16[2,2,2,2,24,768]{5,4,3,2,1,0:T(8,128)(2,1)S(1)}, u32[]{:S(2)}, u32[]{:S(2)}) collective-permute-start(bf16[2,2,2,2,24,768]{5,4,3,2,1,0:T(8,128)(2,1)S(1)} %pad_maximum_fusion.17), channel_id=1, source_target_pairs={{0,4},{4,0},{8,12},{12,8},{16,20},{20,16},{24,28},{28,24},{1,5},{5... | collective-permute-start | bytes 1769480 | tf_op jit(solution)/shard_map/ppermute | solution.py:204
  156.5 28.4 %collective-permute-start.41 = (bf16[2,2,2,96,768]{4,3,2,1,0:T(8,128)(2,1)S(1)}, bf16[2,2,2,96,768]{4,3,2,1,0:T(8,128)(2,1)S(1)}, u32[]{:S(2)}, u32[]{:S(2)}) collective-permute-start(bf16[2,2,2,96,768]{4,3,2,1,0:T(8,128)(2,1)S(1)} %pad_maximum_fusion.10), channel_id=1, source_target_pairs={{0,16},{4,20},{8,24},{12,28},{16,0},{20,4},{24,8},{28,12},{1,17},{... | collective-permute-start | bytes 3538952 | tf_op jit(solution)/shard_map/ppermute | solution.py:204
  157.5 28.4 %collective-permute-start.39 = (bf16[2,2,2,24,3072]{4,3,2,1,0:T(8,128)(2,1)S(1)}, bf16[2,2,2,24,3072]{4,3,2,1,0:T(8,128)(2,1)S(1)}, u32[]{:S(2)}, u32[]{:S(2)}) collective-permute-start(bf16[2,2,2,24,3072]{4,3,2,1,0:T(8,128)(2,1)S(1)} %pad_maximum_fusion.9), channel_id=1, source_target_pairs={{0,8},{4,12},{8,0},{12,4},{16,24},{20,28},{24,16},{28,20},{1,9},{5... | collective-permute-start | bytes 3538952 | tf_op jit(solution)/shard_map/ppermute | solution.py:204
  159.6 9.2 %collective-permute-start.34 = (bf16[64,640]{1,0:T(8,128)(2,1)S(1)}, bf16[64,640]{1,0:T(8,128)(2,1)S(1)}, u32[]{:S(2)}, u32[]{:S(2)}) collective-permute-start(bf16[64,640]{1,0:T(8,128)(2,1)S(1)} %get-tuple-element.169), channel_id=1, source_target_pairs={{0,1},{1,0},{2,3},{3,2},{4,5},{5,4},{6,7},{7,6},{8,9},{9,8},{10,11... | collective-permute-start | bytes 245768 | tf_op jit(solution)/shard_map/ppermute | solution.py:204
  166.4 8.8 %collective-permute-start.35 = (bf16[64,640]{1,0:T(8,128)(2,1)S(1)}, bf16[64,640]{1,0:T(8,128)(2,1)S(1)}, u32[]{:S(2)}, u32[]{:S(2)}) collective-permute-start(bf16[64,640]{1,0:T(8,128)(2,1)S(1)} %get-tuple-element.170), channel_id=1, source_target_pairs={{0,2},{1,3},{2,0},{3,1},{4,6},{5,7},{6,4},{7,5},{8,10},{9,11},{10,... | collective-permute-start | bytes 245768 | tf_op jit(solution)/shard_map/ppermute | solution.py:204
  168.8 17.5 %collective-permute-start.36 = (bf16[64,640]{1,0:T(8,128)(2,1)S(1)}, bf16[64,640]{1,0:T(8,128)(2,1)S(1)}, u32[]{:S(2)}, u32[]{:S(2)}) collective-permute-start(bf16[64,640]{1,0:T(8,128)(2,1)S(1)} %get-tuple-element.171), channel_id=1, source_target_pairs={{0,3},{1,2},{2,1},{3,0},{4,7},{5,6},{6,5},{7,4},{8,11},{9,10},{10,... | collective-permute-start | bytes 245768 | tf_op jit(solution)/shard_map/ppermute | solution.py:204
  223.7 13.7 %collective-permute-start.43 = (bf16[64,640]{1,0:T(8,128)(2,1)S(1)}, bf16[64,640]{1,0:T(8,128)(2,1)S(1)}, u32[]{:S(2)}, u32[]{:S(2)}) collective-permute-start(bf16[64,640]{1,0:T(8,128)(2,1)S(1)} %get-tuple-element.184), channel_id=1, source_target_pairs={{0,1},{1,0},{2,3},{3,2},{4,5},{5,4},{6,7},{7,6},{8,9},{9,8},{10,11... | collective-permute-start | bytes 245768 | tf_op jit(solution)/shard_map/ppermute | solution.py:204
  230.4 9.5 %collective-permute-start.44 = (bf16[64,640]{1,0:T(8,128)(2,1)S(1)}, bf16[64,640]{1,0:T(8,128)(2,1)S(1)}, u32[]{:S(2)}, u32[]{:S(2)}) collective-permute-start(bf16[64,640]{1,0:T(8,128)(2,1)S(1)} %get-tuple-element.185), channel_id=1, source_target_pairs={{0,2},{1,3},{2,0},{3,1},{4,6},{5,7},{6,4},{7,5},{8,10},{9,11},{10,... | collective-permute-start | bytes 245768 | tf_op jit(solution)/shard_map/ppermute | solution.py:204
  231.8 8.1 %collective-permute-start.45 = (bf16[64,640]{1,0:T(8,128)(2,1)S(1)}, bf16[64,640]{1,0:T(8,128)(2,1)S(1)}, u32[]{:S(2)}, u32[]{:S(2)}) collective-permute-start(bf16[64,640]{1,0:T(8,128)(2,1)S(1)} %get-tuple-element.186), channel_id=1, source_target_pairs={{0,3},{1,2},{2,1},{3,0},{4,7},{5,6},{6,5},{7,4},{8,11},{9,10},{10,... | collective-permute-start | bytes 245768 | tf_op jit(solution)/shard_map/ppermute | solution.py:204
  278.8 42.6 %collective-permute-start.58 = (bf16[2,2,2,2,96,768]{5,4,2,3,1,0:T(8,128)(2,1)}, bf16[2,2,2,2,96,768]{5,4,2,3,1,0:T(8,128)(2,1)}, u32[]{:S(2)}, u32[]{:S(2)}) collective-permute-start(bf16[2,2,2,2,96,768]{5,4,2,3,1,0:T(8,128)(2,1)} %get-tuple-element.326), channel_id=1, source_target_pairs={{0,4},{4,0},{8,12},{12,8},{16,20},{20,16},{24,28},{28,24},{1,5},{5... | collective-permute-start | bytes 7077896 | tf_op jit(solution)/shard_map/ppermute | solution.py:204
  281.7 44.0 %collective-permute-start.59 = (bf16[2,2,2,2,24,3840]{5,4,2,3,0,1:T(8,128)(2,1)}, bf16[2,2,2,2,24,3840]{5,4,2,3,0,1:T(8,128)(2,1)}, u32[]{:S(2)}, u32[]{:S(2)}) collective-permute-start(bf16[2,2,2,2,24,3840]{5,4,2,3,0,1:T(8,128)(2,1)} %get-tuple-element.322), channel_id=1, source_target_pairs={{0,4},{4,0},{8,12},{12,8},{16,20},{20,16},{24,28},{28,24},{1,5},{5... | collective-permute-start | bytes 8847368 | tf_op jit(solution)/shard_map/ppermute | solution.py:204
  290.4 9.4 %collective-permute-start.50 = (bf16[64,640]{1,0:T(8,128)(2,1)S(1)}, bf16[64,640]{1,0:T(8,128)(2,1)S(1)}, u32[]{:S(2)}, u32[]{:S(2)}) collective-permute-start(bf16[64,640]{1,0:T(8,128)(2,1)S(1)} %get-tuple-element.200), channel_id=1, source_target_pairs={{0,2},{1,3},{2,0},{3,1},{4,6},{5,7},{6,4},{7,5},{8,10},{9,11},{10,... | collective-permute-start | bytes 245768 | tf_op jit(solution)/shard_map/ppermute | solution.py:204
  291.5 8.3 %collective-permute-start.51 = (bf16[64,640]{1,0:T(8,128)(2,1)S(1)}, bf16[64,640]{1,0:T(8,128)(2,1)S(1)}, u32[]{:S(2)}, u32[]{:S(2)}) collective-permute-start(bf16[64,640]{1,0:T(8,128)(2,1)S(1)} %get-tuple-element.201), channel_id=1, source_target_pairs={{0,3},{1,2},{2,1},{3,0},{4,7},{5,6},{6,5},{7,4},{8,11},{9,10},{10,... | collective-permute-start | bytes 245768 | tf_op jit(solution)/shard_map/ppermute | solution.py:204
  293.2 43.4 %collective-permute-start.46 = (bf16[192,640]{1,0:T(8,128)(2,1)S(1)}, bf16[192,640]{1,0:T(8,128)(2,1)S(1)}, u32[]{:S(2)}, u32[]{:S(2)}) collective-permute-start(bf16[192,640]{1,0:T(8,128)(2,1)S(1)} %get-tuple-element.192), channel_id=1, source_target_pairs={{0,1},{1,0},{2,3},{3,2},{4,5},{5,4},{6,7},{7,6},{8,9},{9,8},{10,11... | collective-permute-start | bytes 737288 | tf_op jit(solution)/shard_map/ppermute | solution.py:204
  299.8 56.7 %collective-permute-start.47 = (bf16[192,640]{1,0:T(8,128)(2,1)S(1)}, bf16[192,640]{1,0:T(8,128)(2,1)S(1)}, u32[]{:S(2)}, u32[]{:S(2)}) collective-permute-start(bf16[192,640]{1,0:T(8,128)(2,1)S(1)} %get-tuple-element.193), channel_id=1, source_target_pairs={{0,2},{1,3},{2,0},{3,1},{4,6},{5,7},{6,4},{7,5},{8,10},{9,11},{10,... | collective-permute-start | bytes 737288 | tf_op jit(solution)/shard_map/ppermute | solution.py:204
  299.8 32.4 %collective-permute-start.55 = (bf16[64,640]{1,0:T(8,128)(2,1)S(1)}, bf16[64,640]{1,0:T(8,128)(2,1)S(1)}, u32[]{:S(2)}, u32[]{:S(2)}) collective-permute-start(bf16[64,640]{1,0:T(8,128)(2,1)S(1)} %get-tuple-element.218), channel_id=1, source_target_pairs={{0,1},{1,0},{2,3},{3,2},{4,5},{5,4},{6,7},{7,6},{8,9},{9,8},{10,11... | collective-permute-start | bytes 245768 | tf_op jit(solution)/shard_map/ppermute | solution.py:204
  321.4 12.6 %collective-permute-start.56 = (bf16[64,640]{1,0:T(8,128)(2,1)S(1)}, bf16[64,640]{1,0:T(8,128)(2,1)S(1)}, u32[]{:S(2)}, u32[]{:S(2)}) collective-permute-start(bf16[64,640]{1,0:T(8,128)(2,1)S(1)} %get-tuple-element.219), channel_id=1, source_target_pairs={{0,2},{1,3},{2,0},{3,1},{4,6},{5,7},{6,4},{7,5},{8,10},{9,11},{10,... | collective-permute-start | bytes 245768 | tf_op jit(solution)/shard_map/ppermute | solution.py:204
  325.7 8.7 %collective-permute-start.57 = (bf16[64,640]{1,0:T(8,128)(2,1)S(1)}, bf16[64,640]{1,0:T(8,128)(2,1)S(1)}, u32[]{:S(2)}, u32[]{:S(2)}) collective-permute-start(bf16[64,640]{1,0:T(8,128)(2,1)S(1)} %get-tuple-element.220), channel_id=1, source_target_pairs={{0,3},{1,2},{2,1},{3,0},{4,7},{5,6},{6,5},{7,4},{8,11},{9,10},{10,... | collective-permute-start | bytes 245768 | tf_op jit(solution)/shard_map/ppermute | solution.py:204
  332.2 25.2 %collective-permute-start.48 = (bf16[192,640]{1,0:T(8,128)(2,1)S(1)}, bf16[192,640]{1,0:T(8,128)(2,1)S(1)}, u32[]{:S(2)}, u32[]{:S(2)}) collective-permute-start(bf16[192,640]{1,0:T(8,128)(2,1)S(1)} %get-tuple-element.194), channel_id=1, source_target_pairs={{0,3},{1,2},{2,1},{3,0},{4,7},{5,6},{6,5},{7,4},{8,11},{9,10},{10,... | collective-permute-start | bytes 737288 | tf_op jit(solution)/shard_map/ppermute | solution.py:204
  334.0 25.2 %collective-permute-start.52 = (bf16[192,640]{1,0:T(8,128)(2,1)S(1)}, bf16[192,640]{1,0:T(8,128)(2,1)S(1)}, u32[]{:S(2)}, u32[]{:S(2)}) collective-permute-start(bf16[192,640]{1,0:T(8,128)(2,1)S(1)} %get-tuple-element.211), channel_id=1, source_target_pairs={{0,1},{1,0},{2,3},{3,2},{4,5},{5,4},{6,7},{7,6},{8,9},{9,8},{10,11... | collective-permute-start | bytes 737288 | tf_op jit(solution)/shard_map/ppermute | solution.py:204
  334.5 26.3 %collective-permute-start.53 = (bf16[192,640]{1,0:T(8,128)(2,1)S(1)}, bf16[192,640]{1,0:T(8,128)(2,1)S(1)}, u32[]{:S(2)}, u32[]{:S(2)}) collective-permute-start(bf16[192,640]{1,0:T(8,128)(2,1)S(1)} %get-tuple-element.212), channel_id=1, source_target_pairs={{0,2},{1,3},{2,0},{3,1},{4,6},{5,7},{6,4},{7,5},{8,10},{9,11},{10,... | collective-permute-start | bytes 737288 | tf_op jit(solution)/shard_map/ppermute | solution.py:204
  336.6 25.4 %collective-permute-start.54 = (bf16[192,640]{1,0:T(8,128)(2,1)S(1)}, bf16[192,640]{1,0:T(8,128)(2,1)S(1)}, u32[]{:S(2)}, u32[]{:S(2)}) collective-permute-start(bf16[192,640]{1,0:T(8,128)(2,1)S(1)} %get-tuple-element.213), channel_id=1, source_target_pairs={{0,3},{1,2},{2,1},{3,0},{4,7},{5,6},{6,5},{7,4},{8,11},{9,10},{10,... | collective-permute-start | bytes 737288 | tf_op jit(solution)/shard_map/ppermute | solution.py:204
  356.5 25.9 %collective-permute-start.63 = (bf16[2,2,2,96,768]{4,3,1,2,0:T(8,128)(2,1)}, bf16[2,2,2,96,768]{4,3,1,2,0:T(8,128)(2,1)}, u32[]{:S(2)}, u32[]{:S(2)}) collective-permute-start(bf16[2,2,2,96,768]{4,3,1,2,0:T(8,128)(2,1)} %get-tuple-element.340), channel_id=1, source_target_pairs={{0,16},{4,20},{8,24},{12,28},{16,0},{20,4},{24,8},{28,12},{1,17},{... | collective-permute-start | bytes 3538952 | tf_op jit(solution)/shard_map/ppermute | solution.py:204
  357.5 35.5 %collective-permute-start.64 = (bf16[2,2,2,24,3840]{4,3,1,2,0:T(8,128)(2,1)}, bf16[2,2,2,24,3840]{4,3,1,2,0:T(8,128)(2,1)}, u32[]{:S(2)}, u32[]{:S(2)}) collective-permute-start(bf16[2,2,2,24,3840]{4,3,1,2,0:T(8,128)(2,1)} %get-tuple-element.334), channel_id=1, source_target_pairs={{0,8},{4,12},{8,0},{12,4},{16,24},{20,28},{24,16},{28,20},{1,9},{5... | collective-permute-start | bytes 4423688 | tf_op jit(solution)/shard_map/ppermute | solution.py:204
  359.3 39.6 %collective-permute-start.60 = (bf16[192,640]{1,0:T(8,128)(2,1)S(1)}, bf16[192,640]{1,0:T(8,128)(2,1)S(1)}, u32[]{:S(2)}, u32[]{:S(2)}) collective-permute-start(bf16[192,640]{1,0:T(8,128)(2,1)S(1)} %get-tuple-element.228), channel_id=1, source_target_pairs={{0,1},{1,0},{2,3},{3,2},{4,5},{5,4},{6,7},{7,6},{8,9},{9,8},{10,11... | collective-permute-start | bytes 737288 | tf_op jit(solution)/shard_map/ppermute | solution.py:204
  360.8 38.1 %collective-permute-start.61 = (bf16[192,640]{1,0:T(8,128)(2,1)S(1)}, bf16[192,640]{1,0:T(8,128)(2,1)S(1)}, u32[]{:S(2)}, u32[]{:S(2)}) collective-permute-start(bf16[192,640]{1,0:T(8,128)(2,1)S(1)} %get-tuple-element.229), channel_id=1, source_target_pairs={{0,2},{1,3},{2,0},{3,1},{4,6},{5,7},{6,4},{7,5},{8,10},{9,11},{10,... | collective-permute-start | bytes 737288 | tf_op jit(solution)/shard_map/ppermute | solution.py:204
  362.1 36.9 %collective-permute-start.62 = (bf16[192,640]{1,0:T(8,128)(2,1)S(1)}, bf16[192,640]{1,0:T(8,128)(2,1)}, u32[]{:S(2)}, u32[]{:S(2)}) collective-permute-start(bf16[192,640]{1,0:T(8,128)(2,1)S(1)} %get-tuple-element.230), channel_id=1, source_target_pairs={{0,3},{1,2},{2,1},{3,0},{4,7},{5,6},{6,5},{7,4},{8,11},{9,10},{10,... | collective-permute-start | bytes 737288 | tf_op jit(solution)/shard_map/ppermute | solution.py:204
  385.2 17.1 %collective-permute-start.66 = (bf16[2,2,96,768]{3,2,0,1:T(8,128)(2,1)}, bf16[2,2,96,768]{3,2,0,1:T(8,128)(2,1)}, u32[]{:S(2)}, u32[]{:S(2)}) collective-permute-start(bf16[2,2,96,768]{3,2,0,1:T(8,128)(2,1)} %get-tuple-element.356), channel_id=1, source_target_pairs={{0,8},{4,12},{8,0},{12,4},{16,24},{20,28},{24,16},{28,20},{1,9},{5... | collective-permute-start | bytes 1769480 | tf_op jit(solution)/shard_map/ppermute | solution.py:204
  395.9 23.9 %collective-permute-start.67 = (bf16[2,2,24,3840]{3,2,0,1:T(8,128)(2,1)}, bf16[2,2,24,3840]{3,2,0,1:T(8,128)(2,1)}, u32[]{:S(2)}, u32[]{:S(2)}) collective-permute-start(bf16[2,2,24,3840]{3,2,0,1:T(8,128)(2,1)} %get-tuple-element.350), channel_id=1, source_target_pairs={{0,16},{4,20},{8,24},{12,28},{16,0},{20,4},{24,8},{28,12},{1,17},{... | collective-permute-start | bytes 2211848 | tf_op jit(solution)/shard_map/ppermute | solution.py:204
  398.9 23.6 %collective-permute-start.65 = (bf16[2,2,2,2,24,1536]{5,4,2,3,1,0:T(8,128)(2,1)}, bf16[2,2,2,2,24,1536]{5,4,2,3,1,0:T(8,128)(2,1)}, u32[]{:S(2)}, u32[]{:S(2)}) collective-permute-start(bf16[2,2,2,2,24,1536]{5,4,2,3,1,0:T(8,128)(2,1)} %get-tuple-element.336), channel_id=1, source_target_pairs={{0,4},{4,0},{8,12},{12,8},{16,20},{20,16},{24,28},{28,24},{1,5},{5... | collective-permute-start | bytes 3538952 | tf_op jit(solution)/shard_map/ppermute | solution.py:204
  404.7 26.7 %collective-permute-start.71 = (bf16[2,96,768]{2,1,0:T(8,128)(2,1)}, bf16[2,96,768]{2,1,0:T(8,128)(2,1)}, u32[]{:S(2)}, u32[]{:S(2)}) collective-permute-start(bf16[2,96,768]{2,1,0:T(8,128)(2,1)} %get-tuple-element.392), channel_id=1, source_target_pairs={{0,1},{1,0},{2,3},{3,2},{4,5},{5,4},{6,7},{7,6},{8,9},{9,8},{10,11... | collective-permute-start | bytes 884744 | tf_op jit(solution)/shard_map/ppermute | solution.py:204
  422.1 9.2 %collective-permute-start.72 = (bf16[2,24,3840]{2,1,0:T(8,128)(2,1)}, bf16[2,24,3840]{2,1,0:T(8,128)(2,1)S(1)}, u32[]{:S(2)}, u32[]{:S(2)}) collective-permute-start(bf16[2,24,3840]{2,1,0:T(8,128)(2,1)} %get-tuple-element.386), channel_id=1, source_target_pairs={{0,1},{1,0},{2,3},{3,2},{4,5},{5,4},{6,7},{7,6},{8,9},{9,8},{10,11... | collective-permute-start | bytes 1105928 | tf_op jit(solution)/shard_map/ppermute | solution.py:204
  424.3 13.5 %collective-permute-start.68 = (bf16[2,2,2,24,1536]{4,3,1,2,0:T(8,128)(2,1)S(1)}, bf16[2,2,2,24,1536]{4,3,1,2,0:T(8,128)(2,1)}, u32[]{:S(2)}, u32[]{:S(2)}) collective-permute-start(bf16[2,2,2,24,1536]{4,3,1,2,0:T(8,128)(2,1)S(1)} %get-tuple-element.354), channel_id=1, source_target_pairs={{0,16},{4,20},{8,24},{12,28},{16,0},{20,4},{24,8},{28,12},{1,17},{... | collective-permute-start | bytes 1769480 | tf_op jit(solution)/shard_map/ppermute | solution.py:204
  431.1 8.7 %collective-permute-start.70 = (bf16[2,2,2,2,24,896]{5,4,3,2,1,0:T(8,128)(2,1)S(1)}, bf16[2,2,2,2,24,896]{5,4,3,2,1,0:T(8,128)(2,1)S(1)}, u32[]{:S(2)}, u32[]{:S(2)}) collective-permute-start(bf16[2,2,2,2,24,896]{5,4,3,2,1,0:T(8,128)(2,1)S(1)} %get-tuple-element.352), channel_id=1, source_target_pairs={{0,4},{4,0},{8,12},{12,8},{16,20},{20,16},{24,28},{28,24},{1,5},{5... | collective-permute-start | bytes 2064392 | tf_op jit(solution)/shard_map/ppermute | solution.py:204
  431.4 15.6 %collective-permute-start.76 = (bf16[24,3840]{1,0:T(8,128)(2,1)S(1)}, bf16[24,3840]{1,0:T(8,128)(2,1)S(1)}, u32[]{:S(2)}, u32[]{:S(2)}) collective-permute-start(bf16[24,3840]{1,0:T(8,128)(2,1)S(1)} %get-tuple-element.404), channel_id=1, source_target_pairs={{0,2},{1,3},{2,0},{3,1},{4,6},{5,7},{6,4},{7,5},{8,10},{9,11},{10,... | collective-permute-start | bytes 552968 | tf_op jit(solution)/shard_map/ppermute | solution.py:204
  435.2 14.5 %collective-permute-start.75 = (bf16[96,768]{1,0:T(8,128)(2,1)S(1)}, bf16[96,768]{1,0:T(8,128)(2,1)S(1)}, u32[]{:S(2)}, u32[]{:S(2)}) collective-permute-start(bf16[96,768]{1,0:T(8,128)(2,1)S(1)} %get-tuple-element.422), channel_id=1, source_target_pairs={{0,2},{1,3},{2,0},{3,1},{4,6},{5,7},{6,4},{7,5},{8,10},{9,11},{10,... | collective-permute-start | bytes 442376 | tf_op jit(solution)/shard_map/ppermute | solution.py:204
  439.0 11.5 %collective-permute-start.69 = (bf16[2,2,24,1536]{3,2,0,1:T(8,128)(2,1)S(1)}, bf16[2,2,24,1536]{3,2,0,1:T(8,128)(2,1)S(1)}, u32[]{:S(2)}, u32[]{:S(2)}) collective-permute-start(bf16[2,2,24,1536]{3,2,0,1:T(8,128)(2,1)S(1)} %get-tuple-element.390), channel_id=1, source_target_pairs={{0,8},{4,12},{8,0},{12,4},{16,24},{20,28},{24,16},{28,20},{1,9},{5... | collective-permute-start | bytes 884744 | tf_op jit(solution)/shard_map/ppermute | solution.py:204
  440.0 13.2 %collective-permute-start.74 = (bf16[2,2,2,24,896]{4,3,2,1,0:T(8,128)(2,1)S(1)}, bf16[2,2,2,24,896]{4,3,2,1,0:T(8,128)(2,1)S(1)}, u32[]{:S(2)}, u32[]{:S(2)}) collective-permute-start(bf16[2,2,2,24,896]{4,3,2,1,0:T(8,128)(2,1)S(1)} %get-tuple-element.388), channel_id=1, source_target_pairs={{0,8},{4,12},{8,0},{12,4},{16,24},{20,28},{24,16},{28,20},{1,9},{5... | collective-permute-start | bytes 1032200 | tf_op jit(solution)/shard_map/ppermute | solution.py:204
  (84 other events, 1619.4 us)
where the time goes:
time: 485 us; the launch traced here: 476 us
  starting transfers between devices  127 us (26%)
  waiting for transfers between devices  109 us (22%)
  Pallas kernels  75.5 us (16%)
  matrix products  63.7 us (13%)
  other arithmetic  61.8 us (13%)
  local copies, waits for them, and re-layouts  35.9 us (7%)
    ppermute x81, starting transfers between devices, swap_with(): return lax.ppermute(values, axis, [(i, i ^ step) for i in range(size)])  127 us
    ppermute x81, waiting for transfers between devices, swap_with(): return lax.ppermute(values, axis, [(i, i ^ step) for i in range(size)])  109 us
    dot_general x18, matrix products, contract(): lax.dot_general(left, right, (dims, ((), ())), preferred_element_type=f32)  63.7 us
    pallas_call x3, Pallas kernels, attend_back(): pl.pallas_call(functools.partial(backward_kernel, groups), out_shape=[jax...  53.5 us
    pallas_call x3, Pallas kernels, attend(): pl.pallas_call(functools.partial(forward_kernel, groups), out_shape=[jax....  22 us
    convert_element_type x19, other arithmetic, receive(): self.piece = (self.kept.astype(f32) + other.astype(f32)).astype(bf16)  15.6 us
    select_n x18, other arithmetic, send(): self.kept = jnp.where(mine, high, low)  14.9 us
    unnamed x136, local copies, waits for them, and re-layouts  11 us
  transfers between devices with their start and end apart: 81, of which 35 were waited for; matrix products, arithmetic and copies ran while one was open for 20% of the time, Pallas kernels for 12%

commit v1 on v0

--- a/solution.py
+++ b/solution.py
@@ -12,6 +12,7 @@
 HEAD = 64
 PASSES = 5
 PASS_SLOTS = 512
+PART = 256
 
 
 masked_value = -1e30
@@ -34,9 +35,10 @@
     return lax.dot_general(left, right, (dims, ((), ())), preferred_element_type=f32)
 
 
-def tile_visible(length):
-    key_place = lax.broadcasted_iota(jnp.int32, (PASS_SLOTS, PASS_SLOTS), 0)
-    query_place = lax.broadcasted_iota(jnp.int32, (PASS_SLOTS, PASS_SLOTS), 1)
+def tile_visible(length, part):
+    shape = ((part + 1) * PART, PART)
+    key_place = lax.broadcasted_iota(jnp.int32, shape, 0)
+    query_place = lax.broadcasted_iota(jnp.int32, shape, 1) + part * PART
     return (key_place <= query_place) & (key_place < length)
 
 
@@ -68,24 +70,29 @@
     place_pieces(here[0], pieces, shelf, packed)
     key_rows[...] = turned(packed[HEAD : 2 * HEAD, :])
     for query_index in range(PASSES):
-        query_span = slice(query_index * PASS_SLOTS, (query_index + 1) * PASS_SLOTS)
-        queries = packed[:HEAD, query_span] * jnp.asarray(0.125, bf16)
-        top = jnp.full((1, PASS_SLOTS), masked_value, f32)
-        total = jnp.zeros((1, PASS_SLOTS), f32)
-        acc = jnp.zeros((HEAD, PASS_SLOTS), f32)
-        for key_index in range(query_index + 1):
-            key_span = slice(key_index * PASS_SLOTS, (key_index + 1) * PASS_SLOTS)
-            scores = contract(key_rows[key_span, :], queries, ((1,), (0,)))
-            scores = jnp.where(tile_visible(lengths[0, key_index]), scores, masked_value)
-            newest = jnp.maximum(top, jnp.max(scores, axis=0, keepdims=True))
-            shares = jnp.exp(scores - newest)
-            fade = jnp.exp(top - newest)
-            total = total * fade + jnp.sum(shares, axis=0, keepdims=True)
-            values = packed[2 * HEAD :, key_span]
-            acc = acc * fade + contract(values, shares.astype(bf16), ((1,), (0,)))
-            top = newest
-        mixed[:, query_span] = (acc / total).astype(bf16)
-        totals[query_index : query_index + 1, :] = top + jnp.log(total)
+        for part in range(PASS_SLOTS // PART):
+            query_at = query_index * PASS_SLOTS + part * PART
+            query_span = slice(query_at, query_at + PART)
+            queries = packed[:HEAD, query_span] * jnp.asarray(0.125, bf16)
+            top = jnp.full((1, PART), masked_value, f32)
+            total = jnp.zeros((1, PART), f32)
+            acc = jnp.zeros((HEAD, PART), f32)
+            for key_index in range(query_index + 1):
+                key_at = key_index * PASS_SLOTS
+                key_span = slice(key_at, key_at + (part + 1) * PART)
+                scores = contract(key_rows[key_span, :], queries, ((1,), (0,)))
+                shown = tile_visible(lengths[0, key_index], part)
+                scores = jnp.where(shown, scores, masked_value)
+                newest = jnp.maximum(top, jnp.max(scores, axis=0, keepdims=True))
+                shares = jnp.exp(scores - newest)
+                fade = jnp.exp(top - newest)
+                total = total * fade + jnp.sum(shares, axis=0, keepdims=True)
+                values = packed[2 * HEAD :, key_span]
+                acc = acc * fade + contract(values, shares.astype(bf16), ((1,), (0,)))
+                top = newest
+            mixed[:, query_span] = (acc / total).astype(bf16)
+            place = slice(part * PART, (part + 1) * PART)
+            totals[query_index : query_index + 1, place] = top + jnp.log(total)
     hand_out(here[0], mixed, out_shelf, outs)
 
 
@@ -98,6 +105,7 @@
     grad_rows[...] = turned(grad[...])
     grad_query[...] = jnp.zeros_like(grad_query)
     eighth = jnp.asarray(0.125, bf16)
+    parts = PASS_SLOTS // PART
 
     def key_pass(key_index, _):
         key_at = pl.multiple_of(key_index * PASS_SLOTS, PASS_SLOTS)
@@ -105,28 +113,38 @@
         keys = rows[key_span, HEAD : 2 * HEAD] * eighth
         keys_turned = packed[HEAD : 2 * HEAD, key_span] * eighth
         values = rows[key_span, 2 * HEAD :]
-        shown = tile_visible(lengths[0, key_index])
+        length = lengths[0, key_index]
 
         def query_pass(query_index, carried):
-            grad_key, grad_value = carried
-            query_at = pl.multiple_of(query_index * PASS_SLOTS, PASS_SLOTS)
-            query_span = pl.ds(query_at, PASS_SLOTS)
-            grads = grad[:, query_span]
-            product = grads.astype(f32) * mixed[:, query_span].astype(f32)
-            delta = jnp.sum(product, axis=0, keepdims=True)
-            scores = contract(keys, packed[:HEAD, query_span], ((1,), (0,)))
-            shares = jnp.exp(scores - totals[pl.ds(query_index, 1), :])
-            shares = jnp.where(shown, shares, 0.0)
-            grad_shares = contract(values, grads, ((1,), (0,)))
-            grad_scores = (shares * (grad_shares - delta)).astype(bf16)
-            grad_query[:, query_span] += contract(keys_turned, grad_scores, ((1,), (0,)))
-            grad_value += contract(shares.astype(bf16), grad_rows[query_span, :], ((1,), (0,)))
-            queries = rows[query_span, :HEAD] * eighth
-            grad_key += contract(grad_scores, queries, ((1,), (0,)))
-            return grad_key, grad_value
-
-        empty = jnp.zeros((PASS_SLOTS, HEAD), f32)
-        grad_key, grad_value = lax.fori_loop(key_index, PASSES, query_pass, (empty, empty))
+            carried = list(carried)
+            for part in range(parts):
+                seen = (part + 1) * PART
+                start = query_index * PASS_SLOTS + part * PART
+                query_span = pl.ds(pl.multiple_of(start, PART), PART)
+                place = slice(part * PART, seen)
+                grads = grad[:, query_span]
+                product = grads.astype(f32) * mixed[:, query_span].astype(f32)
+                delta = jnp.sum(product, axis=0, keepdims=True)
+                scores = contract(keys[:seen], packed[:HEAD, query_span], ((1,), (0,)))
+                shares = jnp.exp(scores - totals[pl.ds(query_index, 1), place])
+                shares = jnp.where(tile_visible(length, part), shares, 0.0)
+                grad_shares = contract(values[:seen], grads, ((1,), (0,)))
+                grad_scores = (shares * (grad_shares - delta)).astype(bf16)
+                add_query = contract(keys_turned[:, :seen], grad_scores, ((1,), (0,)))
+                grad_query[:, query_span] += add_query
+                add_value = contract(shares.astype(bf16), grad_rows[query_span, :], ((1,), (0,)))
+                queries = rows[query_span, :HEAD] * eighth
+                add_key = contract(grad_scores, queries, ((1,), (0,)))
+                for n in range(part + 1):
+                    block = slice(n * PART, (n + 1) * PART)
+                    carried[n] += add_key[block]
+                    carried[parts + n] += add_value[block]
+            return tuple(carried)
+
+        empty = jnp.zeros((PART, HEAD), f32)
+        found = lax.fori_loop(key_index, PASSES, query_pass, (empty,) * (2 * parts))
+        grad_key = jnp.concatenate(found[:parts], axis=0)
+        grad_value = jnp.concatenate(found[parts:], axis=0)
         result[HEAD : 2 * HEAD, key_span] = grad_key.T.astype(bf16)
         result[2 * HEAD :, key_span] = grad_value.T.astype(bf16)
         return 0
@@ -426,21 +444,20 @@
         arrived = pieces
         if h == 0:
             pieces = after(pieces, outcome)
-        if late:
-            if h > 1:
-                for one in late:
-                    one.receive(parts[-1])
-            pieces = after(pieces, [one.send() for one in late])
-        back = attend_back(lengths, here[None], *kept[h], pieces)
         if not late:
             hidden_late, grad_branch_late, grad_upsum_late, grad_attn_late = after(
-                (hidden, grad_branch, grad_upsum, grad_attn), back
+                (hidden, grad_branch, grad_upsum, grad_attn), sending
             )
             grad_down = contract(hidden_late, grad_branch_late, ((0,), (0,))).astype(bf16)
             grad_up = contract(normed_b, grad_upsum_late, ((0,), (0,))).astype(bf16)
             grad_out = contract(heads_out, grad_attn_late, ((1,), (0,))).astype(bf16)
             grad_up = jnp.concatenate([grad_up, grad_out], axis=1)
             late = [Scatter(grad_down, True), Scatter(grad_up, False)]
+        else:
+            for one in late:
+                one.receive(parts[-1])
+        pieces = after(pieces, [one.send() for one in late])
+        back = attend_back(lengths, here[None], *kept[h], pieces)
         parts.append(back)
     grad_projected = []
     for back in parts:

time: 485 us -> 490 us (1.010)
  Pallas kernels: 75.5 us -> 83.4 us
    pallas_call x3, Pallas kernels: 22 us -> 31.5 us  [attend(): pl.pallas_call(functools.partial(forward_kernel, groups), out_shape=[jax....]
    unnamed x136 -> x170, local copies, waits for them, and re-layouts: 11 us -> 10.8 us
  transfers between devices with their start and end apart: 81 -> 81, of which waited for: 35 -> 31; matrix products, arithmetic and copies ran while one was open for 20% -> 21% of each run, Pallas kernels for 12% -> 17%
where the time goes in v1:
time: 490 us; the launch traced here: 481 us
  starting transfers between devices  126 us (26%)
  waiting for transfers between devices  110 us (22%)
  Pallas kernels  83.4 us (17%)
  matrix products  62.1 us (13%)
  other arithmetic  61.6 us (13%)
  local copies, waits for them, and re-layouts  35 us (7%)
    ppermute x81, starting transfers between devices, swap_with(): return lax.ppermute(values, axis, [(i, i ^ step) for i in range(size)])  126 us
    ppermute x81, waiting for transfers between devices, swap_with(): return lax.ppermute(values, axis, [(i, i ^ step) for i in range(size)])  110 us
    dot_general x18, matrix products, contract(): lax.dot_general(left, right, (dims, ((), ())), preferred_element_type=f32)  62.1 us
    pallas_call x3, Pallas kernels, attend_back(): pl.pallas_call(functools.partial(backward_kernel, groups), out_shape=[jax...  51.9 us
    pallas_call x3, Pallas kernels, attend(): pl.pallas_call(functools.partial(forward_kernel, groups), out_shape=[jax....  31.5 us
    convert_element_type x19, other arithmetic, receive(): self.piece = (self.kept.astype(f32) + other.astype(f32)).astype(bf16)  12.6 us
    select_n x18, other arithmetic, send(): self.kept = jnp.where(mine, high, low)  12.6 us
    unnamed x170, local copies, waits for them, and re-layouts  10.8 us
  transfers between devices with their start and end apart: 81, of which 31 were waited for; matrix products, arithmetic and copies ran while one was open for 21% of the time, Pallas kernels for 17%

profile of v1, /device:TPU:0, one launch (start us, length us, event | category | flops | bytes accessed | tf_op | source)
XLA Modules:
  0.0 481.2 jit_solution(13527354667637104357)
XLA Ops:
  2.1 4.1 collective-permute-start.11
  17.2 2.7 collective-permute-done.1
  20.0 2.5 collective-permute-start.25
  29.9 2.9 collective-permute-start.19
  34.5 5.6 %collective-permute-done.19 = bf16[24,3072]{1,0:T(8,128)(2,1)S(1)} collective-permute-done((bf16[24,3072]{1,0:T(8,128)(2,1)S(1)}, bf16[24,3072]{1,0:T(8,128)(2,1)S(1)}, u32[]{:S(2)}, u32[]{:S(2)}) %collective-permute-start.19) | collective-permute-done | bytes 147488 | tf_op jit(solution)/shard_map/ppermute | solution.py:222
  43.1 6.5 %collective-permute-done.20 = bf16[2,24,3072]{2,1,0:T(8,128)(2,1)S(1)} collective-permute-done((bf16[2,24,3072]{2,1,0:T(8,128)(2,1)S(1)}, bf16[2,24,3072]{2,1,0:T(8,128)(2,1)S(1)}, u32[]{:S(2)}, u32[]{:S(2)}) %collective-permute-start.20) | collective-permute-done | bytes 294944 | tf_op jit(solution)/shard_map/ppermute | solution.py:222
  49.7 3.1 collective-permute-done.23
  57.8 2.7 slice_reduce_fusion
  62.4 2.5 add_convert_fusion.9
  65.0 2.3 fusion.28
  67.3 2.9 select_reduce_fusion
  76.8 3.7 collective-permute-start.7
  83.6 2.3 collective-permute-done.5.refs_1_
  87.5 9.5 %collective-permute-done.6.refs_2_ = bf16[192,640]{1,0:T(8,128)(2,1)S(1)} collective-permute-done((bf16[192,640]{1,0:T(8,128)(2,1)}, bf16[192,640]{1,0:T(8,128)(2,1)S(1)}, u32[]{:S(2)}, u32[]{:S(2)}) %collective-permute-start.6) | collective-permute-done | bytes 245792 | tf_op jit(solution)/shard_map/ppermute | solution.py:222
  97.0 4.7 collective-permute-start.16
  101.7 10.4 %attend.3 = (bf16[192,2560]{1,0:T(8,128)(2,1)S(1)}, bf16[64,2560]{1,0:T(8,128)(2,1)S(1)}, f32[5,512]{1,0:T(8,128)S(1)}, bf16[64,640]{1,0:T(8,128)(2,1)S(1)}, bf1...) custom-call(s32[1,5]{1,0:T(1,128)S(1)} %copy-done, s32[1]{0:T(128)} %bitcast.16.here, ...), custom_call_target="tpu_custom_call" | custom-call | flops 10000000000 | bytes 1000000 | tf_op jit(solution)/shard_map/attend/pallas_call | solution.py:165
  112.9 2.4 collective-permute-start.18
  117.7 5.4 %collective-permute-done.18.refs_3_ = bf16[192,640]{1,0:T(8,128)(2,1)S(1)} collective-permute-done((bf16[192,640]{1,0:T(8,128)(2,1)S(1)}, bf16[192,640]{1,0:T(8,128)(2,1)S(1)}, u32[]{:S(2)}, u32[]{:S(2)}) %collective-permute-start.18) | collective-permute-done | bytes 245792 | tf_op jit(solution)/shard_map/ppermute | solution.py:222
  123.1 5.8 %collective-permute-start.31 = (bf16[192,640]{1,0:T(8,128)(2,1)S(1)}, bf16[192,640]{1,0:T(8,128)(2,1)S(1)}, u32[]{:S(2)}, u32[]{:S(2)}) collective-permute-start(bf16[192,640]{1,0:T(8,128)(2,1)S(1)} %copy-done.38), channel_id=1, source_target_pairs={{0,1},{1,0},{2,3},{3,2},{4,5},{5,4},{6,7},{7,6},{8,9},{9,8},{10,11... | collective-permute-start | bytes 737288 | tf_op jit(solution)/shard_map/ppermute | solution.py:222
  134.0 10.4 %attend.4 = (bf16[192,2560]{1,0:T(8,128)(2,1)S(1)}, bf16[64,2560]{1,0:T(8,128)(2,1)S(1)}, f32[5,512]{1,0:T(8,128)S(1)}, bf16[64,640]{1,0:T(8,128)(2,1)S(1)}, bf1...) custom-call(s32[1,5]{1,0:T(1,128)S(1)} %copy-done, s32[1]{0:T(128)} %bitcast.16.here, ...), custom_call_target="tpu_custom_call" | custom-call | flops 10000000000 | bytes 1000000 | tf_op jit(solution)/shard_map/attend/pallas_call | solution.py:165
  144.4 2.5 collective-permute-start.10
  146.9 2.9 collective-permute-done.32.refs_2_
  149.8 7.0 %collective-permute-start.29 = (bf16[64,640]{1,0:T(8,128)(2,1)S(1)}, bf16[64,640]{1,0:T(8,128)(2,1)S(1)}, u32[]{:S(2)}, u32[]{:S(2)}) collective-permute-start(bf16[64,640]{1,0:T(8,128)(2,1)S(1)} %get-tuple-element.166), channel_id=1, source_target_pairs={{0,2},{1,3},{2,0},{3,1},{4,6},{5,7},{6,4},{7,5},{8,10},{9,11},{10,... | collective-permute-start | bytes 245768 | tf_op jit(solution)/shard_map/ppermute | solution.py:222
  156.8 10.8 %attend.5 = (bf16[192,2560]{1,0:T(8,128)(2,1)S(1)}, bf16[64,2560]{1,0:T(8,128)(2,1)S(1)}, f32[5,512]{1,0:T(8,128)S(1)}, bf16[64,640]{1,0:T(8,128)(2,1)S(1)}, bf1...) custom-call(s32[1,5]{1,0:T(1,128)S(1)} %copy-done, s32[1]{0:T(128)} %bitcast.16.here, ...), custom_call_target="tpu_custom_call" | custom-call | flops 10000000000 | bytes 1000000 | tf_op jit(solution)/shard_map/attend/pallas_call | solution.py:165
  170.6 3.4 collective-permute-done.30
  176.5 2.6 collective-permute-start.36
  179.9 16.8 %collective-permute-done.39 = bf16[2,2,2,24,3072]{4,3,2,1,0:T(8,128)(2,1)S(1)} collective-permute-done((bf16[2,2,2,24,3072]{4,3,2,1,0:T(8,128)(2,1)S(1)}, bf16[2,2,2,24,3072]{4,3,2,1,0:T(8,128)(2,1)S(1)}, u32[]{:S(2)}, u32[]{:S(2)}) %collective-permute-start.39) | collective-permute-done | bytes 1179680 | tf_op jit(solution)/shard_map/ppermute | solution.py:222
  202.4 2.6 collective-permute-done.42
  206.1 8.1 %multiply_convert_fusion = (bf16[640,3072]{1,0:T(8,128)(2,1)}, f32[640,3072]{1,0:T(8,128)}) fusion(f32[3072]{0:T(1024)S(1)} %copy-done.70, bf16[768,3072]{1,0:T(8,128)(2,1)S(1)} %bitcast.433, f32[640,768]{1,0:T(8,128)S(1)} %get-tuple-element.458, f32[768]{0:T(1024)S(1)} %copy-done.77, f32[768]{0:T(1024)S(1)} %copy-done.69, f32[640]{0:T(1024)S(1)} %add_rsqrt_fusion, ...), kind=kOutput, calls=%fused_computation.9 | convolution fusion | flops 3042017280 | bytes 18504704 | tf_op jit(solution)/shard_map/dot_general | solution.py:35
  214.2 11.5 %fusion.75 = (bf16[3072]{0:T(1024)(128)(2,1)S(1)}, bf16[640,3072]{1,0:T(8,128)(2,1)}) fusion(f32[640,3072]{1,0:T(8,128)} %get-tuple-element.460, f32[3072]{0:T(1024)S(1)} %copy-done.70, bf16[3072,768]{1,0:T(8,128)(2,1)S(1)} %bitcast.429, bf16[1,640,768]{2,1,0:T(8,128)(2,1)S(1)} %copy-done.31, f32[640]{0:T(1024)S(1)} %copy-done.68), kind=kOutput, calls=%fused_computation.362 | convolution fusion | flops 3064624128 | bytes 17519104 | tf_op jit(solution)/shard_map/dot_general | solution.py:35
  225.7 5.8 %multiply_reduce_fusion = (bf16[768]{0:T(1024)(128)(2,1)S(1)}, f32[640]{0:T(1024)S(1)}, f32[640]{0:T(1024)S(1)}, bf16[768]{0:T(1024)(128)(2,1)S(1)}, f32[640,768]{1,0:T(8,128)S(1)}) fusion(f32[640,768]{1,0:T(8,128)S(1)} %get-tuple-element.458, f32[640]{0:T(1024)S(1)} %add_rsqrt_fusion, f32[640]{0:T(1024)S(1)} %broadcast_multiply_fusion.4, ...), kind=kOutput, calls=%fused_computation.48 | convolution fusion | flops 3024319744 | bytes 12599296 | tf_op jit(solution)/shard_map/dot_general | solution.py:35
  231.5 2.3 fusion.64
  235.8 3.8 collective-permute-start.44
  241.5 4.2 convolution_convert_fusion.1
  245.7 2.6 fusion.69
  250.6 6.5 %convolution_convert_fusion = bf16[768,3072]{1,0:T(8,128)(2,1)} fusion(bf16[640,3072]{1,0:T(8,128)(2,1)S(1)} %copy-done.81, f32[640,768]{1,0:T(8,128)S(1)} %get-tuple-element.458, f32[768]{0:T(1024)S(1)} %copy-done.77, f32[768]{0:T(1024)S(1)} %copy-done.69, f32[640]{0:T(1024)S(1)} %add_rsqrt_fusion, f32[640]{0:T(1024)S(1)} %broadcast_multiply_fusion.4), kind=kOutput, calls=%fused_computation.14 | convolution fusion | flops 3024715776 | bytes 10628096 | tf_op jit(solution)/shard_map/dot_general | solution.py:35
  257.1 3.1 pad_maximum_fusion
  262.6 2.4 select_bitcast_fusion.2
  265.0 3.4 select_bitcast_fusion
  270.6 4.2 multiply_add_fusion.1
  278.4 3.8 collective-permute-start.50
  282.7 17.3 %attend_back.3 = (bf16[192,640]{1,0:T(8,128)(2,1)S(1)}, bf16[192,640]{1,0:T(8,128)(2,1)S(1)}, bf16[192,640]{1,0:T(8,128)(2,1)S(1)}, bf16[192,640]{1,0:T(8,128)(2,1)S(1)}) custom-call(s32[1,5]{1,0:T(1,128)S(1)} %copy-done, s32[1]{0:T(128)} %bitcast.16.here, bf16[192,2560]{1,0:T(8,128)(2,1)S(1)} %get-tuple-element.184.packed, bf16[64,2560]{1,0:T(8,128)(2,1)S(1)} %copy-done.4, ...), custom_call_target="tpu_custom_call" | custom-call | flops 15000000512 | bytes 1000000 | tf_op jit(solution)/shard_map/attend_back/pallas_call | solution.py:190
  300.1 3.8 collective-permute-start.47
  304.0 2.4 add_convert_fusion.1
  308.3 2.6 add_convert_fusion
  312.1 17.4 %attend_back.4 = (bf16[192,640]{1,0:T(8,128)(2,1)S(1)}, bf16[192,640]{1,0:T(8,128)(2,1)S(1)}, bf16[192,640]{1,0:T(8,128)(2,1)S(1)}, bf16[192,640]{1,0:T(8,128)(2,1)S(1)}) custom-call(s32[1,5]{1,0:T(1,128)S(1)} %copy-done, s32[1]{0:T(128)} %bitcast.16.here, bf16[192,2560]{1,0:T(8,128)(2,1)S(1)} %copy-done.2, bf16[64,2560]{1,0:T(8,128)(2,1)S(1)} %get-tuple-element.208.mixed, ...), custom_call_target="tpu_custom_call" | custom-call | flops 15000000512 | bytes 1000000 | tf_op jit(solution)/shard_map/attend_back/pallas_call | solution.py:190
  329.5 4.1 collective-permute-done.60
  334.8 9.7 %collective-permute-done.61 = bf16[2,2,2,24,3840]{4,3,1,2,0:T(8,128)(2,1)S(1)} collective-permute-done((bf16[2,2,2,24,3840]{4,3,1,2,0:T(8,128)(2,1)S(1)}, bf16[2,2,2,24,3840]{4,3,1,2,0:T(8,128)(2,1)S(1)}, u32[]{:S(2)}, u32[]{:S(2)}) %collective-permute-start.61) | collective-permute-done | bytes 1474592 | tf_op jit(solution)/shard_map/ppermute | solution.py:222
  347.5 2.4 collective-permute-start.48
  351.8 3.2 collective-permute-start.55
  355.0 3.9 collective-permute-start.56
  358.9 17.2 %attend_back.5 = (bf16[192,640]{1,0:T(8,128)(2,1)S(1)}, bf16[192,640]{1,0:T(8,128)(2,1)S(1)}, bf16[192,640]{1,0:T(8,128)(2,1)S(1)}, bf16[192,640]{1,0:T(8,128)(2,1)S(1)}) custom-call(s32[1,5]{1,0:T(1,128)S(1)} %copy-done, s32[1]{0:T(128)} %bitcast.16.here, bf16[192,2560]{1,0:T(8,128)(2,1)S(1)} %get-tuple-element.224.packed, ...), custom_call_target="tpu_custom_call" | custom-call | flops 15000000512 | bytes 1000000 | tf_op jit(solution)/shard_map/attend_back/pallas_call | solution.py:190
  378.9 3.8 collective-permute-start.64
  386.4 2.3 fusion.60
  392.0 11.8 %collective-permute-start.68 = (bf16[2,96,768]{2,1,0:T(8,128)(2,1)}, bf16[2,96,768]{2,1,0:T(8,128)(2,1)}, u32[]{:S(2)}, u32[]{:S(2)}) collective-permute-start(bf16[2,96,768]{2,1,0:T(8,128)(2,1)} %get-tuple-element.400), channel_id=1, source_target_pairs={{0,1},{1,0},{2,3},{3,2},{4,5},{5,4},{6,7},{7,6},{8,9},{9,8},{10,11... | collective-permute-start | bytes 884744 | tf_op jit(solution)/shard_map/ppermute | solution.py:222
  407.9 2.2 fusion.20
  419.9 3.5 convolution_convert_fusion.2
  423.4 3.5 collective-permute-start.73
  434.8 2.8 select_reduce_fusion.1
  443.9 2.6 collective-permute-done.70
  449.1 7.5 %collective-permute-done.71 = bf16[2,2,24,1536]{3,2,0,1:T(8,128)(2,1)S(1)} collective-permute-done((bf16[2,2,24,1536]{3,2,0,1:T(8,128)(2,1)S(1)}, bf16[2,2,24,1536]{3,2,0,1:T(8,128)(2,1)S(1)}, u32[]{:S(2)}, u32[]{:S(2)}) %collective-permute-start.71) | collective-permute-done | bytes 294944 | tf_op jit(solution)/shard_map/ppermute | solution.py:222
  458.0 3.8 collective-permute-done.76
  463.4 3.9 collective-permute-done.78
  475.1 2.9 collective-permute-done.80
  (506 shorter events, 140.8 us)
Async XLA Ops:
  2.1 7.1 %collective-permute-start.11 = (bf16[24,1152]{1,0:T(8,128)(2,1)S(1)}, bf16[24,1152]{1,0:T(8,128)(2,1)S(1)}, u32[]{:S(2)}, u32[]{:S(2)}) collective-permute-start(bf16[24,1152]{1,0:T(8,128)(2,1)S(1)} %slice.366), channel_id=1, source_target_pairs={{0,2},{1,3},{2,0},{3,1},{4,6},{5,7},{6,4},{7,5},{8,10},{9,11},{10,... | collective-permute-start | bytes 165896 | tf_op jit(solution)/shard_map/ppermute | solution.py:222
  25.0 7.9 %collective-permute-start.26 = (bf16[2,24,768]{2,1,0:T(8,128)(2,1)S(1)}, bf16[2,24,768]{2,1,0:T(8,128)(2,1)S(1)}, u32[]{:S(2)}, u32[]{:S(2)}) collective-permute-start(bf16[2,24,768]{2,1,0:T(8,128)(2,1)S(1)} %pad_maximum_fusion.28), channel_id=1, source_target_pairs={{0,1},{1,0},{2,3},{3,2},{4,5},{5,4},{6,7},{7,6},{8,9},{9,8},{10,11... | collective-permute-start | bytes 221192 | tf_op jit(solution)/shard_map/ppermute | solution.py:222
  28.4 14.0 %collective-permute-start.2 = (bf16[2,2,24,1280]{3,2,0,1:T(8,128)(2,1)S(1)}, bf16[2,2,24,1280]{3,2,0,1:T(8,128)(2,1)S(1)}, u32[]{:S(2)}, u32[]{:S(2)}) collective-permute-start(bf16[2,2,24,1280]{3,2,0,1:T(8,128)(2,1)S(1)} %pad_maximum_fusion.23), channel_id=1, source_target_pairs={{0,16},{4,20},{8,24},{12,28},{16,0},{20,4},{24,8},{28,12},{1,17},{... | collective-permute-start | bytes 737288 | tf_op jit(solution)/shard_map/ppermute | solution.py:222
  29.9 10.2 %collective-permute-start.19 = (bf16[24,3072]{1,0:T(8,128)(2,1)S(1)}, bf16[24,3072]{1,0:T(8,128)(2,1)S(1)}, u32[]{:S(2)}, u32[]{:S(2)}) collective-permute-start(bf16[24,3072]{1,0:T(8,128)(2,1)S(1)} %copy-done.39), channel_id=1, source_target_pairs={{0,2},{1,3},{2,0},{3,1},{4,6},{5,7},{6,4},{7,5},{8,10},{9,11},{10,... | collective-permute-start | bytes 442376 | tf_op jit(solution)/shard_map/ppermute | solution.py:222
  32.9 8.8 %collective-permute-start.22 = (bf16[96,768]{1,0:T(8,128)(2,1)S(1)}, bf16[96,768]{1,0:T(8,128)(2,1)S(1)}, u32[]{:S(2)}, u32[]{:S(2)}) collective-permute-start(bf16[96,768]{1,0:T(8,128)(2,1)S(1)} %copy-done.40), channel_id=1, source_target_pairs={{0,2},{1,3},{2,0},{3,1},{4,6},{5,7},{6,4},{7,5},{8,10},{9,11},{10,... | collective-permute-start | bytes 442376 | tf_op jit(solution)/shard_map/ppermute | solution.py:222
  33.1 19.8 %collective-permute-start.14 = (bf16[2,2,2,24,1152]{4,3,1,2,0:T(8,128)(2,1)S(1)}, bf16[2,2,2,24,1152]{4,3,1,2,0:T(8,128)(2,1)S(1)}, u32[]{:S(2)}, u32[]{:S(2)}) collective-permute-start(bf16[2,2,2,24,1152]{4,3,1,2,0:T(8,128)(2,1)S(1)} %pad_maximum_fusion.19), channel_id=1, source_target_pairs={{0,16},{4,20},{8,24},{12,28},{16,0},{20,4},{24,8},{28,12},{1,17},{... | collective-permute-start | bytes 1327112 | tf_op jit(solution)/shard_map/ppermute | solution.py:222
  40.2 9.4 %collective-permute-start.20 = (bf16[2,24,3072]{2,1,0:T(8,128)(2,1)S(1)}, bf16[2,24,3072]{2,1,0:T(8,128)(2,1)S(1)}, u32[]{:S(2)}, u32[]{:S(2)}) collective-permute-start(bf16[2,24,3072]{2,1,0:T(8,128)(2,1)S(1)} %pad_maximum_fusion.20), channel_id=1, source_target_pairs={{0,1},{1,0},{2,3},{3,2},{4,5},{5,4},{6,7},{7,6},{8,9},{9,8},{10,11... | collective-permute-start | bytes 884744 | tf_op jit(solution)/shard_map/ppermute | solution.py:222
  41.8 11.0 %collective-permute-start.23 = (bf16[2,96,768]{2,1,0:T(8,128)(2,1)S(1)}, bf16[2,96,768]{2,1,0:T(8,128)(2,1)S(1)}, u32[]{:S(2)}, u32[]{:S(2)}) collective-permute-start(bf16[2,96,768]{2,1,0:T(8,128)(2,1)S(1)} %pad_maximum_fusion.21), channel_id=1, source_target_pairs={{0,1},{1,0},{2,3},{3,2},{4,5},{5,4},{6,7},{7,6},{8,9},{9,8},{10,11... | collective-permute-start | bytes 884744 | tf_op jit(solution)/shard_map/ppermute | solution.py:222
  42.5 10.7 %collective-permute-start.3 = (bf16[2,2,2,24,1280]{4,3,1,2,0:T(8,128)(2,1)S(1)}, bf16[2,2,2,24,1280]{4,3,1,2,0:T(8,128)(2,1)S(1)}, u32[]{:S(2)}, u32[]{:S(2)}) collective-permute-start(bf16[2,2,2,24,1280]{4,3,1,2,0:T(8,128)(2,1)S(1)} %pad_maximum_fusion.18), channel_id=1, source_target_pairs={{0,8},{4,12},{8,0},{12,4},{16,24},{20,28},{24,16},{28,20},{1,9},{5... | collective-permute-start | bytes 1474568 | tf_op jit(solution)/shard_map/ppermute | solution.py:222
  72.6 10.3 %collective-permute-start.27 = (bf16[2,2,24,768]{3,2,1,0:T(8,128)(2,1)S(1)}, bf16[2,2,24,768]{3,2,1,0:T(8,128)(2,1)S(1)}, u32[]{:S(2)}, u32[]{:S(2)}) collective-permute-start(bf16[2,2,24,768]{3,2,1,0:T(8,128)(2,1)S(1)} %pad_maximum_fusion.25), channel_id=1, source_target_pairs={{0,16},{4,20},{8,24},{12,28},{16,0},{20,4},{24,8},{28,12},{1,17},{... | collective-permute-start | bytes 442376 | tf_op jit(solution)/shard_map/ppermute | solution.py:222
  76.1 9.8 %collective-permute-start.5 = (bf16[192,640]{1,0:T(8,128)(2,1)}, bf16[192,640]{1,0:T(8,128)(2,1)S(1)}, u32[]{:S(2)}, u32[]{:S(2)}) collective-permute-start(bf16[192,640]{1,0:T(8,128)(2,1)} %get-tuple-element.140), channel_id=1, source_target_pairs={{0,1},{1,0},{2,3},{3,2},{4,5},{5,4},{6,7},{7,6},{8,9},{9,8},{10,11... | collective-permute-start | bytes 737288 | tf_op jit(solution)/shard_map/ppermute | solution.py:222
  76.8 20.2 %collective-permute-start.6 = (bf16[192,640]{1,0:T(8,128)(2,1)}, bf16[192,640]{1,0:T(8,128)(2,1)S(1)}, u32[]{:S(2)}, u32[]{:S(2)}) collective-permute-start(bf16[192,640]{1,0:T(8,128)(2,1)} %get-tuple-element.141), channel_id=1, source_target_pairs={{0,2},{1,3},{2,0},{3,1},{4,6},{5,7},{6,4},{7,5},{8,10},{9,11},{10,... | collective-permute-start | bytes 737288 | tf_op jit(solution)/shard_map/ppermute | solution.py:222
  76.8 20.2 %collective-permute-start.7 = (bf16[192,640]{1,0:T(8,128)(2,1)}, bf16[192,640]{1,0:T(8,128)(2,1)S(1)}, u32[]{:S(2)}, u32[]{:S(2)}) collective-permute-start(bf16[192,640]{1,0:T(8,128)(2,1)} %get-tuple-element.142), channel_id=1, source_target_pairs={{0,3},{1,2},{2,1},{3,0},{4,7},{5,6},{6,5},{7,4},{8,11},{9,10},{10,... | collective-permute-start | bytes 737288 | tf_op jit(solution)/shard_map/ppermute | solution.py:222
  80.5 48.4 %collective-permute-start.21 = (bf16[2,2,24,3072]{3,2,1,0:T(8,128)(2,1)S(1)}, bf16[2,2,24,3072]{3,2,1,0:T(8,128)(2,1)}, u32[]{:S(2)}, u32[]{:S(2)}) collective-permute-start(bf16[2,2,24,3072]{3,2,1,0:T(8,128)(2,1)S(1)} %pad_maximum_fusion.15), channel_id=1, source_target_pairs={{0,16},{4,20},{8,24},{12,28},{16,0},{20,4},{24,8},{28,12},{1,17},{... | collective-permute-start | bytes 1769480 | tf_op jit(solution)/shard_map/ppermute | solution.py:222
  82.9 48.4 %collective-permute-start.24 = (bf16[2,2,96,768]{3,2,1,0:T(8,128)(2,1)}, bf16[2,2,96,768]{3,2,1,0:T(8,128)(2,1)S(1)}, u32[]{:S(2)}, u32[]{:S(2)}) collective-permute-start(bf16[2,2,96,768]{3,2,1,0:T(8,128)(2,1)} %pad_maximum_fusion.16), channel_id=1, source_target_pairs={{0,8},{4,12},{8,0},{12,4},{16,24},{20,28},{24,16},{28,20},{1,9},{5... | collective-permute-start | bytes 1769480 | tf_op jit(solution)/shard_map/ppermute | solution.py:222
  85.9 26.9 %collective-permute-start.37 = (bf16[2,2,2,24,768]{4,3,2,1,0:T(8,128)(2,1)S(1)}, bf16[2,2,2,24,768]{4,3,2,1,0:T(8,128)(2,1)S(1)}, u32[]{:S(2)}, u32[]{:S(2)}) collective-permute-start(bf16[2,2,2,24,768]{4,3,2,1,0:T(8,128)(2,1)S(1)} %pad_maximum_fusion.22), channel_id=1, source_target_pairs={{0,8},{4,12},{8,0},{12,4},{16,24},{20,28},{24,16},{28,20},{1,9},{5... | collective-permute-start | bytes 884744 | tf_op jit(solution)/shard_map/ppermute | solution.py:222
  97.0 18.6 %collective-permute-start.16 = (bf16[192,640]{1,0:T(8,128)(2,1)S(1)}, bf16[192,640]{1,0:T(8,128)(2,1)S(1)}, u32[]{:S(2)}, u32[]{:S(2)}) collective-permute-start(bf16[192,640]{1,0:T(8,128)(2,1)S(1)} %get-tuple-element.148), channel_id=1, source_target_pairs={{0,1},{1,0},{2,3},{3,2},{4,5},{5,4},{6,7},{7,6},{8,9},{9,8},{10,11... | collective-permute-start | bytes 737288 | tf_op jit(solution)/shard_map/ppermute | solution.py:222
  101.7 15.1 %collective-permute-start.17 = (bf16[192,640]{1,0:T(8,128)(2,1)S(1)}, bf16[192,640]{1,0:T(8,128)(2,1)S(1)}, u32[]{:S(2)}, u32[]{:S(2)}) collective-permute-start(bf16[192,640]{1,0:T(8,128)(2,1)S(1)} %get-tuple-element.149), channel_id=1, source_target_pairs={{0,2},{1,3},{2,0},{3,1},{4,6},{5,7},{6,4},{7,5},{8,10},{9,11},{10,... | collective-permute-start | bytes 737288 | tf_op jit(solution)/shard_map/ppermute | solution.py:222
  112.9 10.2 %collective-permute-start.18 = (bf16[192,640]{1,0:T(8,128)(2,1)S(1)}, bf16[192,640]{1,0:T(8,128)(2,1)S(1)}, u32[]{:S(2)}, u32[]{:S(2)}) collective-permute-start(bf16[192,640]{1,0:T(8,128)(2,1)S(1)} %get-tuple-element.150), channel_id=1, source_target_pairs={{0,3},{1,2},{2,1},{3,0},{4,7},{5,6},{6,5},{7,4},{8,11},{9,10},{10,... | collective-permute-start | bytes 737288 | tf_op jit(solution)/shard_map/ppermute | solution.py:222
  115.6 52.0 %collective-permute-start.8 = (bf16[64,640]{1,0:T(8,128)(2,1)S(1)}, bf16[64,640]{1,0:T(8,128)(2,1)S(1)}, u32[]{:S(2)}, u32[]{:S(2)}) collective-permute-start(bf16[64,640]{1,0:T(8,128)(2,1)S(1)} %get-tuple-element.144), channel_id=1, source_target_pairs={{0,1},{1,0},{2,3},{3,2},{4,5},{5,4},{6,7},{7,6},{8,9},{9,8},{10,11... | collective-permute-start | bytes 245768 | tf_op jit(solution)/shard_map/ppermute | solution.py:222
  116.8 51.4 %collective-permute-start.9 = (bf16[64,640]{1,0:T(8,128)(2,1)S(1)}, bf16[64,640]{1,0:T(8,128)(2,1)S(1)}, u32[]{:S(2)}, u32[]{:S(2)}) collective-permute-start(bf16[64,640]{1,0:T(8,128)(2,1)S(1)} %get-tuple-element.145), channel_id=1, source_target_pairs={{0,2},{1,3},{2,0},{3,1},{4,6},{5,7},{6,4},{7,5},{8,10},{9,11},{10,... | collective-permute-start | bytes 245768 | tf_op jit(solution)/shard_map/ppermute | solution.py:222
  123.1 21.3 %collective-permute-start.31 = (bf16[192,640]{1,0:T(8,128)(2,1)S(1)}, bf16[192,640]{1,0:T(8,128)(2,1)S(1)}, u32[]{:S(2)}, u32[]{:S(2)}) collective-permute-start(bf16[192,640]{1,0:T(8,128)(2,1)S(1)} %copy-done.38), channel_id=1, source_target_pairs={{0,1},{1,0},{2,3},{3,2},{4,5},{5,4},{6,7},{7,6},{8,9},{9,8},{10,11... | collective-permute-start | bytes 737288 | tf_op jit(solution)/shard_map/ppermute | solution.py:222
  128.9 21.0 %collective-permute-start.32 = (bf16[192,640]{1,0:T(8,128)(2,1)S(1)}, bf16[192,640]{1,0:T(8,128)(2,1)S(1)}, u32[]{:S(2)}, u32[]{:S(2)}) collective-permute-start(bf16[192,640]{1,0:T(8,128)(2,1)S(1)} %copy-done.37), channel_id=1, source_target_pairs={{0,2},{1,3},{2,0},{3,1},{4,6},{5,7},{6,4},{7,5},{8,10},{9,11},{10,... | collective-permute-start | bytes 737288 | tf_op jit(solution)/shard_map/ppermute | solution.py:222
  131.3 18.5 %collective-permute-start.33 = (bf16[192,640]{1,0:T(8,128)(2,1)S(1)}, bf16[192,640]{1,0:T(8,128)(2,1)S(1)}, u32[]{:S(2)}, u32[]{:S(2)}) collective-permute-start(bf16[192,640]{1,0:T(8,128)(2,1)S(1)} %copy-done.36), channel_id=1, source_target_pairs={{0,3},{1,2},{2,1},{3,0},{4,7},{5,6},{6,5},{7,4},{8,11},{9,10},{10,... | collective-permute-start | bytes 737288 | tf_op jit(solution)/shard_map/ppermute | solution.py:222
  144.4 23.9 %collective-permute-start.10 = (bf16[64,640]{1,0:T(8,128)(2,1)S(1)}, bf16[64,640]{1,0:T(8,128)(2,1)S(1)}, u32[]{:S(2)}, u32[]{:S(2)}) collective-permute-start(bf16[64,640]{1,0:T(8,128)(2,1)S(1)} %get-tuple-element.146), channel_id=1, source_target_pairs={{0,3},{1,2},{2,1},{3,0},{4,7},{5,6},{6,5},{7,4},{8,11},{9,10},{10,... | collective-permute-start | bytes 245768 | tf_op jit(solution)/shard_map/ppermute | solution.py:222
  149.8 19.2 %collective-permute-start.28 = (bf16[64,640]{1,0:T(8,128)(2,1)S(1)}, bf16[64,640]{1,0:T(8,128)(2,1)S(1)}, u32[]{:S(2)}, u32[]{:S(2)}) collective-permute-start(bf16[64,640]{1,0:T(8,128)(2,1)S(1)} %get-tuple-element.165), channel_id=1, source_target_pairs={{0,1},{1,0},{2,3},{3,2},{4,5},{5,4},{6,7},{7,6},{8,9},{9,8},{10,11... | collective-permute-start | bytes 245768 | tf_op jit(solution)/shard_map/ppermute | solution.py:222
  149.8 20.7 %collective-permute-start.29 = (bf16[64,640]{1,0:T(8,128)(2,1)S(1)}, bf16[64,640]{1,0:T(8,128)(2,1)S(1)}, u32[]{:S(2)}, u32[]{:S(2)}) collective-permute-start(bf16[64,640]{1,0:T(8,128)(2,1)S(1)} %get-tuple-element.166), channel_id=1, source_target_pairs={{0,2},{1,3},{2,0},{3,1},{4,6},{5,7},{6,4},{7,5},{8,10},{9,11},{10,... | collective-permute-start | bytes 245768 | tf_op jit(solution)/shard_map/ppermute | solution.py:222
  168.2 29.1 %collective-permute-start.38 = (bf16[2,2,2,2,24,768]{5,4,3,2,1,0:T(8,128)(2,1)S(1)}, bf16[2,2,2,2,24,768]{5,4,3,2,1,0:T(8,128)(2,1)S(1)}, u32[]{:S(2)}, u32[]{:S(2)}) collective-permute-start(bf16[2,2,2,2,24,768]{5,4,3,2,1,0:T(8,128)(2,1)S(1)} %pad_maximum_fusion.17), channel_id=1, source_target_pairs={{0,4},{4,0},{8,12},{12,8},{16,20},{20,16},{24,28},{28,24},{1,5},{5... | collective-permute-start | bytes 1769480 | tf_op jit(solution)/shard_map/ppermute | solution.py:222
  168.3 28.4 %collective-permute-start.39 = (bf16[2,2,2,24,3072]{4,3,2,1,0:T(8,128)(2,1)S(1)}, bf16[2,2,2,24,3072]{4,3,2,1,0:T(8,128)(2,1)S(1)}, u32[]{:S(2)}, u32[]{:S(2)}) collective-permute-start(bf16[2,2,2,24,3072]{4,3,2,1,0:T(8,128)(2,1)S(1)} %pad_maximum_fusion.9), channel_id=1, source_target_pairs={{0,8},{4,12},{8,0},{12,4},{16,24},{20,28},{24,16},{28,20},{1,9},{5... | collective-permute-start | bytes 3538952 | tf_op jit(solution)/shard_map/ppermute | solution.py:222
  169.0 28.5 %collective-permute-start.41 = (bf16[2,2,2,96,768]{4,3,2,1,0:T(8,128)(2,1)S(1)}, bf16[2,2,2,96,768]{4,3,2,1,0:T(8,128)(2,1)S(1)}, u32[]{:S(2)}, u32[]{:S(2)}) collective-permute-start(bf16[2,2,2,96,768]{4,3,2,1,0:T(8,128)(2,1)S(1)} %pad_maximum_fusion.10), channel_id=1, source_target_pairs={{0,16},{4,20},{8,24},{12,28},{16,0},{20,4},{24,8},{28,12},{1,17},{... | collective-permute-start | bytes 3538952 | tf_op jit(solution)/shard_map/ppermute | solution.py:222
  176.5 20.7 %collective-permute-start.36 = (bf16[64,640]{1,0:T(8,128)(2,1)S(1)}, bf16[64,640]{1,0:T(8,128)(2,1)S(1)}, u32[]{:S(2)}, u32[]{:S(2)}) collective-permute-start(bf16[64,640]{1,0:T(8,128)(2,1)S(1)} %get-tuple-element.175), channel_id=1, source_target_pairs={{0,3},{1,2},{2,1},{3,0},{4,7},{5,6},{6,5},{7,4},{8,11},{9,10},{10,... | collective-permute-start | bytes 245768 | tf_op jit(solution)/shard_map/ppermute | solution.py:222
  235.7 42.5 %collective-permute-start.43 = (bf16[64,640]{1,0:T(8,128)(2,1)}, bf16[64,640]{1,0:T(8,128)(2,1)S(1)}, u32[]{:S(2)}, u32[]{:S(2)}) collective-permute-start(bf16[64,640]{1,0:T(8,128)(2,1)} %get-tuple-element.188), channel_id=1, source_target_pairs={{0,1},{1,0},{2,3},{3,2},{4,5},{5,4},{6,7},{7,6},{8,9},{9,8},{10,11... | collective-permute-start | bytes 245768 | tf_op jit(solution)/shard_map/ppermute | solution.py:222
  235.8 42.4 %collective-permute-start.44 = (bf16[64,640]{1,0:T(8,128)(2,1)}, bf16[64,640]{1,0:T(8,128)(2,1)S(1)}, u32[]{:S(2)}, u32[]{:S(2)}) collective-permute-start(bf16[64,640]{1,0:T(8,128)(2,1)} %get-tuple-element.189), channel_id=1, source_target_pairs={{0,2},{1,3},{2,0},{3,1},{4,6},{5,7},{6,4},{7,5},{8,10},{9,11},{10,... | collective-permute-start | bytes 245768 | tf_op jit(solution)/shard_map/ppermute | solution.py:222
  239.6 38.6 %collective-permute-start.45 = (bf16[64,640]{1,0:T(8,128)(2,1)}, bf16[64,640]{1,0:T(8,128)(2,1)S(1)}, u32[]{:S(2)}, u32[]{:S(2)}) collective-permute-start(bf16[64,640]{1,0:T(8,128)(2,1)} %get-tuple-element.190), channel_id=1, source_target_pairs={{0,3},{1,2},{2,1},{3,0},{4,7},{5,6},{6,5},{7,4},{8,11},{9,10},{10,... | collective-permute-start | bytes 245768 | tf_op jit(solution)/shard_map/ppermute | solution.py:222
  265.0 39.0 %collective-permute-start.52 = (bf16[2,2,2,2,96,768]{5,4,2,3,1,0:T(8,128)(2,1)}, bf16[2,2,2,2,96,768]{5,4,2,3,1,0:T(8,128)(2,1)}, u32[]{:S(2)}, u32[]{:S(2)}) collective-permute-start(bf16[2,2,2,2,96,768]{5,4,2,3,1,0:T(8,128)(2,1)} %get-tuple-element.334), channel_id=1, source_target_pairs={{0,4},{4,0},{8,12},{12,8},{16,20},{20,16},{24,28},{28,24},{1,5},{5... | collective-permute-start | bytes 7077896 | tf_op jit(solution)/shard_map/ppermute | solution.py:222
  268.4 39.7 %collective-permute-start.53 = (bf16[2,2,2,2,24,3840]{5,4,2,3,0,1:T(8,128)(2,1)}, bf16[2,2,2,2,24,3840]{5,4,2,3,0,1:T(8,128)(2,1)}, u32[]{:S(2)}, u32[]{:S(2)}) collective-permute-start(bf16[2,2,2,2,24,3840]{5,4,2,3,0,1:T(8,128)(2,1)} %get-tuple-element.330), channel_id=1, source_target_pairs={{0,4},{4,0},{8,12},{12,8},{16,20},{20,16},{24,28},{28,24},{1,5},{5... | collective-permute-start | bytes 8847368 | tf_op jit(solution)/shard_map/ppermute | solution.py:222
  278.2 21.7 %collective-permute-start.49 = (bf16[64,640]{1,0:T(8,128)(2,1)}, bf16[64,640]{1,0:T(8,128)(2,1)S(1)}, u32[]{:S(2)}, u32[]{:S(2)}) collective-permute-start(bf16[64,640]{1,0:T(8,128)(2,1)} %get-tuple-element.211), channel_id=1, source_target_pairs={{0,1},{1,0},{2,3},{3,2},{4,5},{5,4},{6,7},{7,6},{8,9},{9,8},{10,11... | collective-permute-start | bytes 245768 | tf_op jit(solution)/shard_map/ppermute | solution.py:222
  278.4 21.7 %collective-permute-start.50 = (bf16[64,640]{1,0:T(8,128)(2,1)}, bf16[64,640]{1,0:T(8,128)(2,1)S(1)}, u32[]{:S(2)}, u32[]{:S(2)}) collective-permute-start(bf16[64,640]{1,0:T(8,128)(2,1)} %get-tuple-element.212), channel_id=1, source_target_pairs={{0,2},{1,3},{2,0},{3,1},{4,6},{5,7},{6,4},{7,5},{8,10},{9,11},{10,... | collective-permute-start | bytes 245768 | tf_op jit(solution)/shard_map/ppermute | solution.py:222
  282.2 21.7 %collective-permute-start.51 = (bf16[64,640]{1,0:T(8,128)(2,1)}, bf16[64,640]{1,0:T(8,128)(2,1)S(1)}, u32[]{:S(2)}, u32[]{:S(2)}) collective-permute-start(bf16[64,640]{1,0:T(8,128)(2,1)} %get-tuple-element.213), channel_id=1, source_target_pairs={{0,3},{1,2},{2,1},{3,0},{4,7},{5,6},{6,5},{7,4},{8,11},{9,10},{10,... | collective-permute-start | bytes 245768 | tf_op jit(solution)/shard_map/ppermute | solution.py:222
  300.0 55.0 %collective-permute-start.46 = (bf16[192,640]{1,0:T(8,128)(2,1)S(1)}, bf16[192,640]{1,0:T(8,128)(2,1)S(1)}, u32[]{:S(2)}, u32[]{:S(2)}) collective-permute-start(bf16[192,640]{1,0:T(8,128)(2,1)S(1)} %get-tuple-element.204), channel_id=1, source_target_pairs={{0,1},{1,0},{2,3},{3,2},{4,5},{5,4},{6,7},{7,6},{8,9},{9,8},{10,11... | collective-permute-start | bytes 737288 | tf_op jit(solution)/shard_map/ppermute | solution.py:222
  300.1 76.0 %collective-permute-start.47 = (bf16[192,640]{1,0:T(8,128)(2,1)S(1)}, bf16[192,640]{1,0:T(8,128)(2,1)S(1)}, u32[]{:S(2)}, u32[]{:S(2)}) collective-permute-start(bf16[192,640]{1,0:T(8,128)(2,1)S(1)} %get-tuple-element.205), channel_id=1, source_target_pairs={{0,2},{1,3},{2,0},{3,1},{4,6},{5,7},{6,4},{7,5},{8,10},{9,11},{10,... | collective-permute-start | bytes 737288 | tf_op jit(solution)/shard_map/ppermute | solution.py:222
  304.0 43.6 %collective-permute-start.57 = (bf16[64,640]{1,0:T(8,128)(2,1)S(1)}, bf16[64,640]{1,0:T(8,128)(2,1)S(1)}, u32[]{:S(2)}, u32[]{:S(2)}) collective-permute-start(bf16[64,640]{1,0:T(8,128)(2,1)S(1)} %copy-done.49), channel_id=1, source_target_pairs={{0,1},{1,0},{2,3},{3,2},{4,5},{5,4},{6,7},{7,6},{8,9},{9,8},{10,11... | collective-permute-start | bytes 245768 | tf_op jit(solution)/shard_map/ppermute | solution.py:222
  306.6 27.0 %collective-permute-start.60 = (bf16[2,2,2,96,768]{4,3,1,2,0:T(8,128)(2,1)S(1)}, bf16[2,2,2,96,768]{4,3,1,2,0:T(8,128)(2,1)S(1)}, u32[]{:S(2)}, u32[]{:S(2)}) collective-permute-start(bf16[2,2,2,96,768]{4,3,1,2,0:T(8,128)(2,1)S(1)} %get-tuple-element.348), channel_id=1, source_target_pairs={{0,16},{4,20},{8,24},{12,28},{16,0},{20,4},{24,8},{28,12},{1,17},{... | collective-permute-start | bytes 3538952 | tf_op jit(solution)/shard_map/ppermute | solution.py:222
  311.1 33.4 %collective-permute-start.61 = (bf16[2,2,2,24,3840]{4,3,1,2,0:T(8,128)(2,1)S(1)}, bf16[2,2,2,24,3840]{4,3,1,2,0:T(8,128)(2,1)S(1)}, u32[]{:S(2)}, u32[]{:S(2)}) collective-permute-start(bf16[2,2,2,24,3840]{4,3,1,2,0:T(8,128)(2,1)S(1)} %get-tuple-element.342), channel_id=1, source_target_pairs={{0,8},{4,12},{8,0},{12,4},{16,24},{20,28},{24,16},{28,20},{1,9},{5... | collective-permute-start | bytes 4423688 | tf_op jit(solution)/shard_map/ppermute | solution.py:222
  333.7 16.2 %collective-permute-start.58 = (bf16[64,640]{1,0:T(8,128)(2,1)S(1)}, bf16[64,640]{1,0:T(8,128)(2,1)S(1)}, u32[]{:S(2)}, u32[]{:S(2)}) collective-permute-start(bf16[64,640]{1,0:T(8,128)(2,1)S(1)} %copy-done.48), channel_id=1, source_target_pairs={{0,2},{1,3},{2,0},{3,1},{4,6},{5,7},{6,4},{7,5},{8,10},{9,11},{10,... | collective-permute-start | bytes 245768 | tf_op jit(solution)/shard_map/ppermute | solution.py:222
  344.5 7.3 %collective-permute-start.59 = (bf16[64,640]{1,0:T(8,128)(2,1)S(1)}, bf16[64,640]{1,0:T(8,128)(2,1)S(1)}, u32[]{:S(2)}, u32[]{:S(2)}) collective-permute-start(bf16[64,640]{1,0:T(8,128)(2,1)S(1)} %copy-done.47), channel_id=1, source_target_pairs={{0,3},{1,2},{2,1},{3,0},{4,7},{5,6},{6,5},{7,4},{8,11},{9,10},{10,... | collective-permute-start | bytes 245768 | tf_op jit(solution)/shard_map/ppermute | solution.py:222
  347.5 29.2 %collective-permute-start.48 = (bf16[192,640]{1,0:T(8,128)(2,1)S(1)}, bf16[192,640]{1,0:T(8,128)(2,1)S(1)}, u32[]{:S(2)}, u32[]{:S(2)}) collective-permute-start(bf16[192,640]{1,0:T(8,128)(2,1)S(1)} %get-tuple-element.206), channel_id=1, source_target_pairs={{0,3},{1,2},{2,1},{3,0},{4,7},{5,6},{6,5},{7,4},{8,11},{9,10},{10,... | collective-permute-start | bytes 737288 | tf_op jit(solution)/shard_map/ppermute | solution.py:222
  349.9 28.4 %collective-permute-start.54 = (bf16[192,640]{1,0:T(8,128)(2,1)S(1)}, bf16[192,640]{1,0:T(8,128)(2,1)S(1)}, u32[]{:S(2)}, u32[]{:S(2)}) collective-permute-start(bf16[192,640]{1,0:T(8,128)(2,1)S(1)} %get-tuple-element.221), channel_id=1, source_target_pairs={{0,1},{1,0},{2,3},{3,2},{4,5},{5,4},{6,7},{7,6},{8,9},{9,8},{10,11... | collective-permute-start | bytes 737288 | tf_op jit(solution)/shard_map/ppermute | solution.py:222
  351.8 26.6 %collective-permute-start.55 = (bf16[192,640]{1,0:T(8,128)(2,1)S(1)}, bf16[192,640]{1,0:T(8,128)(2,1)S(1)}, u32[]{:S(2)}, u32[]{:S(2)}) collective-permute-start(bf16[192,640]{1,0:T(8,128)(2,1)S(1)} %get-tuple-element.222), channel_id=1, source_target_pairs={{0,2},{1,3},{2,0},{3,1},{4,6},{5,7},{6,4},{7,5},{8,10},{9,11},{10,... | collective-permute-start | bytes 737288 | tf_op jit(solution)/shard_map/ppermute | solution.py:222
  355.0 23.9 %collective-permute-start.56 = (bf16[192,640]{1,0:T(8,128)(2,1)S(1)}, bf16[192,640]{1,0:T(8,128)(2,1)S(1)}, u32[]{:S(2)}, u32[]{:S(2)}) collective-permute-start(bf16[192,640]{1,0:T(8,128)(2,1)S(1)} %get-tuple-element.223), channel_id=1, source_target_pairs={{0,3},{1,2},{2,1},{3,0},{4,7},{5,6},{6,5},{7,4},{8,11},{9,10},{10,... | collective-permute-start | bytes 737288 | tf_op jit(solution)/shard_map/ppermute | solution.py:222
  376.2 14.8 %collective-permute-start.65 = (bf16[2,2,96,768]{3,2,0,1:T(8,128)(2,1)S(1)}, bf16[2,2,96,768]{3,2,0,1:T(8,128)(2,1)S(1)}, u32[]{:S(2)}, u32[]{:S(2)}) collective-permute-start(bf16[2,2,96,768]{3,2,0,1:T(8,128)(2,1)S(1)} %get-tuple-element.364), channel_id=1, source_target_pairs={{0,8},{4,12},{8,0},{12,4},{16,24},{20,28},{24,16},{28,20},{1,9},{5... | collective-permute-start | bytes 1769480 | tf_op jit(solution)/shard_map/ppermute | solution.py:222
  376.7 33.4 %collective-permute-start.66 = (bf16[2,2,24,3840]{3,2,0,1:T(8,128)(2,1)}, bf16[2,2,24,3840]{3,2,0,1:T(8,128)(2,1)}, u32[]{:S(2)}, u32[]{:S(2)}) collective-permute-start(bf16[2,2,24,3840]{3,2,0,1:T(8,128)(2,1)} %get-tuple-element.358), channel_id=1, source_target_pairs={{0,16},{4,20},{8,24},{12,28},{16,0},{20,4},{24,8},{28,12},{1,17},{... | collective-permute-start | bytes 2211848 | tf_op jit(solution)/shard_map/ppermute | solution.py:222
  378.3 35.7 %collective-permute-start.62 = (bf16[192,640]{1,0:T(8,128)(2,1)S(1)}, bf16[192,640]{1,0:T(8,128)(2,1)S(1)}, u32[]{:S(2)}, u32[]{:S(2)}) collective-permute-start(bf16[192,640]{1,0:T(8,128)(2,1)S(1)} %get-tuple-element.238), channel_id=1, source_target_pairs={{0,1},{1,0},{2,3},{3,2},{4,5},{5,4},{6,7},{7,6},{8,9},{9,8},{10,11... | collective-permute-start | bytes 737288 | tf_op jit(solution)/shard_map/ppermute | solution.py:222
  378.4 35.7 %collective-permute-start.63 = (bf16[192,640]{1,0:T(8,128)(2,1)S(1)}, bf16[192,640]{1,0:T(8,128)(2,1)}, u32[]{:S(2)}, u32[]{:S(2)}) collective-permute-start(bf16[192,640]{1,0:T(8,128)(2,1)S(1)} %get-tuple-element.239), channel_id=1, source_target_pairs={{0,2},{1,3},{2,0},{3,1},{4,6},{5,7},{6,4},{7,5},{8,10},{9,11},{10,... | collective-permute-start | bytes 737288 | tf_op jit(solution)/shard_map/ppermute | solution.py:222
  378.9 35.1 %collective-permute-start.64 = (bf16[192,640]{1,0:T(8,128)(2,1)S(1)}, bf16[192,640]{1,0:T(8,128)(2,1)}, u32[]{:S(2)}, u32[]{:S(2)}) collective-permute-start(bf16[192,640]{1,0:T(8,128)(2,1)S(1)} %get-tuple-element.240), channel_id=1, source_target_pairs={{0,3},{1,2},{2,1},{3,0},{4,7},{5,6},{6,5},{7,4},{8,11},{9,10},{10,... | collective-permute-start | bytes 737288 | tf_op jit(solution)/shard_map/ppermute | solution.py:222
  392.0 22.8 %collective-permute-start.68 = (bf16[2,96,768]{2,1,0:T(8,128)(2,1)}, bf16[2,96,768]{2,1,0:T(8,128)(2,1)}, u32[]{:S(2)}, u32[]{:S(2)}) collective-permute-start(bf16[2,96,768]{2,1,0:T(8,128)(2,1)} %get-tuple-element.400), channel_id=1, source_target_pairs={{0,1},{1,0},{2,3},{3,2},{4,5},{5,4},{6,7},{7,6},{8,9},{9,8},{10,11... | collective-permute-start | bytes 884744 | tf_op jit(solution)/shard_map/ppermute | solution.py:222
  412.2 15.8 %collective-permute-start.69 = (bf16[2,24,3840]{2,1,0:T(8,128)(2,1)}, bf16[2,24,3840]{2,1,0:T(8,128)(2,1)}, u32[]{:S(2)}, u32[]{:S(2)}) collective-permute-start(bf16[2,24,3840]{2,1,0:T(8,128)(2,1)} %get-tuple-element.394), channel_id=1, source_target_pairs={{0,1},{1,0},{2,3},{3,2},{4,5},{5,4},{6,7},{7,6},{8,9},{9,8},{10,11... | collective-permute-start | bytes 1105928 | tf_op jit(solution)/shard_map/ppermute | solution.py:222
  414.1 15.8 %collective-permute-start.67 = (bf16[2,2,2,2,24,1536]{5,4,2,3,1,0:T(8,128)(2,1)}, bf16[2,2,2,2,24,1536]{5,4,2,3,1,0:T(8,128)(2,1)}, u32[]{:S(2)}, u32[]{:S(2)}) collective-permute-start(bf16[2,2,2,2,24,1536]{5,4,2,3,1,0:T(8,128)(2,1)} %get-tuple-element.344), channel_id=1, source_target_pairs={{0,4},{4,0},{8,12},{12,8},{16,20},{20,16},{24,28},{28,24},{1,5},{5... | collective-permute-start | bytes 3538952 | tf_op jit(solution)/shard_map/ppermute | solution.py:222
  423.4 15.8 %collective-permute-start.73 = (bf16[96,768]{1,0:T(8,128)(2,1)}, bf16[96,768]{1,0:T(8,128)(2,1)}, u32[]{:S(2)}, u32[]{:S(2)}) collective-permute-start(bf16[96,768]{1,0:T(8,128)(2,1)} %get-tuple-element.430), channel_id=1, source_target_pairs={{0,2},{1,3},{2,0},{3,1},{4,6},{5,7},{6,4},{7,5},{8,10},{9,11},{10,... | collective-permute-start | bytes 442376 | tf_op jit(solution)/shard_map/ppermute | solution.py:222
  429.9 12.3 %collective-permute-start.74 = (bf16[24,3840]{1,0:T(8,128)(2,1)}, bf16[24,3840]{1,0:T(8,128)(2,1)}, u32[]{:S(2)}, u32[]{:S(2)}) collective-permute-start(bf16[24,3840]{1,0:T(8,128)(2,1)} %get-tuple-element.412), channel_id=1, source_target_pairs={{0,2},{1,3},{2,0},{3,1},{4,6},{5,7},{6,4},{7,5},{8,10},{9,11},{10,... | collective-permute-start | bytes 552968 | tf_op jit(solution)/shard_map/ppermute | solution.py:222
  431.6 14.9 %collective-permute-start.70 = (bf16[2,2,2,24,1536]{4,3,1,2,0:T(8,128)(2,1)S(1)}, bf16[2,2,2,24,1536]{4,3,1,2,0:T(8,128)(2,1)S(1)}, u32[]{:S(2)}, u32[]{:S(2)}) collective-permute-start(bf16[2,2,2,24,1536]{4,3,1,2,0:T(8,128)(2,1)S(1)} %get-tuple-element.362), channel_id=1, source_target_pairs={{0,16},{4,20},{8,24},{12,28},{16,0},{20,4},{24,8},{28,12},{1,17},{... | collective-permute-start | bytes 1769480 | tf_op jit(solution)/shard_map/ppermute | solution.py:222
  439.2 8.0 %collective-permute-start.72 = (bf16[2,2,2,2,24,896]{5,4,3,2,1,0:T(8,128)(2,1)S(1)}, bf16[2,2,2,2,24,896]{5,4,3,2,1,0:T(8,128)(2,1)S(1)}, u32[]{:S(2)}, u32[]{:S(2)}) collective-permute-start(bf16[2,2,2,2,24,896]{5,4,3,2,1,0:T(8,128)(2,1)S(1)} %get-tuple-element.360), channel_id=1, source_target_pairs={{0,4},{4,0},{8,12},{12,8},{16,20},{20,16},{24,28},{28,24},{1,5},{5... | collective-permute-start | bytes 2064392 | tf_op jit(solution)/shard_map/ppermute | solution.py:222
  446.7 9.9 %collective-permute-start.71 = (bf16[2,2,24,1536]{3,2,0,1:T(8,128)(2,1)S(1)}, bf16[2,2,24,1536]{3,2,0,1:T(8,128)(2,1)S(1)}, u32[]{:S(2)}, u32[]{:S(2)}) collective-permute-start(bf16[2,2,24,1536]{3,2,0,1:T(8,128)(2,1)S(1)} %get-tuple-element.398), channel_id=1, source_target_pairs={{0,8},{4,12},{8,0},{12,4},{16,24},{20,28},{24,16},{28,20},{1,9},{5... | collective-permute-start | bytes 884744 | tf_op jit(solution)/shard_map/ppermute | solution.py:222
  447.5 14.3 %collective-permute-start.76 = (bf16[2,2,2,24,896]{4,3,2,1,0:T(8,128)(2,1)S(1)}, bf16[2,2,2,24,896]{4,3,2,1,0:T(8,128)(2,1)S(1)}, u32[]{:S(2)}, u32[]{:S(2)}) collective-permute-start(bf16[2,2,2,24,896]{4,3,2,1,0:T(8,128)(2,1)S(1)} %get-tuple-element.396), channel_id=1, source_target_pairs={{0,8},{4,12},{8,0},{12,4},{16,24},{20,28},{24,16},{28,20},{1,9},{5... | collective-permute-start | bytes 1032200 | tf_op jit(solution)/shard_map/ppermute | solution.py:222
  (101 other events, 863.2 us)

commit v2 on v0

--- a/solution.py
+++ b/solution.py
@@ -439,7 +439,6 @@
             grad_down = contract(hidden_late, grad_branch_late, ((0,), (0,))).astype(bf16)
             grad_up = contract(normed_b, grad_upsum_late, ((0,), (0,))).astype(bf16)
             grad_out = contract(heads_out, grad_attn_late, ((1,), (0,))).astype(bf16)
-            grad_up = jnp.concatenate([grad_up, grad_out], axis=1)
             late = [Scatter(grad_down, True), Scatter(grad_up, False)]
         parts.append(back)
     grad_projected = []
@@ -452,7 +451,7 @@
 
     whole = [in_order(pieces).reshape(groups * span, row_count) for pieces in grad_projected[:-1]]
     early = [row_major(contract(normed_a, part, ((0,), (1,))).astype(bf16)) for part in whole]
-    early = Scatter(after(jnp.concatenate(early, axis=1), sent), True)
+    early = Scatter(after(jnp.concatenate(early + [grad_out], axis=1), sent), True)
     pieces = after(grad_projected[-1], early.send())
     whole.append(in_order(pieces).reshape(groups * span, row_count))
     final = row_major(contract(normed_a, whole[-1], ((0,), (1,))).astype(bf16))
@@ -497,7 +496,7 @@
             for one in late:
                 one.receive(tied)
                 sent.append(one.send())
-        elif not late[0].order:
+        elif wave > 2 and not late[0].order:
             for one in late:
                 one.receive(tied)
                 sent.append(one.piece)
@@ -510,9 +509,10 @@
         one.receive(tied)
         one.finish()
     grad_down = late[0].piece
-    grad_up = late[1].piece[:, :wide]
-    grad_out = late[1].piece[:, wide:]
-    grad_qkv = [early.finish(), last.piece[:, : groups * span]]
+    grad_up = late[1].piece
+    early = early.finish()
+    grad_out = early[:, -width:]
+    grad_qkv = [early[:, :-width], last.piece[:, : groups * span]]
     extra = last.piece[:, groups * span :].astype(f32)
     return (
         outcome.astype(bf16)[None],

time: 485 us -> 475 us (0.979)
  waiting for transfers between devices: 109 us -> 94.3 us
  other arithmetic: 61.8 us -> 53.5 us
  starting transfers between devices: 127 us -> 135 us
  local copies, waits for them, and re-layouts: 35.9 us -> 43.5 us
    ppermute x81, waiting for transfers between devices: 109 us -> 94.3 us  [swap_with(): return lax.ppermute(values, axis, [(i, i ^ step) for i in range(size)])]
    another operation x15, local copies, waits for them, and re-layouts: 2.82 us -> 10.3 us  [on_device(): jnp.stack(grad_embed + [gain_grad_a, shift_grad_a, column_sums[:width], c...]
    ppermute x81, starting transfers between devices: 127 us -> 135 us  [swap_with(): return lax.ppermute(values, axis, [(i, i ^ step) for i in range(size)])]
    convert_element_type x19 -> x18, other arithmetic: 15.6 us -> 13.2 us  [receive(): self.piece = (self.kept.astype(f32) + other.astype(f32)).astype(bf16)]
    unnamed x136 -> x144, local copies, waits for them, and re-layouts: 11 us -> 12.8 us
  transfers between devices with their start and end apart: 81 -> 81, of which waited for: 35 -> 26; matrix products, arithmetic and copies ran while one was open for 20% -> 23% of each run, Pallas kernels for 12% -> 12%
where the time goes in v2:
time: 475 us; the launch traced here: 467 us
  starting transfers between devices  135 us (28%)
  waiting for transfers between devices  94.3 us (20%)
  Pallas kernels  75.5 us (16%)
  matrix products  62.8 us (13%)
  other arithmetic  53.5 us (11%)
  local copies, waits for them, and re-layouts  43.5 us (9%)
    ppermute x81, starting transfers between devices, swap_with(): return lax.ppermute(values, axis, [(i, i ^ step) for i in range(size)])  135 us
    ppermute x81, waiting for transfers between devices, swap_with(): return lax.ppermute(values, axis, [(i, i ^ step) for i in range(size)])  94.3 us
    dot_general x18, matrix products, contract(): lax.dot_general(left, right, (dims, ((), ())), preferred_element_type=f32)  62.8 us
    pallas_call x3, Pallas kernels, attend_back(): pl.pallas_call(functools.partial(backward_kernel, groups), out_shape=[jax...  53.4 us
    pallas_call x3, Pallas kernels, attend(): pl.pallas_call(functools.partial(forward_kernel, groups), out_shape=[jax....  22 us
    convert_element_type x18, other arithmetic, receive(): self.piece = (self.kept.astype(f32) + other.astype(f32)).astype(bf16)  13.2 us
    unnamed x144, local copies, waits for them, and re-layouts  12.8 us
    another operation x15, local copies, waits for them, and re-layouts, on_device(): jnp.stack(grad_embed + [gain_grad_a, shift_grad_a, column_sums[:width], c...  10.3 us
  transfers between devices with their start and end apart: 81, of which 26 were waited for; matrix products, arithmetic and copies ran while one was open for 23% of the time, Pallas kernels for 12%

profile of v2, /device:TPU:0, one launch (start us, length us, event | category | flops | bytes accessed | tf_op | source)
XLA Modules:
  0.0 466.8 jit_solution(909051203342618057)
XLA Ops:
  2.1 4.1 collective-permute-start.11
  9.1 2.4 collective-permute-start
  11.6 2.1 collective-permute-start.12
  19.4 3.0 collective-permute-start.25
  24.4 2.1 collective-permute-start.26
  29.6 3.3 collective-permute-start.22
  33.0 6.1 %collective-permute-done.22 = bf16[96,768]{1,0:T(8,128)(2,1)S(1)} collective-permute-done((bf16[96,768]{1,0:T(8,128)(2,1)S(1)}, bf16[96,768]{1,0:T(8,128)(2,1)S(1)}, u32[]{:S(2)}, u32[]{:S(2)}) %collective-permute-start.22) | collective-permute-done | bytes 147488 | tf_op jit(solution)/shard_map/ppermute | solution.py:204
  43.1 9.0 %collective-permute-done.20 = bf16[2,24,3072]{2,1,0:T(8,128)(2,1)S(1)} collective-permute-done((bf16[2,24,3072]{2,1,0:T(8,128)(2,1)S(1)}, bf16[2,24,3072]{2,1,0:T(8,128)(2,1)S(1)}, u32[]{:S(2)}, u32[]{:S(2)}) %collective-permute-start.20) | collective-permute-done | bytes 294944 | tf_op jit(solution)/shard_map/ppermute | solution.py:204
  57.2 2.7 slice_reduce_fusion
  61.8 2.6 add_convert_fusion.9
  64.4 2.3 fusion.28
  67.3 2.9 select_reduce_fusion
  74.3 2.1 add_convert_fusion.6
  81.4 3.7 collective-permute-start.7
  87.5 6.4 %collective-permute-done.6.refs_2_ = bf16[192,640]{1,0:T(8,128)(2,1)S(1)} collective-permute-done((bf16[192,640]{1,0:T(8,128)(2,1)S(1)}, bf16[192,640]{1,0:T(8,128)(2,1)S(1)}, u32[]{:S(2)}, u32[]{:S(2)}) %collective-permute-start.6) | collective-permute-done | bytes 245792 | tf_op jit(solution)/shard_map/ppermute | solution.py:204
  94.0 4.2 collective-permute-start.16
  98.2 7.3 %attend.3 = (bf16[192,2560]{1,0:T(8,128)(2,1)S(1)}, bf16[64,2560]{1,0:T(8,128)(2,1)S(1)}, f32[5,512]{1,0:T(8,128)S(1)}, bf16[64,640]{1,0:T(8,128)(2,1)S(1)}, bf1...) custom-call(s32[1,5]{1,0:T(1,128)S(1)} %copy-done, s32[1]{0:T(128)} %bitcast.16.here, ...), custom_call_target="tpu_custom_call" | custom-call | flops 10000000000 | bytes 1000000 | tf_op jit(solution)/shard_map/attend/pallas_call | solution.py:147
  106.2 2.4 collective-permute-start.18
  110.2 8.8 %collective-permute-start.8 = (bf16[64,640]{1,0:T(8,128)(2,1)S(1)}, bf16[64,640]{1,0:T(8,128)(2,1)S(1)}, u32[]{:S(2)}, u32[]{:S(2)}) collective-permute-start(bf16[64,640]{1,0:T(8,128)(2,1)S(1)} %get-tuple-element.140), channel_id=1, source_target_pairs={{0,1},{1,0},{2,3},{3,2},{4,5},{5,4},{6,7},{7,6},{8,9},{9,8},{10,11... | collective-permute-start | bytes 245768 | tf_op jit(solution)/shard_map/ppermute | solution.py:204
  119.0 4.8 %collective-permute-start.31 = (bf16[192,640]{1,0:T(8,128)(2,1)S(1)}, bf16[192,640]{1,0:T(8,128)(2,1)S(1)}, u32[]{:S(2)}, u32[]{:S(2)}) collective-permute-start(bf16[192,640]{1,0:T(8,128)(2,1)S(1)} %get-tuple-element.165), channel_id=1, source_target_pairs={{0,1},{1,0},{2,3},{3,2},{4,5},{5,4},{6,7},{7,6},{8,9},{9,8},{10,11... | collective-permute-start | bytes 737288 | tf_op jit(solution)/shard_map/ppermute | solution.py:204
  130.0 7.5 %attend.4 = (bf16[192,2560]{1,0:T(8,128)(2,1)S(1)}, bf16[64,2560]{1,0:T(8,128)(2,1)S(1)}, f32[5,512]{1,0:T(8,128)S(1)}, bf16[64,640]{1,0:T(8,128)(2,1)S(1)}, bf1...) custom-call(s32[1,5]{1,0:T(1,128)S(1)} %copy-done, s32[1]{0:T(128)} %bitcast.16.here, ...), custom_call_target="tpu_custom_call" | custom-call | flops 10000000000 | bytes 1000000 | tf_op jit(solution)/shard_map/attend/pallas_call | solution.py:147
  137.5 2.1 collective-permute-start.9
  140.5 7.0 %collective-permute-done.32.refs_2_ = bf16[192,640]{1,0:T(8,128)(2,1)S(1)} collective-permute-done((bf16[192,640]{1,0:T(8,128)(2,1)S(1)}, bf16[192,640]{1,0:T(8,128)(2,1)S(1)}, u32[]{:S(2)}, u32[]{:S(2)}) %collective-permute-start.32) | collective-permute-done | bytes 245792 | tf_op jit(solution)/shard_map/ppermute | solution.py:204
  147.6 3.4 collective-permute-start.30
  151.0 7.3 %attend.5 = (bf16[192,2560]{1,0:T(8,128)(2,1)S(1)}, bf16[64,2560]{1,0:T(8,128)(2,1)S(1)}, f32[5,512]{1,0:T(8,128)S(1)}, bf16[64,640]{1,0:T(8,128)(2,1)S(1)}, bf1...) custom-call(s32[1,5]{1,0:T(1,128)S(1)} %copy-done, s32[1]{0:T(128)} %bitcast.16.here, ...), custom_call_target="tpu_custom_call" | custom-call | flops 10000000000 | bytes 1000000 | tf_op jit(solution)/shard_map/attend/pallas_call | solution.py:147
  160.8 6.1 %collective-permute-start.34 = (bf16[64,640]{1,0:T(8,128)(2,1)S(1)}, bf16[64,640]{1,0:T(8,128)(2,1)S(1)}, u32[]{:S(2)}, u32[]{:S(2)}) collective-permute-start(bf16[64,640]{1,0:T(8,128)(2,1)S(1)} %get-tuple-element.169), channel_id=1, source_target_pairs={{0,1},{1,0},{2,3},{3,2},{4,5},{5,4},{6,7},{7,6},{8,9},{9,8},{10,11... | collective-permute-start | bytes 245768 | tf_op jit(solution)/shard_map/ppermute | solution.py:204
  167.3 2.3 collective-permute-done.34
  170.5 4.4 collective-permute-done.35
  174.8 12.3 %collective-permute-done.41 = bf16[2,2,2,96,768]{4,3,2,1,0:T(8,128)(2,1)S(1)} collective-permute-done((bf16[2,2,2,96,768]{4,3,2,1,0:T(8,128)(2,1)S(1)}, bf16[2,2,2,96,768]{4,3,2,1,0:T(8,128)(2,1)S(1)}, u32[]{:S(2)}, u32[]{:S(2)}) %collective-permute-start.41) | collective-permute-done | bytes 1179680 | tf_op jit(solution)/shard_map/ppermute | solution.py:204
  193.0 2.5 collective-permute-done.40
  196.5 7.9 %multiply_convert_fusion = (bf16[640,3072]{1,0:T(8,128)(2,1)}, f32[640,3072]{1,0:T(8,128)}) fusion(f32[3072]{0:T(1024)S(1)} %copy-done.63, bf16[768,3072]{1,0:T(8,128)(2,1)S(1)} %bitcast.432, f32[640,768]{1,0:T(8,128)S(1)} %get-tuple-element.450, f32[768]{0:T(1024)S(1)} %copy-done.65, f32[768]{0:T(1024)S(1)} %copy-done.62, f32[640]{0:T(1024)S(1)} %add_rsqrt_fusion, ...), kind=kOutput, calls=%fused_computation.9 | convolution fusion | flops 3042017280 | bytes 18504704 | tf_op jit(solution)/shard_map/dot_general | solution.py:34
  204.5 10.4 %fusion.75 = (bf16[3072]{0:T(1024)(128)(2,1)S(1)}, bf16[640,3072]{1,0:T(8,128)(2,1)S(1)}) fusion(f32[640,3072]{1,0:T(8,128)} %get-tuple-element.452, f32[3072]{0:T(1024)S(1)} %copy-done.63, bf16[3072,768]{1,0:T(8,128)(2,1)S(1)} %bitcast.430, bf16[1,640,768]{2,1,0:T(8,128)(2,1)S(1)} %copy-done.32, f32[640]{0:T(1024)S(1)} %fusion.59), kind=kOutput, calls=%fused_computation.361 | convolution fusion | flops 3064624128 | bytes 17519104 | tf_op jit(solution)/shard_map/dot_general | solution.py:34
  214.8 3.7 multiply_reduce_fusion
  218.5 2.3 fusion.64
  223.5 6.1 %collective-permute-start.43 = (bf16[64,640]{1,0:T(8,128)(2,1)}, bf16[64,640]{1,0:T(8,128)(2,1)S(1)}, u32[]{:S(2)}, u32[]{:S(2)}) collective-permute-start(bf16[64,640]{1,0:T(8,128)(2,1)} %get-tuple-element.184), channel_id=1, source_target_pairs={{0,1},{1,0},{2,3},{3,2},{4,5},{5,4},{6,7},{7,6},{8,9},{9,8},{10,11... | collective-permute-start | bytes 245768 | tf_op jit(solution)/shard_map/ppermute | solution.py:204
  229.7 2.4 collective-permute-start.45
  235.6 8.4 %multiply_add_fusion.1 = bf16[640,768]{1,0:T(8,128)(2,1)} fusion(f32[640,768]{1,0:T(8,128)} %copy-done.14, bf16[640,3072]{1,0:T(8,128)(2,1)} %get-tuple-element.202, bf16[3072,768]{1,0:T(8,128)(2,1)} %bitcast.431, f32[768]{0:T(1024)S(1)} %copy-done.66, f32[640]{0:T(1024)S(1)} %fusion.59), kind=kOutput, calls=%fused_computation.62 | convolution fusion | flops 3021864960 | bytes 11605504 | tf_op jit(solution)/shard_map/dot_general | solution.py:34
  244.1 17.7 %attend_back.3 = (bf16[192,640]{1,0:T(8,128)(2,1)S(1)}, bf16[192,640]{1,0:T(8,128)(2,1)S(1)}, bf16[192,640]{1,0:T(8,128)(2,1)S(1)}, bf16[192,640]{1,0:T(8,128)(2,1)S(1)}) custom-call(s32[1,5]{1,0:T(1,128)S(1)} %copy-done, s32[1]{0:T(128)} %bitcast.16.here, bf16[192,2560]{1,0:T(8,128)(2,1)S(1)} %copy-done.2, bf16[64,2560]{1,0:T(8,128)(2,1)S(1)} %copy-done.4, ...), custom_call_target="tpu_custom_call" | custom-call | flops 15000000512 | bytes 1000000 | tf_op jit(solution)/shard_map/attend_back/pallas_call | solution.py:172
  263.0 5.0 %convolution_convert_fusion = bf16[768,3072]{1,0:T(8,128)(2,1)S(1)} fusion(bf16[640,3072]{1,0:T(8,128)(2,1)S(1)} %copy-done.70, f32[640,768]{1,0:T(8,128)S(1)} %copy-done.15, f32[768]{0:T(1024)S(1)} %copy-done.65, f32[768]{0:T(1024)S(1)} %copy-done.62, f32[640]{0:T(1024)S(1)} %add_rsqrt_fusion, f32[640]{0:T(1024)S(1)} %broadcast_multiply_fusion.4), kind=kOutput, calls=%fused_computation.12 | convolution fusion | flops 3024715776 | bytes 10628096 | tf_op jit(solution)/shard_map/dot_general | solution.py:34
  270.9 4.2 convolution_convert_fusion.1
  277.5 2.8 collective-permute-start.51
  281.8 2.1 convolution_convert_fusion.3
  284.0 6.8 %collective-permute-done.50.refs_2_ = bf16[64,640]{1,0:T(8,128)(2,1)S(1)} collective-permute-done((bf16[64,640]{1,0:T(8,128)(2,1)S(1)}, bf16[64,640]{1,0:T(8,128)(2,1)S(1)}, u32[]{:S(2)}, u32[]{:S(2)}) %collective-permute-start.50) | collective-permute-done | bytes 81952 | tf_op jit(solution)/shard_map/ppermute | solution.py:204
  290.8 2.3 collective-permute-start.55
  293.1 17.7 %attend_back.4 = (bf16[192,640]{1,0:T(8,128)(2,1)S(1)}, bf16[192,640]{1,0:T(8,128)(2,1)S(1)}, bf16[192,640]{1,0:T(8,128)(2,1)S(1)}, bf16[192,640]{1,0:T(8,128)(2,1)S(1)}) custom-call(s32[1,5]{1,0:T(1,128)S(1)} %copy-done, s32[1]{0:T(128)} %bitcast.16.here, bf16[192,2560]{1,0:T(8,128)(2,1)S(1)} %get-tuple-element.195.packed, ...), custom_call_target="tpu_custom_call" | custom-call | flops 15000000512 | bytes 1000000 | tf_op jit(solution)/shard_map/attend_back/pallas_call | solution.py:172
  313.4 2.3 collective-permute-start.57
  319.8 2.7 collective-permute-start.53
  324.0 18.1 %attend_back.5 = (bf16[192,640]{1,0:T(8,128)(2,1)S(1)}, bf16[192,640]{1,0:T(8,128)(2,1)S(1)}, bf16[192,640]{1,0:T(8,128)(2,1)S(1)}, bf16[192,640]{1,0:T(8,128)(2,1)S(1)}) custom-call(s32[1,5]{1,0:T(1,128)S(1)} %copy-done, s32[1]{0:T(128)} %bitcast.16.here, bf16[192,2560]{1,0:T(8,128)(2,1)S(1)} %get-tuple-element.213.packed, ...), custom_call_target="tpu_custom_call" | custom-call | flops 15000000512 | bytes 1000000 | tf_op jit(solution)/shard_map/attend_back/pallas_call | solution.py:172
  344.1 4.1 collective-permute-done.53
  351.9 2.3 fusion.60
  354.1 2.1 convolution_convert_fusion.4
  358.7 2.8 convolution_convert_fusion.5
  361.5 2.3 fusion.20
  364.1 4.5 collective-permute-done.64
  376.9 2.1 select_bitcast_fusion.8
  382.7 3.5 convolution_convert_fusion.2
  390.0 12.3 %collective-permute-start.72 = (bf16[2,24,3072]{2,1,0:T(8,128)(2,1)}, bf16[2,24,3072]{2,1,0:T(8,128)(2,1)}, u32[]{:S(2)}, u32[]{:S(2)}) collective-permute-start(bf16[2,24,3072]{2,1,0:T(8,128)(2,1)} %get-tuple-element.390), channel_id=1, source_target_pairs={{0,1},{1,0},{2,3},{3,2},{4,5},{5,4},{6,7},{7,6},{8,9},{9,8},{10,11... | collective-permute-start | bytes 884744 | tf_op jit(solution)/shard_map/ppermute | solution.py:204
  409.4 2.8 select_reduce_fusion.1
  416.3 2.7 stack.415
  431.2 10.7 %collective-permute-done.69 = bf16[2,2,24,2304]{3,2,0,1:T(8,128)(2,1)S(1)} collective-permute-done((bf16[2,2,24,2304]{3,2,0,1:T(8,128)(2,1)S(1)}, bf16[2,2,24,2304]{3,2,0,1:T(8,128)(2,1)S(1)}, u32[]{:S(2)}, u32[]{:S(2)}) %collective-permute-start.69) | collective-permute-done | bytes 442400 | tf_op jit(solution)/shard_map/ppermute | solution.py:204
  442.1 2.1 collective-permute-start.73
  444.1 4.1 collective-permute-done.74
  453.9 2.1 collective-permute-start.77
  461.2 2.3 collective-permute-done.80
  (478 shorter events, 141.4 us)
Async XLA Ops:
  24.4 8.6 %collective-permute-start.26 = (bf16[2,24,768]{2,1,0:T(8,128)(2,1)S(1)}, bf16[2,24,768]{2,1,0:T(8,128)(2,1)S(1)}, u32[]{:S(2)}, u32[]{:S(2)}) collective-permute-start(bf16[2,24,768]{2,1,0:T(8,128)(2,1)S(1)} %pad_maximum_fusion.27), channel_id=1, source_target_pairs={{0,1},{1,0},{2,3},{3,2},{4,5},{5,4},{6,7},{7,6},{8,9},{9,8},{10,11... | collective-permute-start | bytes 221192 | tf_op jit(solution)/shard_map/ppermute | solution.py:204
  26.5 12.8 %collective-permute-start.13 = (bf16[2,2,24,1152]{3,2,0,1:T(8,128)(2,1)S(1)}, bf16[2,2,24,1152]{3,2,0,1:T(8,128)(2,1)S(1)}, u32[]{:S(2)}, u32[]{:S(2)}) collective-permute-start(bf16[2,2,24,1152]{3,2,0,1:T(8,128)(2,1)S(1)} %pad_maximum_fusion.23), channel_id=1, source_target_pairs={{0,8},{4,12},{8,0},{12,4},{16,24},{20,28},{24,16},{28,20},{1,9},{5... | collective-permute-start | bytes 663560 | tf_op jit(solution)/shard_map/ppermute | solution.py:204
  28.1 14.3 %collective-permute-start.2 = (bf16[2,2,24,1280]{3,2,0,1:T(8,128)(2,1)S(1)}, bf16[2,2,24,1280]{3,2,0,1:T(8,128)(2,1)S(1)}, u32[]{:S(2)}, u32[]{:S(2)}) collective-permute-start(bf16[2,2,24,1280]{3,2,0,1:T(8,128)(2,1)S(1)} %pad_maximum_fusion.22), channel_id=1, source_target_pairs={{0,16},{4,20},{8,24},{12,28},{16,0},{20,4},{24,8},{28,12},{1,17},{... | collective-permute-start | bytes 737288 | tf_op jit(solution)/shard_map/ppermute | solution.py:204
  29.6 9.6 %collective-permute-start.22 = (bf16[96,768]{1,0:T(8,128)(2,1)S(1)}, bf16[96,768]{1,0:T(8,128)(2,1)S(1)}, u32[]{:S(2)}, u32[]{:S(2)}) collective-permute-start(bf16[96,768]{1,0:T(8,128)(2,1)S(1)} %copy-done.42), channel_id=1, source_target_pairs={{0,2},{1,3},{2,0},{3,1},{4,6},{5,7},{6,4},{7,5},{8,10},{9,11},{10,... | collective-permute-start | bytes 442376 | tf_op jit(solution)/shard_map/ppermute | solution.py:204
  32.9 8.2 %collective-permute-start.19 = (bf16[24,3072]{1,0:T(8,128)(2,1)S(1)}, bf16[24,3072]{1,0:T(8,128)(2,1)S(1)}, u32[]{:S(2)}, u32[]{:S(2)}) collective-permute-start(bf16[24,3072]{1,0:T(8,128)(2,1)S(1)} %copy-done.43), channel_id=1, source_target_pairs={{0,2},{1,3},{2,0},{3,1},{4,6},{5,7},{6,4},{7,5},{8,10},{9,11},{10,... | collective-permute-start | bytes 442376 | tf_op jit(solution)/shard_map/ppermute | solution.py:204
  39.2 12.9 %collective-permute-start.23 = (bf16[2,96,768]{2,1,0:T(8,128)(2,1)S(1)}, bf16[2,96,768]{2,1,0:T(8,128)(2,1)S(1)}, u32[]{:S(2)}, u32[]{:S(2)}) collective-permute-start(bf16[2,96,768]{2,1,0:T(8,128)(2,1)S(1)} %pad_maximum_fusion.20), channel_id=1, source_target_pairs={{0,1},{1,0},{2,3},{3,2},{4,5},{5,4},{6,7},{7,6},{8,9},{9,8},{10,11... | collective-permute-start | bytes 884744 | tf_op jit(solution)/shard_map/ppermute | solution.py:204
  39.4 12.9 %collective-permute-start.14 = (bf16[2,2,2,24,1152]{4,3,1,2,0:T(8,128)(2,1)S(1)}, bf16[2,2,2,24,1152]{4,3,1,2,0:T(8,128)(2,1)S(1)}, u32[]{:S(2)}, u32[]{:S(2)}) collective-permute-start(bf16[2,2,2,24,1152]{4,3,1,2,0:T(8,128)(2,1)S(1)} %pad_maximum_fusion.18), channel_id=1, source_target_pairs={{0,16},{4,20},{8,24},{12,28},{16,0},{20,4},{24,8},{28,12},{1,17},{... | collective-permute-start | bytes 1327112 | tf_op jit(solution)/shard_map/ppermute | solution.py:204
  41.2 10.9 %collective-permute-start.20 = (bf16[2,24,3072]{2,1,0:T(8,128)(2,1)S(1)}, bf16[2,24,3072]{2,1,0:T(8,128)(2,1)S(1)}, u32[]{:S(2)}, u32[]{:S(2)}) collective-permute-start(bf16[2,24,3072]{2,1,0:T(8,128)(2,1)S(1)} %pad_maximum_fusion.19), channel_id=1, source_target_pairs={{0,1},{1,0},{2,3},{3,2},{4,5},{5,4},{6,7},{7,6},{8,9},{9,8},{10,11... | collective-permute-start | bytes 884744 | tf_op jit(solution)/shard_map/ppermute | solution.py:204
  42.5 10.1 %collective-permute-start.3 = (bf16[2,2,2,24,1280]{4,3,1,2,0:T(8,128)(2,1)S(1)}, bf16[2,2,2,24,1280]{4,3,1,2,0:T(8,128)(2,1)S(1)}, u32[]{:S(2)}, u32[]{:S(2)}) collective-permute-start(bf16[2,2,2,24,1280]{4,3,1,2,0:T(8,128)(2,1)S(1)} %pad_maximum_fusion.17), channel_id=1, source_target_pairs={{0,8},{4,12},{8,0},{12,4},{16,24},{20,28},{24,16},{28,20},{1,9},{5... | collective-permute-start | bytes 1474568 | tf_op jit(solution)/shard_map/ppermute | solution.py:204
  66.6 57.2 %collective-permute-start.24 = (bf16[2,2,96,768]{3,2,1,0:T(8,128)(2,1)}, bf16[2,2,96,768]{3,2,1,0:T(8,128)(2,1)}, u32[]{:S(2)}, u32[]{:S(2)}) collective-permute-start(bf16[2,2,96,768]{3,2,1,0:T(8,128)(2,1)} %pad_maximum_fusion.15), channel_id=1, source_target_pairs={{0,8},{4,12},{8,0},{12,4},{16,24},{20,28},{24,16},{28,20},{1,9},{5... | collective-permute-start | bytes 1769480 | tf_op jit(solution)/shard_map/ppermute | solution.py:204
  70.2 10.5 %collective-permute-start.27 = (bf16[2,2,24,768]{3,2,1,0:T(8,128)(2,1)S(1)}, bf16[2,2,24,768]{3,2,1,0:T(8,128)(2,1)S(1)}, u32[]{:S(2)}, u32[]{:S(2)}) collective-permute-start(bf16[2,2,24,768]{3,2,1,0:T(8,128)(2,1)S(1)} %pad_maximum_fusion.24), channel_id=1, source_target_pairs={{0,16},{4,20},{8,24},{12,28},{16,0},{20,4},{24,8},{28,12},{1,17},{... | collective-permute-start | bytes 442376 | tf_op jit(solution)/shard_map/ppermute | solution.py:204
  70.8 56.4 %collective-permute-start.21 = (bf16[2,2,24,3072]{3,2,1,0:T(8,128)(2,1)S(1)}, bf16[2,2,24,3072]{3,2,1,0:T(8,128)(2,1)}, u32[]{:S(2)}, u32[]{:S(2)}) collective-permute-start(bf16[2,2,24,3072]{3,2,1,0:T(8,128)(2,1)S(1)} %pad_maximum_fusion.14), channel_id=1, source_target_pairs={{0,16},{4,20},{8,24},{12,28},{16,0},{20,4},{24,8},{28,12},{1,17},{... | collective-permute-start | bytes 1769480 | tf_op jit(solution)/shard_map/ppermute | solution.py:204
  73.6 12.5 %collective-permute-start.5 = (bf16[192,640]{1,0:T(8,128)(2,1)S(1)}, bf16[192,640]{1,0:T(8,128)(2,1)S(1)}, u32[]{:S(2)}, u32[]{:S(2)}) collective-permute-start(bf16[192,640]{1,0:T(8,128)(2,1)S(1)} %get-tuple-element.136), channel_id=1, source_target_pairs={{0,1},{1,0},{2,3},{3,2},{4,5},{5,4},{6,7},{7,6},{8,9},{9,8},{10,11... | collective-permute-start | bytes 737288 | tf_op jit(solution)/shard_map/ppermute | solution.py:204
  73.6 20.3 %collective-permute-start.6 = (bf16[192,640]{1,0:T(8,128)(2,1)S(1)}, bf16[192,640]{1,0:T(8,128)(2,1)S(1)}, u32[]{:S(2)}, u32[]{:S(2)}) collective-permute-start(bf16[192,640]{1,0:T(8,128)(2,1)S(1)} %get-tuple-element.137), channel_id=1, source_target_pairs={{0,2},{1,3},{2,0},{3,1},{4,6},{5,7},{6,4},{7,5},{8,10},{9,11},{10,... | collective-permute-start | bytes 737288 | tf_op jit(solution)/shard_map/ppermute | solution.py:204
  81.4 12.6 %collective-permute-start.7 = (bf16[192,640]{1,0:T(8,128)(2,1)S(1)}, bf16[192,640]{1,0:T(8,128)(2,1)S(1)}, u32[]{:S(2)}, u32[]{:S(2)}) collective-permute-start(bf16[192,640]{1,0:T(8,128)(2,1)S(1)} %get-tuple-element.138), channel_id=1, source_target_pairs={{0,3},{1,2},{2,1},{3,0},{4,7},{5,6},{6,5},{7,4},{8,11},{9,10},{10,... | collective-permute-start | bytes 737288 | tf_op jit(solution)/shard_map/ppermute | solution.py:204
  86.1 20.1 %collective-permute-start.37 = (bf16[2,2,2,24,768]{4,3,2,1,0:T(8,128)(2,1)S(1)}, bf16[2,2,2,24,768]{4,3,2,1,0:T(8,128)(2,1)S(1)}, u32[]{:S(2)}, u32[]{:S(2)}) collective-permute-start(bf16[2,2,2,24,768]{4,3,2,1,0:T(8,128)(2,1)S(1)} %pad_maximum_fusion.21), channel_id=1, source_target_pairs={{0,8},{4,12},{8,0},{12,4},{16,24},{20,28},{24,16},{28,20},{1,9},{5... | collective-permute-start | bytes 884744 | tf_op jit(solution)/shard_map/ppermute | solution.py:204
  94.0 14.7 %collective-permute-start.16 = (bf16[192,640]{1,0:T(8,128)(2,1)}, bf16[192,640]{1,0:T(8,128)(2,1)S(1)}, u32[]{:S(2)}, u32[]{:S(2)}) collective-permute-start(bf16[192,640]{1,0:T(8,128)(2,1)} %get-tuple-element.144), channel_id=1, source_target_pairs={{0,1},{1,0},{2,3},{3,2},{4,5},{5,4},{6,7},{7,6},{8,9},{9,8},{10,11... | collective-permute-start | bytes 737288 | tf_op jit(solution)/shard_map/ppermute | solution.py:204
  98.2 12.0 %collective-permute-start.17 = (bf16[192,640]{1,0:T(8,128)(2,1)}, bf16[192,640]{1,0:T(8,128)(2,1)S(1)}, u32[]{:S(2)}, u32[]{:S(2)}) collective-permute-start(bf16[192,640]{1,0:T(8,128)(2,1)} %get-tuple-element.145), channel_id=1, source_target_pairs={{0,2},{1,3},{2,0},{3,1},{4,6},{5,7},{6,4},{7,5},{8,10},{9,11},{10,... | collective-permute-start | bytes 737288 | tf_op jit(solution)/shard_map/ppermute | solution.py:204
  106.2 12.8 %collective-permute-start.18 = (bf16[192,640]{1,0:T(8,128)(2,1)S(1)}, bf16[192,640]{1,0:T(8,128)(2,1)S(1)}, u32[]{:S(2)}, u32[]{:S(2)}) collective-permute-start(bf16[192,640]{1,0:T(8,128)(2,1)S(1)} %get-tuple-element.146), channel_id=1, source_target_pairs={{0,3},{1,2},{2,1},{3,0},{4,7},{5,6},{6,5},{7,4},{8,11},{9,10},{10,... | collective-permute-start | bytes 737288 | tf_op jit(solution)/shard_map/ppermute | solution.py:204
  108.7 28.9 %collective-permute-start.10 = (bf16[64,640]{1,0:T(8,128)(2,1)S(1)}, bf16[64,640]{1,0:T(8,128)(2,1)S(1)}, u32[]{:S(2)}, u32[]{:S(2)}) collective-permute-start(bf16[64,640]{1,0:T(8,128)(2,1)S(1)} %get-tuple-element.142), channel_id=1, source_target_pairs={{0,3},{1,2},{2,1},{3,0},{4,7},{5,6},{6,5},{7,4},{8,11},{9,10},{10,... | collective-permute-start | bytes 245768 | tf_op jit(solution)/shard_map/ppermute | solution.py:204
  110.2 48.0 %collective-permute-start.8 = (bf16[64,640]{1,0:T(8,128)(2,1)S(1)}, bf16[64,640]{1,0:T(8,128)(2,1)S(1)}, u32[]{:S(2)}, u32[]{:S(2)}) collective-permute-start(bf16[64,640]{1,0:T(8,128)(2,1)S(1)} %get-tuple-element.140), channel_id=1, source_target_pairs={{0,1},{1,0},{2,3},{3,2},{4,5},{5,4},{6,7},{7,6},{8,9},{9,8},{10,11... | collective-permute-start | bytes 245768 | tf_op jit(solution)/shard_map/ppermute | solution.py:204
  119.0 20.7 %collective-permute-start.31 = (bf16[192,640]{1,0:T(8,128)(2,1)S(1)}, bf16[192,640]{1,0:T(8,128)(2,1)S(1)}, u32[]{:S(2)}, u32[]{:S(2)}) collective-permute-start(bf16[192,640]{1,0:T(8,128)(2,1)S(1)} %get-tuple-element.165), channel_id=1, source_target_pairs={{0,1},{1,0},{2,3},{3,2},{4,5},{5,4},{6,7},{7,6},{8,9},{9,8},{10,11... | collective-permute-start | bytes 737288 | tf_op jit(solution)/shard_map/ppermute | solution.py:204
  123.8 23.8 %collective-permute-start.32 = (bf16[192,640]{1,0:T(8,128)(2,1)S(1)}, bf16[192,640]{1,0:T(8,128)(2,1)S(1)}, u32[]{:S(2)}, u32[]{:S(2)}) collective-permute-start(bf16[192,640]{1,0:T(8,128)(2,1)S(1)} %get-tuple-element.166), channel_id=1, source_target_pairs={{0,2},{1,3},{2,0},{3,1},{4,6},{5,7},{6,4},{7,5},{8,10},{9,11},{10,... | collective-permute-start | bytes 737288 | tf_op jit(solution)/shard_map/ppermute | solution.py:204
  127.2 20.4 %collective-permute-start.33 = (bf16[192,640]{1,0:T(8,128)(2,1)S(1)}, bf16[192,640]{1,0:T(8,128)(2,1)S(1)}, u32[]{:S(2)}, u32[]{:S(2)}) collective-permute-start(bf16[192,640]{1,0:T(8,128)(2,1)S(1)} %get-tuple-element.167), channel_id=1, source_target_pairs={{0,3},{1,2},{2,1},{3,0},{4,7},{5,6},{6,5},{7,4},{8,11},{9,10},{10,... | collective-permute-start | bytes 737288 | tf_op jit(solution)/shard_map/ppermute | solution.py:204
  137.5 21.2 %collective-permute-start.9 = (bf16[64,640]{1,0:T(8,128)(2,1)S(1)}, bf16[64,640]{1,0:T(8,128)(2,1)S(1)}, u32[]{:S(2)}, u32[]{:S(2)}) collective-permute-start(bf16[64,640]{1,0:T(8,128)(2,1)S(1)} %get-tuple-element.141), channel_id=1, source_target_pairs={{0,2},{1,3},{2,0},{3,1},{4,6},{5,7},{6,4},{7,5},{8,10},{9,11},{10,... | collective-permute-start | bytes 245768 | tf_op jit(solution)/shard_map/ppermute | solution.py:204
  139.6 19.7 %collective-permute-start.28 = (bf16[64,640]{1,0:T(8,128)(2,1)S(1)}, bf16[64,640]{1,0:T(8,128)(2,1)S(1)}, u32[]{:S(2)}, u32[]{:S(2)}) collective-permute-start(bf16[64,640]{1,0:T(8,128)(2,1)S(1)} %get-tuple-element.161), channel_id=1, source_target_pairs={{0,1},{1,0},{2,3},{3,2},{4,5},{5,4},{6,7},{7,6},{8,9},{9,8},{10,11... | collective-permute-start | bytes 245768 | tf_op jit(solution)/shard_map/ppermute | solution.py:204
  147.6 13.2 %collective-permute-start.29 = (bf16[64,640]{1,0:T(8,128)(2,1)S(1)}, bf16[64,640]{1,0:T(8,128)(2,1)S(1)}, u32[]{:S(2)}, u32[]{:S(2)}) collective-permute-start(bf16[64,640]{1,0:T(8,128)(2,1)S(1)} %get-tuple-element.162), channel_id=1, source_target_pairs={{0,2},{1,3},{2,0},{3,1},{4,6},{5,7},{6,4},{7,5},{8,10},{9,11},{10,... | collective-permute-start | bytes 245768 | tf_op jit(solution)/shard_map/ppermute | solution.py:204
  147.6 19.4 %collective-permute-start.30 = (bf16[64,640]{1,0:T(8,128)(2,1)S(1)}, bf16[64,640]{1,0:T(8,128)(2,1)S(1)}, u32[]{:S(2)}, u32[]{:S(2)}) collective-permute-start(bf16[64,640]{1,0:T(8,128)(2,1)S(1)} %get-tuple-element.163), channel_id=1, source_target_pairs={{0,3},{1,2},{2,1},{3,0},{4,7},{5,6},{6,5},{7,4},{8,11},{9,10},{10,... | collective-permute-start | bytes 245768 | tf_op jit(solution)/shard_map/ppermute | solution.py:204
  158.2 30.5 %collective-permute-start.38 = (bf16[2,2,2,2,24,768]{5,4,3,2,1,0:T(8,128)(2,1)S(1)}, bf16[2,2,2,2,24,768]{5,4,3,2,1,0:T(8,128)(2,1)S(1)}, u32[]{:S(2)}, u32[]{:S(2)}) collective-permute-start(bf16[2,2,2,2,24,768]{5,4,3,2,1,0:T(8,128)(2,1)S(1)} %pad_maximum_fusion.16), channel_id=1, source_target_pairs={{0,4},{4,0},{8,12},{12,8},{16,20},{20,16},{24,28},{28,24},{1,5},{5... | collective-permute-start | bytes 1769480 | tf_op jit(solution)/shard_map/ppermute | solution.py:204
  158.7 28.4 %collective-permute-start.41 = (bf16[2,2,2,96,768]{4,3,2,1,0:T(8,128)(2,1)S(1)}, bf16[2,2,2,96,768]{4,3,2,1,0:T(8,128)(2,1)S(1)}, u32[]{:S(2)}, u32[]{:S(2)}) collective-permute-start(bf16[2,2,2,96,768]{4,3,2,1,0:T(8,128)(2,1)S(1)} %pad_maximum_fusion.9), channel_id=1, source_target_pairs={{0,16},{4,20},{8,24},{12,28},{16,0},{20,4},{24,8},{28,12},{1,17},{... | collective-permute-start | bytes 3538952 | tf_op jit(solution)/shard_map/ppermute | solution.py:204
  159.4 28.2 %collective-permute-start.39 = (bf16[2,2,2,24,3072]{4,3,2,1,0:T(8,128)(2,1)S(1)}, bf16[2,2,2,24,3072]{4,3,2,1,0:T(8,128)(2,1)S(1)}, u32[]{:S(2)}, u32[]{:S(2)}) collective-permute-start(bf16[2,2,2,24,3072]{4,3,2,1,0:T(8,128)(2,1)S(1)} %pad_maximum_fusion.8), channel_id=1, source_target_pairs={{0,8},{4,12},{8,0},{12,4},{16,24},{20,28},{24,16},{28,20},{1,9},{5... | collective-permute-start | bytes 3538952 | tf_op jit(solution)/shard_map/ppermute | solution.py:204
  160.8 8.7 %collective-permute-start.34 = (bf16[64,640]{1,0:T(8,128)(2,1)S(1)}, bf16[64,640]{1,0:T(8,128)(2,1)S(1)}, u32[]{:S(2)}, u32[]{:S(2)}) collective-permute-start(bf16[64,640]{1,0:T(8,128)(2,1)S(1)} %get-tuple-element.169), channel_id=1, source_target_pairs={{0,1},{1,0},{2,3},{3,2},{4,5},{5,4},{6,7},{7,6},{8,9},{9,8},{10,11... | collective-permute-start | bytes 245768 | tf_op jit(solution)/shard_map/ppermute | solution.py:204
  169.5 19.0 %collective-permute-start.36 = (bf16[64,640]{1,0:T(8,128)(2,1)S(1)}, bf16[64,640]{1,0:T(8,128)(2,1)S(1)}, u32[]{:S(2)}, u32[]{:S(2)}) collective-permute-start(bf16[64,640]{1,0:T(8,128)(2,1)S(1)} %get-tuple-element.171), channel_id=1, source_target_pairs={{0,3},{1,2},{2,1},{3,0},{4,7},{5,6},{6,5},{7,4},{8,11},{9,10},{10,... | collective-permute-start | bytes 245768 | tf_op jit(solution)/shard_map/ppermute | solution.py:204
  223.5 20.5 %collective-permute-start.43 = (bf16[64,640]{1,0:T(8,128)(2,1)}, bf16[64,640]{1,0:T(8,128)(2,1)S(1)}, u32[]{:S(2)}, u32[]{:S(2)}) collective-permute-start(bf16[64,640]{1,0:T(8,128)(2,1)} %get-tuple-element.184), channel_id=1, source_target_pairs={{0,1},{1,0},{2,3},{3,2},{4,5},{5,4},{6,7},{7,6},{8,9},{9,8},{10,11... | collective-permute-start | bytes 245768 | tf_op jit(solution)/shard_map/ppermute | solution.py:204
  229.7 14.3 %collective-permute-start.44 = (bf16[64,640]{1,0:T(8,128)(2,1)}, bf16[64,640]{1,0:T(8,128)(2,1)S(1)}, u32[]{:S(2)}, u32[]{:S(2)}) collective-permute-start(bf16[64,640]{1,0:T(8,128)(2,1)} %get-tuple-element.185), channel_id=1, source_target_pairs={{0,2},{1,3},{2,0},{3,1},{4,6},{5,7},{6,4},{7,5},{8,10},{9,11},{10,... | collective-permute-start | bytes 245768 | tf_op jit(solution)/shard_map/ppermute | solution.py:204
  229.7 14.3 %collective-permute-start.45 = (bf16[64,640]{1,0:T(8,128)(2,1)S(1)}, bf16[64,640]{1,0:T(8,128)(2,1)S(1)}, u32[]{:S(2)}, u32[]{:S(2)}) collective-permute-start(bf16[64,640]{1,0:T(8,128)(2,1)S(1)} %get-tuple-element.186), channel_id=1, source_target_pairs={{0,3},{1,2},{2,1},{3,0},{4,7},{5,6},{6,5},{7,4},{8,11},{9,10},{10,... | collective-permute-start | bytes 245768 | tf_op jit(solution)/shard_map/ppermute | solution.py:204
  261.8 60.7 %collective-permute-start.46 = (bf16[192,640]{1,0:T(8,128)(2,1)S(1)}, bf16[192,640]{1,0:T(8,128)(2,1)S(1)}, u32[]{:S(2)}, u32[]{:S(2)}) collective-permute-start(bf16[192,640]{1,0:T(8,128)(2,1)S(1)} %get-tuple-element.192), channel_id=1, source_target_pairs={{0,1},{1,0},{2,3},{3,2},{4,5},{5,4},{6,7},{7,6},{8,9},{9,8},{10,11... | collective-permute-start | bytes 737288 | tf_op jit(solution)/shard_map/ppermute | solution.py:204
  268.8 42.0 %collective-permute-start.59 = (bf16[2,2,2,2,24,3072]{5,4,2,3,0,1:T(8,128)(2,1)S(1)}, bf16[2,2,2,2,24,3072]{5,4,2,3,0,1:T(8,128)(2,1)S(1)}, u32[]{:S(2)}, u32[]{:S(2)}) collective-permute-start(bf16[2,2,2,2,24,3072]{5,4,2,3,0,1:T(8,128)(2,1)S(1)} %get-tuple-element.322), channel_id=1, source_target_pairs={{0,4},{4,0},{8,12},{12,8},{16,20},{20,16},{24,28},{28,24},{1,5},{5... | collective-permute-start | bytes 7077896 | tf_op jit(solution)/shard_map/ppermute | solution.py:204
  276.9 14.0 %collective-permute-start.50 = (bf16[64,640]{1,0:T(8,128)(2,1)S(1)}, bf16[64,640]{1,0:T(8,128)(2,1)S(1)}, u32[]{:S(2)}, u32[]{:S(2)}) collective-permute-start(bf16[64,640]{1,0:T(8,128)(2,1)S(1)} %copy-done.47), channel_id=1, source_target_pairs={{0,2},{1,3},{2,0},{3,1},{4,6},{5,7},{6,4},{7,5},{8,10},{9,11},{10,... | collective-permute-start | bytes 245768 | tf_op jit(solution)/shard_map/ppermute | solution.py:204
  277.5 13.3 %collective-permute-start.51 = (bf16[64,640]{1,0:T(8,128)(2,1)S(1)}, bf16[64,640]{1,0:T(8,128)(2,1)S(1)}, u32[]{:S(2)}, u32[]{:S(2)}) collective-permute-start(bf16[64,640]{1,0:T(8,128)(2,1)S(1)} %get-tuple-element.201), channel_id=1, source_target_pairs={{0,3},{1,2},{2,1},{3,0},{4,7},{5,6},{6,5},{7,4},{8,11},{9,10},{10,... | collective-permute-start | bytes 245768 | tf_op jit(solution)/shard_map/ppermute | solution.py:204
  284.0 58.1 %collective-permute-start.47 = (bf16[192,640]{1,0:T(8,128)(2,1)S(1)}, bf16[192,640]{1,0:T(8,128)(2,1)S(1)}, u32[]{:S(2)}, u32[]{:S(2)}) collective-permute-start(bf16[192,640]{1,0:T(8,128)(2,1)S(1)} %get-tuple-element.193), channel_id=1, source_target_pairs={{0,2},{1,3},{2,0},{3,1},{4,6},{5,7},{6,4},{7,5},{8,10},{9,11},{10,... | collective-permute-start | bytes 737288 | tf_op jit(solution)/shard_map/ppermute | solution.py:204
  290.8 22.6 %collective-permute-start.58 = (bf16[2,2,2,2,96,768]{5,4,2,3,1,0:T(8,128)(2,1)S(1)}, bf16[2,2,2,2,96,768]{5,4,2,3,1,0:T(8,128)(2,1)S(1)}, u32[]{:S(2)}, u32[]{:S(2)}) collective-permute-start(bf16[2,2,2,2,96,768]{5,4,2,3,1,0:T(8,128)(2,1)S(1)} %get-tuple-element.326), channel_id=1, source_target_pairs={{0,4},{4,0},{8,12},{12,8},{16,20},{20,16},{24,28},{28,24},{1,5},{5... | collective-permute-start | bytes 7077896 | tf_op jit(solution)/shard_map/ppermute | solution.py:204
  290.8 27.2 %collective-permute-start.55 = (bf16[64,640]{1,0:T(8,128)(2,1)S(1)}, bf16[64,640]{1,0:T(8,128)(2,1)S(1)}, u32[]{:S(2)}, u32[]{:S(2)}) collective-permute-start(bf16[64,640]{1,0:T(8,128)(2,1)S(1)} %get-tuple-element.217), channel_id=1, source_target_pairs={{0,1},{1,0},{2,3},{3,2},{4,5},{5,4},{6,7},{7,6},{8,9},{9,8},{10,11... | collective-permute-start | bytes 245768 | tf_op jit(solution)/shard_map/ppermute | solution.py:204
  310.8 8.8 %collective-permute-start.56 = (bf16[64,640]{1,0:T(8,128)(2,1)S(1)}, bf16[64,640]{1,0:T(8,128)(2,1)S(1)}, u32[]{:S(2)}, u32[]{:S(2)}) collective-permute-start(bf16[64,640]{1,0:T(8,128)(2,1)S(1)} %get-tuple-element.218), channel_id=1, source_target_pairs={{0,2},{1,3},{2,0},{3,1},{4,6},{5,7},{6,4},{7,5},{8,10},{9,11},{10,... | collective-permute-start | bytes 245768 | tf_op jit(solution)/shard_map/ppermute | solution.py:204
  318.0 25.5 %collective-permute-start.48 = (bf16[192,640]{1,0:T(8,128)(2,1)S(1)}, bf16[192,640]{1,0:T(8,128)(2,1)S(1)}, u32[]{:S(2)}, u32[]{:S(2)}) collective-permute-start(bf16[192,640]{1,0:T(8,128)(2,1)S(1)} %get-tuple-element.194), channel_id=1, source_target_pairs={{0,3},{1,2},{2,1},{3,0},{4,7},{5,6},{6,5},{7,4},{8,11},{9,10},{10,... | collective-permute-start | bytes 737288 | tf_op jit(solution)/shard_map/ppermute | solution.py:204
  319.6 24.6 %collective-permute-start.52 = (bf16[192,640]{1,0:T(8,128)(2,1)S(1)}, bf16[192,640]{1,0:T(8,128)(2,1)S(1)}, u32[]{:S(2)}, u32[]{:S(2)}) collective-permute-start(bf16[192,640]{1,0:T(8,128)(2,1)S(1)} %get-tuple-element.210), channel_id=1, source_target_pairs={{0,1},{1,0},{2,3},{3,2},{4,5},{5,4},{6,7},{7,6},{8,9},{9,8},{10,11... | collective-permute-start | bytes 737288 | tf_op jit(solution)/shard_map/ppermute | solution.py:204
  319.8 28.4 %collective-permute-start.53 = (bf16[192,640]{1,0:T(8,128)(2,1)S(1)}, bf16[192,640]{1,0:T(8,128)(2,1)S(1)}, u32[]{:S(2)}, u32[]{:S(2)}) collective-permute-start(bf16[192,640]{1,0:T(8,128)(2,1)S(1)} %get-tuple-element.211), channel_id=1, source_target_pairs={{0,2},{1,3},{2,0},{3,1},{4,6},{5,7},{6,4},{7,5},{8,10},{9,11},{10,... | collective-permute-start | bytes 737288 | tf_op jit(solution)/shard_map/ppermute | solution.py:204
  322.5 25.7 %collective-permute-start.54 = (bf16[192,640]{1,0:T(8,128)(2,1)S(1)}, bf16[192,640]{1,0:T(8,128)(2,1)S(1)}, u32[]{:S(2)}, u32[]{:S(2)}) collective-permute-start(bf16[192,640]{1,0:T(8,128)(2,1)S(1)} %get-tuple-element.212), channel_id=1, source_target_pairs={{0,3},{1,2},{2,1},{3,0},{4,7},{5,6},{6,5},{7,4},{8,11},{9,10},{10,... | collective-permute-start | bytes 737288 | tf_op jit(solution)/shard_map/ppermute | solution.py:204
  342.1 26.5 %collective-permute-start.64 = (bf16[2,2,2,24,3072]{4,3,1,2,0:T(8,128)(2,1)}, bf16[2,2,2,24,3072]{4,3,1,2,0:T(8,128)(2,1)}, u32[]{:S(2)}, u32[]{:S(2)}) collective-permute-start(bf16[2,2,2,24,3072]{4,3,1,2,0:T(8,128)(2,1)} %get-tuple-element.338), channel_id=1, source_target_pairs={{0,8},{4,12},{8,0},{12,4},{16,24},{20,28},{24,16},{28,20},{1,9},{5... | collective-permute-start | bytes 3538952 | tf_op jit(solution)/shard_map/ppermute | solution.py:204
  343.5 27.9 %collective-permute-start.63 = (bf16[2,2,2,96,768]{4,3,1,2,0:T(8,128)(2,1)}, bf16[2,2,2,96,768]{4,3,1,2,0:T(8,128)(2,1)}, u32[]{:S(2)}, u32[]{:S(2)}) collective-permute-start(bf16[2,2,2,96,768]{4,3,1,2,0:T(8,128)(2,1)} %get-tuple-element.340), channel_id=1, source_target_pairs={{0,16},{4,20},{8,24},{12,28},{16,0},{20,4},{24,8},{28,12},{1,17},{... | collective-permute-start | bytes 3538952 | tf_op jit(solution)/shard_map/ppermute | solution.py:204
  344.1 34.9 %collective-permute-start.60 = (bf16[192,640]{1,0:T(8,128)(2,1)S(1)}, bf16[192,640]{1,0:T(8,128)(2,1)}, u32[]{:S(2)}, u32[]{:S(2)}) collective-permute-start(bf16[192,640]{1,0:T(8,128)(2,1)S(1)} %get-tuple-element.227), channel_id=1, source_target_pairs={{0,1},{1,0},{2,3},{3,2},{4,5},{5,4},{6,7},{7,6},{8,9},{9,8},{10,11... | collective-permute-start | bytes 737288 | tf_op jit(solution)/shard_map/ppermute | solution.py:204
  348.2 30.8 %collective-permute-start.61 = (bf16[192,640]{1,0:T(8,128)(2,1)S(1)}, bf16[192,640]{1,0:T(8,128)(2,1)}, u32[]{:S(2)}, u32[]{:S(2)}) collective-permute-start(bf16[192,640]{1,0:T(8,128)(2,1)S(1)} %get-tuple-element.228), channel_id=1, source_target_pairs={{0,2},{1,3},{2,0},{3,1},{4,6},{5,7},{6,4},{7,5},{8,10},{9,11},{10,... | collective-permute-start | bytes 737288 | tf_op jit(solution)/shard_map/ppermute | solution.py:204
  348.2 30.8 %collective-permute-start.62 = (bf16[192,640]{1,0:T(8,128)(2,1)S(1)}, bf16[192,640]{1,0:T(8,128)(2,1)}, u32[]{:S(2)}, u32[]{:S(2)}) collective-permute-start(bf16[192,640]{1,0:T(8,128)(2,1)S(1)} %get-tuple-element.229), channel_id=1, source_target_pairs={{0,3},{1,2},{2,1},{3,0},{4,7},{5,6},{6,5},{7,4},{8,11},{9,10},{10,... | collective-permute-start | bytes 737288 | tf_op jit(solution)/shard_map/ppermute | solution.py:204
  374.6 13.0 %collective-permute-start.67 = (bf16[2,2,24,3072]{3,2,0,1:T(8,128)(2,1)}, bf16[2,2,24,3072]{3,2,0,1:T(8,128)(2,1)}, u32[]{:S(2)}, u32[]{:S(2)}) collective-permute-start(bf16[2,2,24,3072]{3,2,0,1:T(8,128)(2,1)} %get-tuple-element.354), channel_id=1, source_target_pairs={{0,16},{4,20},{8,24},{12,28},{16,0},{20,4},{24,8},{28,12},{1,17},{... | collective-permute-start | bytes 1769480 | tf_op jit(solution)/shard_map/ppermute | solution.py:204
  375.3 12.7 %collective-permute-start.66 = (bf16[2,2,96,768]{3,2,0,1:T(8,128)(2,1)}, bf16[2,2,96,768]{3,2,0,1:T(8,128)(2,1)}, u32[]{:S(2)}, u32[]{:S(2)}) collective-permute-start(bf16[2,2,96,768]{3,2,0,1:T(8,128)(2,1)} %get-tuple-element.356), channel_id=1, source_target_pairs={{0,8},{4,12},{8,0},{12,4},{16,24},{20,28},{24,16},{28,20},{1,9},{5... | collective-permute-start | bytes 1769480 | tf_op jit(solution)/shard_map/ppermute | solution.py:204
  379.0 25.3 %collective-permute-start.65 = (bf16[2,2,2,2,24,2304]{5,4,2,3,1,0:T(8,128)(2,1)}, bf16[2,2,2,2,24,2304]{5,4,2,3,1,0:T(8,128)(2,1)}, u32[]{:S(2)}, u32[]{:S(2)}) collective-permute-start(bf16[2,2,2,2,24,2304]{5,4,2,3,1,0:T(8,128)(2,1)} %get-tuple-element.334), channel_id=1, source_target_pairs={{0,4},{4,0},{8,12},{12,8},{16,20},{20,16},{24,28},{28,24},{1,5},{5... | collective-permute-start | bytes 5308424 | tf_op jit(solution)/shard_map/ppermute | solution.py:204
  390.0 32.2 %collective-permute-start.72 = (bf16[2,24,3072]{2,1,0:T(8,128)(2,1)}, bf16[2,24,3072]{2,1,0:T(8,128)(2,1)}, u32[]{:S(2)}, u32[]{:S(2)}) collective-permute-start(bf16[2,24,3072]{2,1,0:T(8,128)(2,1)} %get-tuple-element.390), channel_id=1, source_target_pairs={{0,1},{1,0},{2,3},{3,2},{4,5},{5,4},{6,7},{7,6},{8,9},{9,8},{10,11... | collective-permute-start | bytes 884744 | tf_op jit(solution)/shard_map/ppermute | solution.py:204
  404.3 18.9 %collective-permute-start.71 = (bf16[2,96,768]{2,1,0:T(8,128)(2,1)}, bf16[2,96,768]{2,1,0:T(8,128)(2,1)}, u32[]{:S(2)}, u32[]{:S(2)}) collective-permute-start(bf16[2,96,768]{2,1,0:T(8,128)(2,1)} %get-tuple-element.392), channel_id=1, source_target_pairs={{0,1},{1,0},{2,3},{3,2},{4,5},{5,4},{6,7},{7,6},{8,9},{9,8},{10,11... | collective-permute-start | bytes 884744 | tf_op jit(solution)/shard_map/ppermute | solution.py:204
  406.4 21.0 %collective-permute-start.68 = (bf16[2,2,2,24,2304]{4,3,1,2,0:T(8,128)(2,1)S(1)}, bf16[2,2,2,24,2304]{4,3,1,2,0:T(8,128)(2,1)}, u32[]{:S(2)}, u32[]{:S(2)}) collective-permute-start(bf16[2,2,2,24,2304]{4,3,1,2,0:T(8,128)(2,1)S(1)} %get-tuple-element.348), channel_id=1, source_target_pairs={{0,16},{4,20},{8,24},{12,28},{16,0},{20,4},{24,8},{28,12},{1,17},{... | collective-permute-start | bytes 2654216 | tf_op jit(solution)/shard_map/ppermute | solution.py:204
  423.2 32.8 %collective-permute-start.79 = (bf16[24,3072]{1,0:T(8,128)(2,1)S(1)}, bf16[24,3072]{1,0:T(8,128)(2,1)S(1)}, u32[]{:S(2)}, u32[]{:S(2)}) collective-permute-start(bf16[24,3072]{1,0:T(8,128)(2,1)S(1)} %get-tuple-element.420), channel_id=1, source_target_pairs={{0,2},{1,3},{2,0},{3,1},{4,6},{5,7},{6,4},{7,5},{8,10},{9,11},{10,... | collective-permute-start | bytes 442376 | tf_op jit(solution)/shard_map/ppermute | solution.py:204
  426.3 30.5 %collective-permute-start.78 = (bf16[96,768]{1,0:T(8,128)(2,1)S(1)}, bf16[96,768]{1,0:T(8,128)(2,1)S(1)}, u32[]{:S(2)}, u32[]{:S(2)}) collective-permute-start(bf16[96,768]{1,0:T(8,128)(2,1)S(1)} %get-tuple-element.422), channel_id=1, source_target_pairs={{0,2},{1,3},{2,0},{3,1},{4,6},{5,7},{6,4},{7,5},{8,10},{9,11},{10,... | collective-permute-start | bytes 442376 | tf_op jit(solution)/shard_map/ppermute | solution.py:204
  428.8 13.1 %collective-permute-start.69 = (bf16[2,2,24,2304]{3,2,0,1:T(8,128)(2,1)S(1)}, bf16[2,2,24,2304]{3,2,0,1:T(8,128)(2,1)S(1)}, u32[]{:S(2)}, u32[]{:S(2)}) collective-permute-start(bf16[2,2,24,2304]{3,2,0,1:T(8,128)(2,1)S(1)} %get-tuple-element.384), channel_id=1, source_target_pairs={{0,8},{4,12},{8,0},{12,4},{16,24},{20,28},{24,16},{28,20},{1,9},{5... | collective-permute-start | bytes 1327112 | tf_op jit(solution)/shard_map/ppermute | solution.py:204
  430.5 17.7 %collective-permute-start.74 = (bf16[2,2,2,24,896]{4,3,2,1,0:T(8,128)(2,1)S(1)}, bf16[2,2,2,24,896]{4,3,2,1,0:T(8,128)(2,1)S(1)}, u32[]{:S(2)}, u32[]{:S(2)}) collective-permute-start(bf16[2,2,2,24,896]{4,3,2,1,0:T(8,128)(2,1)S(1)} %get-tuple-element.388), channel_id=1, source_target_pairs={{0,8},{4,12},{8,0},{12,4},{16,24},{20,28},{24,16},{28,20},{1,9},{5... | collective-permute-start | bytes 1032200 | tf_op jit(solution)/shard_map/ppermute | solution.py:204
  449.9 10.6 %collective-permute-start.75 = (bf16[24,2304]{1,0:T(8,128)(2,1)S(1)}, bf16[24,2304]{1,0:T(8,128)(2,1)S(1)}, u32[]{:S(2)}, u32[]{:S(2)}) collective-permute-start(bf16[24,2304]{1,0:T(8,128)(2,1)S(1)} %get-tuple-element.432), channel_id=1, source_target_pairs={{0,2},{1,3},{2,0},{3,1},{4,6},{5,7},{6,4},{7,5},{8,10},{9,11},{10,... | collective-permute-start | bytes 331784 | tf_op jit(solution)/shard_map/ppermute | solution.py:204
  (88 other events, 1445.9 us)
